TPU v7x, 256 devices: a whole 4x4x8 slice. The times are simulated.
256 devices in a mesh: member: 4 (over x_lo, core), space: 64 (over y, z, x_hi).
Axes of the slice: x: 4 (x_hi: 2, x_lo: 2; x = x_hi * 2 + x_lo), y: 4, z: 8, core: 2. Of those that a mesh axis runs over, the one named last changes fastest.
Arguments:
- mesh_latent: bfloat16 [8, 8192, 1024], P('member', 'space'), may hold values from -6 to 6
- w_hidden: bfloat16 [1024, 1024], replicated, may hold values from -0.1875 to 0.1875
- w_out: bfloat16 [100, 1024], replicated, may hold values from -0.1875 to 0.1875
- target: bfloat16 [100, 32768], P(None, 'space'), may hold values from -6 to 6
- slots: int32 [3, 32768], P(None, 'space'), may hold values from 0 to 383, as said below
- lengths: int32 [64], P('space'), may hold values from 1 to 512, 24576 in all
Outputs:
- grad_hidden: float32 [1024, 1024], P('space')
- grad_mesh: bfloat16 [8, 8192, 1024], P('member', 'space')
Inputs may be any that keep to these rules, and one draw needn't show every extreme that they name: The three entries of a column are distinct slots of the padded block of 384 nodes of its tile. `lengths`: local grid positions at or beyond a tile's length are padding.
All inputs are finite; a program needn't handle non-finite values. No bound on the sum of `lengths` on one device may be relied on, other than what follows from the above.
Results may differ from a plain program's by a relative error of at most 0.015.
Values may be sent and summed in bfloat16 or wider, within the bound.
No kernel may reach another device: no remote copies, remote signals or barrier semaphores. Data moves between devices by JAX's collectives and lax.ppermute only.
A program may use at most 64 MiB of HBM per device.

v0:
```python
import jax
import jax.numpy as jnp
from jax import lax
from jax.sharding import Mesh
from jax.sharding import PartitionSpec as P

MEMBER = ("member_0", "member_1")
SPACE = ("space_0", "space_1", "space_2")


fair_eps = 0.05
smooth_sq = 0.01


def extended_2(value, sides, width):
    for axis, dim in sides:
        size, length = (lax.axis_size(axis), value.shape[dim])
        up = [(i, (i + 1) % size) for i in range(size)]
        down = [(j, i) for i, j in up]
        last = lax.slice_in_dim(value, length - width, length, axis=dim)
        leading = lax.slice_in_dim(value, 0, width, axis=dim)
        before = lax.ppermute(last, axis, up)
        after = lax.ppermute(leading, axis, down)
        value = jnp.concatenate([before, value, after], axis=dim)
    return value


def joined_along(parts, dim):
    shape = list(parts.shape[1:])
    shape[dim] *= parts.shape[0]
    return jnp.moveaxis(parts, 0, dim).reshape(shape)


def stacked_from(value, axes, order):
    parts = value
    for k in order:
        parts = lax.all_gather(parts, axes[k])
    done = order[::-1]
    back = [done.index(k) for k in range(len(axes))]
    parts = parts.transpose(*back, *range(len(axes), parts.ndim))
    return parts.reshape(-1, *value.shape)


def gather_axes(value, axes, order, dim):
    return joined_along(stacked_from(value, axes, order), dim)


def sum_by_axis(total, axes):
    for axis in axes:
        total = lax.psum_scatter(total, axis, scatter_dimension=0, tiled=True)
    return total


def over_pieces(value, axis):
    return lax.all_gather(value, axis).astype(jnp.float32).sum(0)


def shifted(value, axis, steps):
    count = lax.axis_size(axis)
    pairs = [(source, (source + steps) % count) for source in range(count)]
    return lax.ppermute(value, axis, pairs)


def smooth_sign(value):
    return value / jnp.sqrt(value * value + smooth_sq)


def loss_grad(own, everyone, truth, live, total):
    values = own.astype(jnp.float32)
    first = smooth_sign(values - truth.astype(jnp.float32)[None]) / total
    pair = jnp.sum(smooth_sign(values[:, None] - everyone.astype(jnp.float32)[None]), axis=1)
    return (live * (first - (1.0 - fair_eps) / (total * (total - 1)) * pair)).astype(jnp.bfloat16)


def shards(mesh_latent, w_hidden, w_out, target, slots, lengths):
    width = mesh_latent.shape[1]
    grid_rows = target.shape[1]
    total = mesh_latent.shape[0] * lax.axis_size(MEMBER)
    extended = extended_2(mesh_latent, ((SPACE, 1),), width)
    positions = jnp.arange(3 * width, dtype=jnp.int32)
    counts_f = jnp.zeros((grid_rows, 3 * width), jnp.float32)
    for k in range(3):
        counts_f = counts_f + (slots[k][:, None] == positions[None, :]).astype(jnp.float32)
    counts = counts_f.astype(jnp.bfloat16)
    area = jnp.einsum("gs,msl->mgl", counts, extended, preferred_element_type=jnp.float32).astype(
        jnp.bfloat16
    )
    pre = jnp.einsum("mgl,lj->mgj", area, w_hidden, preferred_element_type=jnp.float32)
    hidden = jax.nn.silu(pre).astype(jnp.bfloat16)
    pred = jnp.einsum("cj,mgj->mcg", w_out, hidden, preferred_element_type=jnp.float32).astype(
        jnp.bfloat16
    )
    live = (jnp.arange(grid_rows, dtype=jnp.int32) < lengths[0]).astype(jnp.float32)
    everyone = gather_axes(pred, MEMBER, (0, 1), 0)
    dpred = loss_grad(pred, everyone, target, live, total)
    dz = jnp.einsum("mcg,cj->mgj", dpred, w_out, preferred_element_type=jnp.float32)
    sig = jax.nn.sigmoid(pre)
    dpre = (dz * sig * (1.0 + pre * (1.0 - sig))).astype(jnp.bfloat16)
    local_rows = sum_by_axis(
        jnp.einsum("mgi,mgj->ij", area, dpre, preferred_element_type=jnp.float32), SPACE
    )
    grad_hidden = over_pieces(local_rows.astype(jnp.bfloat16), MEMBER).astype(jnp.float32)
    darea = jnp.einsum("mgj,ij->mgi", dpre, w_hidden, preferred_element_type=jnp.float32).astype(
        jnp.bfloat16
    )
    dext = jnp.einsum("gs,mgi->msi", counts, darea, preferred_element_type=jnp.float32)
    from_right = shifted(dext[:, :width].astype(jnp.bfloat16), SPACE, -1).astype(jnp.float32)
    from_left = shifted(dext[:, 2 * width :].astype(jnp.bfloat16), SPACE, 1).astype(jnp.float32)
    grad_mesh = (dext[:, width : 2 * width] + from_right + from_left).astype(jnp.bfloat16)
    return (grad_hidden, grad_mesh)


def solution(mesh):
    finer = Mesh(
        mesh.devices.reshape(2, 2, 4, 8, 2),
        ("member_0", "member_1", "space_0", "space_1", "space_2"),
    )
    in_specs = (P(MEMBER, SPACE, None), P(), P(), P(None, SPACE), P(None, SPACE), P(SPACE))
    out_specs = (P(SPACE, None), P(MEMBER, SPACE, None))
    return jax.shard_map(
        shards, mesh=finer, in_specs=in_specs, out_specs=out_specs, check_vma=False
    )
```

profile of v0, /device:TPU:1, one launch (start us, length us, event | category | flops | bytes accessed | tf_op | source)
XLA Modules:
  0.0 190.4 jit_solution(17604131955529430374)
XLA Ops:
  7.2 1.4 copy.34
  8.7 3.6 %collective-permute-start = (bf16[2,128,1024]{1,2,0:T(8,128)(2,1)S(1)}, bf16[2,128,1024]{1,2,0:T(8,128)(2,1)S(1)}, u32[]{:S(2)}, u32[]{:S(2)}) collective-permute-start(bf16[2,128,1024]{1,2,0:T(8,128)(2,1)S(1)} %copy.34), channel_id=1, source_target_pairs={{0,1},{1,2},{2,3},{3,4},{4,5},{5,6},{6,7},{7,8},{8,9},{9,10},{10,1... | collective-permute-start | bytes 1572872 | tf_op jit(solution)/shard_map/ppermute | solution.py:22
  12.3 7.8 %collective-permute-start.1 = (bf16[2,128,1024]{1,2,0:T(8,128)(2,1)S(1)}, bf16[2,128,1024]{1,2,0:T(8,128)(2,1)S(1)}, u32[]{:S(2)}, u32[]{:S(2)}) collective-permute-start(bf16[2,128,1024]{1,2,0:T(8,128)(2,1)S(1)} %copy.34), channel_id=1, source_target_pairs={{1,0},{2,1},{3,2},{4,3},{5,4},{6,5},{7,6},{8,7},{9,8},{10,9},{11,1... | collective-permute-start | bytes 1572872 | tf_op jit(solution)/shard_map/ppermute | solution.py:23
  20.2 0.9 convert_element_type.90
  21.7 0.8 fusion.52
  22.5 11.6 %collective-permute-done = bf16[2,128,1024]{1,2,0:T(8,128)(2,1)S(1)} collective-permute-done((bf16[2,128,1024]{1,2,0:T(8,128)(2,1)S(1)}, bf16[2,128,1024]{1,2,0:T(8,128)(2,1)S(1)}, u32[]{:S(2)}, u32[]{:S(2)}) %collective-permute-start) | collective-permute-done | bytes 524320 | tf_op jit(solution)/shard_map/ppermute | solution.py:22
  34.2 3.4 %collective-permute-done.1 = bf16[2,128,1024]{1,2,0:T(8,128)(2,1)S(1)} collective-permute-done((bf16[2,128,1024]{1,2,0:T(8,128)(2,1)S(1)}, bf16[2,128,1024]{1,2,0:T(8,128)(2,1)S(1)}, u32[]{:S(2)}, u32[]{:S(2)}) %collective-permute-start.1) | collective-permute-done | bytes 524320 | tf_op jit(solution)/shard_map/ppermute | solution.py:23
  37.6 1.5 convolution_convert_fusion
  39.2 2.4 %fusion.5 = f32[2,512,1024]{2,1,0:T(8,128)S(1)} fusion(bf16[1024,1024]{1,0:T(8,128)(2,1)S(1)} %copy-done, bf16[2,1024,512]{2,1,0:T(8,128)(2,1)S(1)} %convolution_convert_fusion), kind=kOutput, calls=%fused_computation.11 | convolution fusion | flops 2147483648 | bytes 8388608 | tf_op jit(solution)/shard_map/mgl,lj->mgj/dot_general | solution.py:88
  41.6 1.3 fusion.53
  42.9 5.7 %all-gather = bf16[4,100,512]{2,1,0:T(8,128)(2,1)S(1)} all-gather(bf16[2,100,512]{2,1,0:T(8,128)(2,1)S(1)} %get-tuple-element.18), channel_id=2, replica_groups=mesh['member_0'=2,'member_1'=2,'space_0'=4,'space_1'=8,'space_2'=2] {'me..., dimensions={0}, use_global_device_ids=true | all-gather | bytes 614400 | tf_op jit(solution)/shard_map/all_gather | solution.py:37
  48.6 0.3 copy.38
  48.9 4.9 %all-gather.1 = bf16[4,2,100,512]{3,1,2,0:T(2,128)(2,1)S(1)} all-gather(bf16[2,2,100,512]{3,1,2,0:T(2,128)(2,1)S(1)} %copy.38), channel_id=3, replica_groups=mesh['member_0'=2,'member_1'=2,'space_0'=4,'space_1'=8,'space_2'=2] {'me..., dimensions={0}, use_global_device_ids=true | all-gather | bytes 1228800 | tf_op jit(solution)/shard_map/all_gather | solution.py:37
  53.9 0.2 convert_bitcast_fusion
  54.3 1.0 copy.41
  55.3 1.4 fusion.2
  56.6 1.9 multiply_convert_fusion
  58.5 1.3 copy-done.3
  59.8 4.3 %convolution_bitcast_fusion = f32[1024,1024]{1,0:T(8,128)} fusion(bf16[2,512,1024]{2,1,0:T(8,128)(2,1)S(1)} %multiply_convert_fusion, bf16[2,1024,512]{2,1,0:T(8,128)(2,1)S(1)} %convolution_convert_fusion), kind=kOutput, calls=%fused_computation.8 | convolution fusion | flops 2147483648 | bytes 8388608 | tf_op jit(solution)/shard_map/mgi,mgj->ij/dot_general | solution.py:100
  64.2 50.8 %reduce-scatter.4.cloned.1.call-done = f32[256,1024]{1,0:T(8,128)} async-done(((f32[1024,1024]{1,0:T(8,128)}), f32[256,1024]{1,0:T(8,128)}) %reduce-scatter.4.cloned.1.call-update) | async-done | bytes 1048592 | tf_op jit(solution)/shard_map/reduce_scatter | solution.py:50
  115.0 7.2 %fusion.54 = (bf16[2,384,1024]{1,2,0:T(8,128)(2,1)}, f32[2,384,1024]{1,2,0:T(8,128)}) fusion(s32[512]{0:T(512)S(1)} %bitcast.57, s32[512]{0:T(512)S(1)} %bitcast.59, s32[512]{0:T(512)S(1)} %bitcast.55, bf16[2,512,1024]{2,1,0:T(8,128)(2,1)} %copy-done.3, bf16[1024,1024]{1,0:T(8,128)(2,1)S(1)} %copy-done), kind=kOutput, calls=%fused_computation.62 | convolution fusion | flops 2956394496 | bytes 8919040 | tf_op jit(solution)/shard_map/gs,mgi->msi/dot_general | solution.py:106
  122.2 2.2 %fusion.51 = (bf16[2,128,1024]{1,2,0:T(8,128)(2,1)}, bf16[2,128,1024]{1,2,0:T(8,128)(2,1)}) fusion(bf16[2,384,1024]{1,2,0:T(8,128)(2,1)} %get-tuple-element.19), kind=kLoop, calls=%fused_computation.59 | loop fusion | bytes 2097152 | tf_op jit(solution)/shard_map/slice | solution.py:107
  124.4 5.7 %collective-permute-start.2 = (bf16[2,128,1024]{1,2,0:T(8,128)(2,1)}, bf16[2,128,1024]{1,2,0:T(8,128)(2,1)S(1)}, u32[]{:S(2)}, u32[]{:S(2)}) collective-permute-start(bf16[2,128,1024]{1,2,0:T(8,128)(2,1)} %get-tuple-element.12), channel_id=1, source_target_pairs={{0,63},{1,0},{2,1},{3,2},{4,3},{5,4},{6,5},{7,6},{8,7},{9,8},{10,9... | collective-permute-start | bytes 1572872 | tf_op jit(solution)/shard_map/ppermute | solution.py:61
  130.1 24.1 %reduce-scatter.6.cloned.1.call-done = f32[32,1024]{1,0:T(8,128)} async-done(((f32[256,1024]{1,0:T(8,128)}), f32[32,1024]{1,0:T(8,128)}) %reduce-scatter.6.cloned.1.call-update) | async-done | bytes 131088 | tf_op jit(solution)/shard_map/reduce_scatter | solution.py:50
  154.3 0.2 collective-permute-done.3
  154.5 0.8 copy-done.1
  155.3 1.5 fusion.27
  156.9 1.0 copy.43
  157.9 18.3 %reduce-scatter.8.cloned.1.call-done = f32[16,1024]{1,0:T(8,128)} async-done(((f32[32,1024]{1,0:T(8,128)}), f32[16,1024]{1,0:T(8,128)}) %reduce-scatter.8.cloned.1.call-update) | async-done | bytes 65552 | tf_op jit(solution)/shard_map/reduce_scatter | solution.py:50
  176.2 0.8 convert_element_type.96
  177.1 6.1 %all-gather.2 = bf16[64,1024]{1,0:T(8,128)(2,1)S(1)} all-gather(bf16[16,1024]{1,0:T(8,128)(2,1)S(1)} %convert_element_type.96), channel_id=4, replica_groups=mesh['member_0'=2,'member_1'=2,'space_0'=4,'space_1'=8,'space_2'=2] {'me..., dimensions={0}, use_global_device_ids=true | all-gather | bytes 163840 | tf_op jit(solution)/shard_map/all_gather | solution.py:55
  183.2 0.6 convert_reduce_fusion
  (17 shorter events, 0.5 us)
Async XLA Ops:
  7.2 32.0 %copy-start = (bf16[1024,1024]{1,0:T(8,128)(2,1)S(1)}, bf16[1024,1024]{1,0:T(8,128)(2,1)}, u32[]{:S(2)}) copy-start(bf16[1024,1024]{1,0:T(8,128)(2,1)} %param.7) | copy-start | bytes 6291460
  7.2 107.8 %reduce-scatter.4.cloned.1.call-start = ((), (), s32[]{:S(2)}) async-start(), calls=%async_computation.3 | async-start | bytes 5242880 | tf_op jit(solution)/shard_map/reduce_scatter | solution.py:50
  8.7 25.5 %collective-permute-start = (bf16[2,128,1024]{1,2,0:T(8,128)(2,1)S(1)}, bf16[2,128,1024]{1,2,0:T(8,128)(2,1)S(1)}, u32[]{:S(2)}, u32[]{:S(2)}) collective-permute-start(bf16[2,128,1024]{1,2,0:T(8,128)(2,1)S(1)} %copy.34), channel_id=1, source_target_pairs={{0,1},{1,2},{2,3},{3,4},{4,5},{5,6},{6,7},{7,8},{8,9},{9,10},{10,1... | collective-permute-start | bytes 1572872 | tf_op jit(solution)/shard_map/ppermute | solution.py:22
  12.3 25.3 %collective-permute-start.1 = (bf16[2,128,1024]{1,2,0:T(8,128)(2,1)S(1)}, bf16[2,128,1024]{1,2,0:T(8,128)(2,1)S(1)}, u32[]{:S(2)}, u32[]{:S(2)}) collective-permute-start(bf16[2,128,1024]{1,2,0:T(8,128)(2,1)S(1)} %copy.34), channel_id=1, source_target_pairs={{1,0},{2,1},{3,2},{4,3},{5,4},{6,5},{7,6},{8,7},{9,8},{10,9},{11,1... | collective-permute-start | bytes 1572872 | tf_op jit(solution)/shard_map/ppermute | solution.py:23
  39.1 2.5 %copy-start.2 = (bf16[100,1024]{1,0:T(8,128)(2,1)S(1)}, bf16[100,1024]{1,0:T(8,128)(2,1)}, u32[]{:S(2)}) copy-start(bf16[100,1024]{1,0:T(8,128)(2,1)} %param.8) | copy-start | bytes 614404
  58.5 1.3 copy-start.3
  64.1 90.1 %reduce-scatter.6.cloned.1.call-start = ((), (), s32[]{:S(2)}) async-start(), calls=%async_computation.4 | async-start | bytes 1179648 | tf_op jit(solution)/shard_map/reduce_scatter | solution.py:50
  115.0 61.2 %reduce-scatter.8.cloned.1.call-start = ((), (), s32[]{:S(2)}) async-start(), calls=%async_computation.5 | async-start | bytes 196608 | tf_op jit(solution)/shard_map/reduce_scatter | solution.py:50
  124.4 29.9 %collective-permute-start.2 = (bf16[2,128,1024]{1,2,0:T(8,128)(2,1)}, bf16[2,128,1024]{1,2,0:T(8,128)(2,1)S(1)}, u32[]{:S(2)}, u32[]{:S(2)}) collective-permute-start(bf16[2,128,1024]{1,2,0:T(8,128)(2,1)} %get-tuple-element.12), channel_id=1, source_target_pairs={{0,63},{1,0},{2,1},{3,2},{4,3},{5,4},{6,5},{7,6},{8,7},{9,8},{10,9... | collective-permute-start | bytes 1572872 | tf_op jit(solution)/shard_map/ppermute | solution.py:61
  130.1 24.4 %collective-permute-start.3 = (bf16[2,128,1024]{1,2,0:T(8,128)(2,1)}, bf16[2,128,1024]{1,2,0:T(8,128)(2,1)S(1)}, u32[]{:S(2)}, u32[]{:S(2)}) collective-permute-start(bf16[2,128,1024]{1,2,0:T(8,128)(2,1)} %get-tuple-element.13), channel_id=1, source_target_pairs={{0,1},{1,2},{2,3},{3,4},{4,5},{5,6},{6,7},{7,8},{8,9},{9,10},{10,1... | collective-permute-start | bytes 1572872 | tf_op jit(solution)/shard_map/ppermute | solution.py:61
  154.5 0.8 copy-start.1
Sparse Core Ops, SparseCore 0:
  64.3 50.6 reduce-scatter.3
  117.5 36.7 reduce-scatter.5
  156.7 19.4 reduce-scatter.7
where the time goes:
time: 191 us; the launch traced here: 190 us
  waiting for transfers between devices  109 us (57%)
  matrix products  18.6 us (10%)
  starting transfers between devices  17.3 us (9%)
  blocking collectives  16.7 us (9%)
  between operations  14.5 us (8%)
  local copies, waits for them, and re-layouts  9.16 us (5%)
  other arithmetic  5.55 us (3%)
    reduce_scatter x3, waiting for transfers between devices, sum_by_axis(): total = lax.psum_scatter(total, axis, scatter_dimension=0, tiled=True)  93.2 us
    ppermute x1, waiting for transfers between devices, extended_2(): before = lax.ppermute(last, axis, up)  11.6 us
    all_gather x2, blocking collectives, stacked_from(): parts = lax.all_gather(parts, axes[k])  10.5 us
    ppermute x1, starting transfers between devices, extended_2(): after = lax.ppermute(leading, axis, down)  7.83 us
    dot_general x1, matrix products, shards(): jnp.einsum('gs,mgi->msi', counts, darea, preferred_element_type=jnp.float32)  7.15 us
    all_gather x1, blocking collectives, over_pieces(): return lax.all_gather(value, axis).astype(jnp.float32).sum(0)  6.12 us
    ppermute x2, starting transfers between devices, shifted(): return lax.ppermute(value, axis, pairs)  5.71 us
    unnamed x10, local copies, waits for them, and re-layouts  4.57 us
  transfers between devices with their start and end apart: 7, of which 6 were waited for; matrix products, arithmetic and copies ran while one was open for 7% of the time, Pallas kernels for 0%

commit v1 on v0

v1 whole, which is shorter than its diff:
```python
import itertools

import jax
import jax.numpy as jnp
from jax import lax
from jax.sharding import Mesh
from jax.sharding import PartitionSpec as P

NAMES = ("xl", "c", "y", "z", "xh")
MEMBER = ("xl", "c")
SPACE = ("y", "z", "xh")
BF16 = jnp.bfloat16
F32 = jnp.float32

fair_eps = 0.05
smooth_sq = 0.01


def permute(value, axes, moved):
    sizes = [lax.axis_size(a) for a in axes]
    pairs = []
    for at in itertools.product(*[range(s) for s in sizes]):
        source = target = 0
        for size, a, b in zip(sizes, at, moved(*at)):
            source, target = source * size + a, target * size + b % size
        pairs.append((source, target))
    return lax.ppermute(value, axes if len(axes) > 1 else axes[0], pairs)


def shifted(value, axes, steps):
    count = lax.axis_size(axes)
    return lax.ppermute(value, axes, [(i, (i + steps) % count) for i in range(count)])


def piece(parts, at):
    return lax.dynamic_index_in_dim(parts, at, 0, keepdims=False)


def smooth_sign(value):
    return value / jnp.sqrt(value * value + smooth_sq)


def loss_grad(own, everyone, truth, live, total):
    values = own.astype(F32)
    first = smooth_sign(values - truth.astype(F32)[None]) / total
    pair = jnp.sum(smooth_sign(values[:, None] - everyone.astype(F32)[None]), axis=1)
    return (live * (first - (1.0 - fair_eps) / (total * (total - 1)) * pair)).astype(BF16)


def reduce_rows(grad):
    rows, cols = grad.shape
    n_y, n_z, n_x, n_l = (lax.axis_size(a) for a in ("y", "z", "xh", "xl"))
    c, y = lax.axis_index("c"), lax.axis_index("y")
    half = cols // 2
    left, right = grad[:, :half], grad[:, half:]
    keep = jnp.where(c == 0, left, right)
    give = jnp.where(c == 0, right, left)
    got = shifted(give, "c", 1)
    parts = (keep.astype(F32) + got.astype(F32)).astype(BF16).reshape(n_y, rows // n_y, half)
    steps = [s for s in range(1, n_y)]
    got = [shifted(piece(parts, (y + s) % n_y), "y", s) for s in steps]
    total = piece(parts, y).astype(F32)
    for g in got:
        total = total + g.astype(F32)
    own_rows = rows // (n_y * n_z * n_x)
    quarter = half // n_l
    parts = total.astype(BF16).reshape(n_z * n_x, own_rows, n_l, quarter).transpose(2, 0, 1, 3)
    parts = parts.reshape(n_l * n_z * n_x, own_rows, quarter)
    got = lax.all_to_all(parts, ("xl", "z", "xh"), 0, 0)
    mine = got.astype(F32).sum(0).astype(BF16)
    other = shifted(mine, "xl", 1)
    first = lax.axis_index("xl") == 0
    mine = jnp.concatenate([jnp.where(first, mine, other), jnp.where(first, other, mine)], axis=1)
    other = shifted(mine, "c", 1)
    return jnp.concatenate(
        [jnp.where(c == 0, mine, other), jnp.where(c == 0, other, mine)], axis=1
    ).astype(F32)


def shards(mesh_latent, w_hidden, w_out, target, slots, lengths):
    width = mesh_latent.shape[1]
    grid_rows = target.shape[1]
    total = mesh_latent.shape[0] * lax.axis_size(MEMBER)
    before = shifted(mesh_latent, SPACE, 1)
    after = shifted(mesh_latent, SPACE, -1)
    extended = jnp.concatenate([before, mesh_latent, after], axis=1)
    positions = jnp.arange(3 * width, dtype=jnp.int32)
    counts_f = jnp.zeros((grid_rows, 3 * width), F32)
    for k in range(3):
        counts_f = counts_f + (slots[k][:, None] == positions[None, :]).astype(F32)
    counts = counts_f.astype(BF16)
    area = jnp.einsum("gs,msl->mgl", counts, extended, preferred_element_type=F32).astype(BF16)
    pre = jnp.einsum("mgl,lj->mgj", area, w_hidden, preferred_element_type=F32)
    hidden = jax.nn.silu(pre).astype(BF16)
    pred = jnp.einsum("cj,mgj->mcg", w_out, hidden, preferred_element_type=F32).astype(BF16)
    live = (jnp.arange(grid_rows, dtype=jnp.int32) < lengths[0]).astype(F32)
    pair = jnp.concatenate([pred, shifted(pred, "xl", 1)], axis=0)
    everyone = jnp.concatenate([pair, shifted(pair, "c", 1)], axis=0)
    dpred = loss_grad(pred, everyone, target, live, total)
    dz = jnp.einsum("mcg,cj->mgj", dpred, w_out, preferred_element_type=F32)
    sig = jax.nn.sigmoid(pre)
    dpre = (dz * sig * (1.0 + pre * (1.0 - sig))).astype(BF16)
    grad = jnp.einsum("mgi,mgj->ij", area, dpre, preferred_element_type=F32).astype(BF16)
    grad_hidden = reduce_rows(grad)
    darea = jnp.einsum("mgj,ij->mgi", dpre, w_hidden, preferred_element_type=F32).astype(BF16)
    dext = jnp.einsum("gs,mgi->msi", counts, darea, preferred_element_type=F32)
    from_right = shifted(dext[:, :width].astype(BF16), SPACE, -1).astype(F32)
    from_left = shifted(dext[:, 2 * width :].astype(BF16), SPACE, 1).astype(F32)
    grad_mesh = (dext[:, width : 2 * width] + from_right + from_left).astype(BF16)
    return (grad_hidden, grad_mesh)


def solution(mesh):
    finer = Mesh(mesh.devices.reshape(2, 2, 4, 8, 2), NAMES)
    in_specs = (P(MEMBER, SPACE, None), P(), P(), P(None, SPACE), P(None, SPACE), P(SPACE))
    out_specs = (P(SPACE, None), P(MEMBER, SPACE, None))
    return jax.shard_map(
        shards, mesh=finer, in_specs=in_specs, out_specs=out_specs, check_vma=False
    )
```

time: 191 us -> 134 us (0.70)
  waiting for transfers between devices: 109 us -> 57.8 us
  starting transfers between devices: 17.3 us -> 38.7 us
  blocking collectives: 16.7 us -> 0 us
  between operations: 14.5 us -> 1.54 us
  other arithmetic: 5.55 us -> 9.83 us
  matrix products: 18.6 us -> 16.6 us
    reduce_scatter x3 -> x0, waiting for transfers between devices: 93.2 us -> none  [sum_by_axis(): total = lax.psum_scatter(total, axis, scatter_dimension=0, tiled=True)]
    ppermute x4 -> x12, waiting for transfers between devices: 15.3 us -> 57.8 us  [shifted(): lax.ppermute(value, axes, [(i, (i + steps) % count) for i in range(count)])]
    all_gather x3 -> x0, blocking collectives: 16.7 us -> none  [the longest x2 10.5 us: stacked_from(): parts = lax.all_gather(parts, axes[k])]
    all_to_all x0 -> x1, starting transfers between devices: none -> 11.6 us  [reduce_rows(): got = lax.all_to_all(parts, ('xl', 'z', 'xh'), 0, 0)]
    ppermute x4 -> x12, starting transfers between devices: 17.2 us -> 27.1 us  [shifted(): lax.ppermute(value, axes, [(i, (i + steps) % count) for i in range(count)])]
    convert_element_type x5 -> x8, other arithmetic: 3.52 us -> 7.09 us  [the longest x1 2.28 us: reduce_rows(): (keep.astype(F32) + got.astype(F32)).astype(BF16)]
    dot_general x6, matrix products: 18.6 us -> 16.6 us  [the longest x1 7.21 us: shards(): dext = jnp.einsum('gs,mgi->msi', counts, darea, preferred_element_type=F32)]
    unnamed x10 -> x23, local copies, waits for them, and re-layouts: 4.57 us -> 4.61 us
  transfers between devices with their start and end apart: 7 -> 13, of which waited for: 6 -> 10; matrix products, arithmetic and copies ran while one was open for 7% -> 10% of each run, Pallas kernels for 0% -> 0%
where the time goes in v1:
time: 134 us
  waiting for transfers between devices  57.8 us (43%)
  starting transfers between devices  38.7 us (29%)
  matrix products  16.6 us (12%)
  other arithmetic  9.83 us (7%)
  local copies, waits for them, and re-layouts  9.39 us (7%)
  between operations  1.54 us (1%)
    ppermute x12, waiting for transfers between devices, shifted(): lax.ppermute(value, axes, [(i, (i + steps) % count) for i in range(count)])  57.8 us
    ppermute x12, starting transfers between devices, shifted(): lax.ppermute(value, axes, [(i, (i + steps) % count) for i in range(count)])  27.1 us
    all_to_all x1, starting transfers between devices, reduce_rows(): got = lax.all_to_all(parts, ('xl', 'z', 'xh'), 0, 0)  11.6 us
    dot_general x1, matrix products, shards(): dext = jnp.einsum('gs,mgi->msi', counts, darea, preferred_element_type=F32)  7.21 us
    unnamed x23, local copies, waits for them, and re-layouts  4.61 us
  transfers between devices with their start and end apart: 13, of which 10 were waited for; matrix products, arithmetic and copies ran while one was open for 10% of the time, Pallas kernels for 0%

profile of v1, /device:TPU:1, one launch (start us, length us, event | category | flops | bytes accessed | tf_op | source)
XLA Modules:
  0.0 133.8 jit_solution(2972422694603005050)
XLA Ops:
  0.6 1.5 %copy.33 = bf16[2,128,1024]{1,2,0:T(8,128)(2,1)S(1)} copy(bf16[2,128,1024]{2,1,0:T(8,128)(2,1)} %param.6) | data formatting | bytes 1048576 | tf_op args[0]
  2.1 11.4 %collective-permute-start.1 = (bf16[2,128,1024]{1,2,0:T(8,128)(2,1)S(1)}, bf16[2,128,1024]{1,2,0:T(8,128)(2,1)S(1)}, u32[]{:S(2)}, u32[]{:S(2)}) collective-permute-start(bf16[2,128,1024]{1,2,0:T(8,128)(2,1)S(1)} %copy.33), channel_id=1, source_target_pairs={{0,63},{1,0},{2,1},{3,2},{4,3},{5,4},{6,5},{7,6},{8,7},{9,8},{10,9... | collective-permute-start | bytes 1572872 | tf_op jit(solution)/shard_map/ppermute | solution.py:32
  14.3 9.8 %collective-permute-done.1 = bf16[2,128,1024]{1,2,0:T(8,128)(2,1)S(1)} collective-permute-done((bf16[2,128,1024]{1,2,0:T(8,128)(2,1)S(1)}, bf16[2,128,1024]{1,2,0:T(8,128)(2,1)S(1)}, u32[]{:S(2)}, u32[]{:S(2)}) %collective-permute-start.1) | collective-permute-done | bytes 524320 | tf_op jit(solution)/shard_map/ppermute | solution.py:32
  24.1 7.6 %collective-permute-done = bf16[2,128,1024]{1,2,0:T(8,128)(2,1)S(1)} collective-permute-done((bf16[2,128,1024]{1,2,0:T(8,128)(2,1)S(1)}, bf16[2,128,1024]{1,2,0:T(8,128)(2,1)S(1)}, u32[]{:S(2)}, u32[]{:S(2)}) %collective-permute-start) | collective-permute-done | bytes 524320 | tf_op jit(solution)/shard_map/ppermute | solution.py:32
  31.7 1.5 %convolution_convert_fusion = bf16[2,1024,512]{2,1,0:T(8,128)(2,1)S(1)} fusion(bf16[2,128,1024]{1,2,0:T(8,128)(2,1)S(1)} %collective-permute-done.1, bf16[2,128,1024]{1,2,0:T(8,128)(2,1)S(1)} %copy.33, bf16[2,128,1024]{1,2,0:T(8,128)(2,1)S(1)} %collective-permute-done, s32[512]{0:T(512)S(1)} %bitcast.64, s32[512]{0:T(512)S(1)} %bitcast.66, s32[512]{0:T(512)S(1)} %bitcast.62), kind=kOutput, calls=%fused_computation.20 | convolution fusion | flops 812843008 | bytes 3676160 | tf_op jit(solution)/shard_map/gs,msl->mgl/dot_general | solution.py:92
  33.3 2.4 %fusion.5 = f32[2,512,1024]{2,1,0:T(8,128)S(1)} fusion(bf16[1024,1024]{1,0:T(8,128)(2,1)S(1)} %copy-done, bf16[2,1024,512]{2,1,0:T(8,128)(2,1)S(1)} %convolution_convert_fusion), kind=kOutput, calls=%fused_computation.11 | convolution fusion | flops 2147483648 | bytes 8388608 | tf_op jit(solution)/shard_map/mgl,lj->mgj/dot_general | solution.py:93
  35.8 1.3 fusion.24
  38.3 4.3 %collective-permute-done.2 = bf16[2,100,512]{2,0,1:T(2,128)(2,1)S(1)} collective-permute-done((bf16[2,100,512]{2,0,1:T(2,128)(2,1)S(1)}, bf16[2,100,512]{2,0,1:T(2,128)(2,1)S(1)}, u32[]{:S(2)}, u32[]{:S(2)}) %collective-permute-start.2) | collective-permute-done | bytes 204832 | tf_op jit(solution)/shard_map/ppermute | solution.py:32
  42.6 1.2 pad_maximum_fusion
  43.7 3.0 %collective-permute-start.3 = (bf16[4,100,512]{2,0,1:T(4,128)(2,1)}, bf16[4,100,512]{2,0,1:T(4,128)(2,1)S(1)}, u32[]{:S(2)}, u32[]{:S(2)}) collective-permute-start(bf16[4,100,512]{2,0,1:T(4,128)(2,1)} %pad_maximum_fusion), channel_id=1, source_target_pairs={{0,64},{64,0},{1,65},{65,1},{2,66},{66,2},{3,67},{67,3},{4,68},{68... | collective-permute-start | bytes 1228808 | tf_op jit(solution)/shard_map/ppermute | solution.py:32
  48.9 1.4 %fusion.2 = f32[2,100,512]{2,1,0:T(8,128)S(1)} fusion(f32[8,100,512]{2,0,1:T(8,128)S(1)} %maximum_convert_fusion, f32[2,100,512]{2,1,0:T(8,128)S(1)} %copy.38), kind=kLoop, calls=%fused_computation.8 | loop fusion | flops 3993600 | bytes 2457600 | tf_op jit(solution)/shard_map/reduce_sum | solution.py:46
  51.0 1.8 %multiply_convert_fusion = bf16[2,512,1024]{2,1,0:T(8,128)(2,1)S(1)} fusion(f32[2,512,1024]{2,1,0:T(8,128)S(1)} %copy-done.8, bf16[100,1024]{1,0:T(8,128)(2,1)S(1)} %copy-done.4, bf16[2,100,512]{2,0,1:T(2,128)(2,1)S(1)} %fusion.32), kind=kOutput, calls=%fused_computation.3 | convolution fusion | flops 219152384 | bytes 6701056 | tf_op jit(solution)/shard_map/mcg,cj->mgj/dot_general | solution.py:100
  52.8 2.3 %bitcast_convert_fusion = bf16[1024,1024]{1,0:T(8,128)(2,1)S(1)} fusion(bf16[2,512,1024]{2,1,0:T(8,128)(2,1)S(1)} %multiply_convert_fusion, bf16[2,1024,512]{2,1,0:T(8,128)(2,1)S(1)} %copy-done.6), kind=kOutput, calls=%fused_computation.2 | convolution fusion | flops 2148532224 | bytes 6291456 | tf_op jit(solution)/shard_map/mgi,mgj->ij/dot_general | solution.py:103
  55.2 1.3 copy-done.1
  57.1 2.4 %collective-permute-done.4 = bf16[1024,512]{1,0:T(8,128)(2,1)} collective-permute-done((bf16[1024,512]{1,0:T(8,128)(2,1)S(1)}, bf16[1024,512]{1,0:T(8,128)(2,1)}, u32[]{:S(2)}, u32[]{:S(2)}) %collective-permute-start.4) | collective-permute-done | bytes 1048608 | tf_op jit(solution)/shard_map/ppermute | solution.py:32
  59.5 2.3 %add_convert_fusion = bf16[1024,512]{1,0:T(8,128)(2,1)S(1)} fusion(bf16[1024,512]{1,0:T(8,128)(2,1)} %collective-permute-done.4, pred[]{:T(512)S(6)} %eq.58, bf16[1024,1024]{1,0:T(8,128)(2,1)} %copy-done.1), kind=kLoop, calls=%fused_computation.17 | loop fusion | flops 2621440 | bytes 4194305 | tf_op jit(solution)/shard_map/convert_element_type | solution.py:59
  61.8 0.9 dynamic-slice_bitcast_fusion.2
  64.1 6.3 %collective-permute-done.7 = bf16[256,512]{1,0:T(8,128)(2,1)} collective-permute-done((bf16[256,512]{1,0:T(8,128)(2,1)}, bf16[256,512]{1,0:T(8,128)(2,1)}, u32[]{:S(2)}, u32[]{:S(2)}) %collective-permute-start.7) | collective-permute-done | bytes 262176 | tf_op jit(solution)/shard_map/ppermute | solution.py:32
  70.5 1.7 %collective-permute-done.6 = bf16[256,512]{1,0:T(8,128)(2,1)} collective-permute-done((bf16[256,512]{1,0:T(8,128)(2,1)}, bf16[256,512]{1,0:T(8,128)(2,1)}, u32[]{:S(2)}, u32[]{:S(2)}) %collective-permute-start.6) | collective-permute-done | bytes 262176 | tf_op jit(solution)/shard_map/ppermute | solution.py:32
  72.2 6.6 %collective-permute-done.5 = bf16[256,512]{1,0:T(8,128)(2,1)} collective-permute-done((bf16[256,512]{1,0:T(8,128)(2,1)S(1)}, bf16[256,512]{1,0:T(8,128)(2,1)}, u32[]{:S(2)}, u32[]{:S(2)}) %collective-permute-start.5) | collective-permute-done | bytes 262176 | tf_op jit(solution)/shard_map/ppermute | solution.py:32
  78.8 1.3 fusion.29
  80.9 11.6 %all-to-all-start = ((bf16[32,16,256]{2,1,0:T(8,128)(2,1)}), bf16[32,16,256]{2,1,0:T(8,128)(2,1)S(1)}, u32[]{:S(2)}, u32[]{:S(2)}) async-start(bf16[32,16,256]{2,1,0:T(8,128)(2,1)} %bitcast.16), calls=%async_computation | async-start | bytes 524288 | tf_op jit(solution)/shard_map/all_to_all | solution.py:69
  92.5 7.2 %fusion.50 = (bf16[2,384,1024]{1,2,0:T(8,128)(2,1)}, f32[2,384,1024]{1,2,0:T(8,128)}) fusion(s32[512]{0:T(512)S(1)} %bitcast.65, s32[512]{0:T(512)S(1)} %bitcast.67, s32[512]{0:T(512)S(1)} %bitcast.63, bf16[2,512,1024]{2,1,0:T(8,128)(2,1)} %copy-done.9, bf16[1024,1024]{1,0:T(8,128)(2,1)S(1)} %copy-done), kind=kOutput, calls=%fused_computation.71 | convolution fusion | flops 2956394496 | bytes 8919040 | tf_op jit(solution)/shard_map/gs,mgi->msi/dot_general | solution.py:106
  99.7 2.2 %fusion.48 = (bf16[2,128,1024]{1,2,0:T(8,128)(2,1)}, bf16[2,128,1024]{1,2,0:T(8,128)(2,1)}) fusion(bf16[2,384,1024]{1,2,0:T(8,128)(2,1)} %get-tuple-element.24), kind=kLoop, calls=%fused_computation.69 | loop fusion | bytes 2097152 | tf_op jit(solution)/shard_map/slice | solution.py:107
  101.9 2.5 %collective-permute-start.11 = (bf16[2,128,1024]{1,2,0:T(8,128)(2,1)}, bf16[2,128,1024]{1,2,0:T(8,128)(2,1)S(1)}, u32[]{:S(2)}, u32[]{:S(2)}) collective-permute-start(bf16[2,128,1024]{1,2,0:T(8,128)(2,1)} %get-tuple-element.13), channel_id=1, source_target_pairs={{0,1},{1,2},{2,3},{3,4},{4,5},{5,6},{6,7},{7,8},{8,9},{9,10},{10,1... | collective-permute-start | bytes 1572872 | tf_op jit(solution)/shard_map/ppermute | solution.py:32
  104.5 4.7 %collective-permute-start.10 = (bf16[2,128,1024]{1,2,0:T(8,128)(2,1)}, bf16[2,128,1024]{1,2,0:T(8,128)(2,1)}, u32[]{:S(2)}, u32[]{:S(2)}) collective-permute-start(bf16[2,128,1024]{1,2,0:T(8,128)(2,1)} %get-tuple-element.12), channel_id=1, source_target_pairs={{0,63},{1,0},{2,1},{3,2},{4,3},{5,4},{6,5},{7,6},{8,7},{9,8},{10,9... | collective-permute-start | bytes 1572872 | tf_op jit(solution)/shard_map/ppermute | solution.py:32
  109.2 1.1 collective-permute-start.8
  110.3 17.0 %collective-permute-done.8 = bf16[16,256]{1,0:T(8,128)(2,1)S(1)} collective-permute-done((bf16[16,256]{1,0:T(8,128)(2,1)S(1)}, bf16[16,256]{1,0:T(8,128)(2,1)S(1)}, u32[]{:S(2)}, u32[]{:S(2)}) %collective-permute-start.8) | collective-permute-done | bytes 8224 | tf_op jit(solution)/shard_map/ppermute | solution.py:32
  127.3 2.1 %collective-permute-start.9 = (bf16[16,512]{1,0:T(8,128)(2,1)S(1)}, bf16[16,512]{1,0:T(8,128)(2,1)S(1)}, u32[]{:S(2)}, u32[]{:S(2)}) collective-permute-start(bf16[16,512]{1,0:T(8,128)(2,1)S(1)} %pad_maximum_fusion.1), channel_id=1, source_target_pairs={{0,64},{64,0},{1,65},{65,1},{2,66},{66,2},{3,67},{67,3},{4,68},{68... | collective-permute-start | bytes 49160 | tf_op jit(solution)/shard_map/ppermute | solution.py:32
  129.3 1.2 collective-permute-done.10
  130.5 1.6 %fusion.26 = bf16[2,128,1024]{1,2,0:T(8,128)(2,1)S(1)} fusion(f32[2,384,1024]{1,2,0:T(8,128)} %get-tuple-element.25, bf16[2,128,1024]{1,2,0:T(8,128)(2,1)S(1)} %collective-permute-done.11, bf16[2,128,1024]{1,2,0:T(8,128)(2,1)} %collective-permute-done.10), kind=kLoop, calls=%fused_computation.29 | loop fusion | flops 1310720 | bytes 2621440 | tf_op jit(solution)/shard_map/convert_element_type | solution.py:109
  132.1 1.0 copy.43
  (44 shorter events, 7.8 us)
Async XLA Ops:
  0.6 32.7 %copy-start = (bf16[1024,1024]{1,0:T(8,128)(2,1)S(1)}, bf16[1024,1024]{1,0:T(8,128)(2,1)}, u32[]{:S(2)}) copy-start(bf16[1024,1024]{1,0:T(8,128)(2,1)} %param.7) | copy-start | bytes 6291460
  2.1 22.0 %collective-permute-start.1 = (bf16[2,128,1024]{1,2,0:T(8,128)(2,1)S(1)}, bf16[2,128,1024]{1,2,0:T(8,128)(2,1)S(1)}, u32[]{:S(2)}, u32[]{:S(2)}) collective-permute-start(bf16[2,128,1024]{1,2,0:T(8,128)(2,1)S(1)} %copy.33), channel_id=1, source_target_pairs={{0,63},{1,0},{2,1},{3,2},{4,3},{5,4},{6,5},{7,6},{8,7},{9,8},{10,9... | collective-permute-start | bytes 1572872 | tf_op jit(solution)/shard_map/ppermute | solution.py:32
  13.5 18.3 %collective-permute-start = (bf16[2,128,1024]{1,2,0:T(8,128)(2,1)S(1)}, bf16[2,128,1024]{1,2,0:T(8,128)(2,1)S(1)}, u32[]{:S(2)}, u32[]{:S(2)}) collective-permute-start(bf16[2,128,1024]{1,2,0:T(8,128)(2,1)S(1)} %copy.33), channel_id=1, source_target_pairs={{0,1},{1,2},{2,3},{3,4},{4,5},{5,6},{6,7},{7,8},{8,9},{9,10},{10,1... | collective-permute-start | bytes 1572872 | tf_op jit(solution)/shard_map/ppermute | solution.py:32
  33.3 2.4 %copy-start.5 = (bf16[2,1024,512]{2,1,0:T(8,128)(2,1)}, bf16[2,1024,512]{2,1,0:T(8,128)(2,1)S(1)}, u32[]{:S(2)}) copy-start(bf16[2,1024,512]{2,1,0:T(8,128)(2,1)S(1)} %convolution_convert_fusion) | copy-start | bytes 6291460
  33.3 2.4 %copy-start.3 = (bf16[100,1024]{1,0:T(8,128)(2,1)S(1)}, bf16[100,1024]{1,0:T(8,128)(2,1)}, u32[]{:S(2)}) copy-start(bf16[100,1024]{1,0:T(8,128)(2,1)} %param.8) | copy-start | bytes 614404
  35.8 1.9 %copy-start.7 = (f32[2,512,1024]{2,1,0:T(8,128)}, f32[2,512,1024]{2,1,0:T(8,128)S(1)}, u32[]{:S(2)}) copy-start(f32[2,512,1024]{2,1,0:T(8,128)S(1)} %fusion.5) | copy-start | bytes 12582916
  35.8 10.9 %copy-start.2 = (bf16[100,512]{1,0:T(8,128)(2,1)S(1)}, bf16[100,512]{1,0:T(8,128)(2,1)}, u32[]{:S(2)}) copy-start(bf16[100,512]{1,0:T(8,128)(2,1)} %param.9) | copy-start | bytes 307204
  37.9 4.7 %collective-permute-start.2 = (bf16[2,100,512]{2,0,1:T(2,128)(2,1)S(1)}, bf16[2,100,512]{2,0,1:T(2,128)(2,1)S(1)}, u32[]{:S(2)}, u32[]{:S(2)}) collective-permute-start(bf16[2,100,512]{2,0,1:T(2,128)(2,1)S(1)} %bitcast.57), channel_id=1, source_target_pairs={{0,128},{128,0},{1,129},{129,1},{2,130},{130,2},{3,131},{131,3},{4... | collective-permute-start | bytes 614408 | tf_op jit(solution)/shard_map/ppermute | solution.py:32
  43.7 4.5 %collective-permute-start.3 = (bf16[4,100,512]{2,0,1:T(4,128)(2,1)}, bf16[4,100,512]{2,0,1:T(4,128)(2,1)S(1)}, u32[]{:S(2)}, u32[]{:S(2)}) collective-permute-start(bf16[4,100,512]{2,0,1:T(4,128)(2,1)} %pad_maximum_fusion), channel_id=1, source_target_pairs={{0,64},{64,0},{1,65},{65,1},{2,66},{66,2},{3,67},{67,3},{4,68},{68... | collective-permute-start | bytes 1228808 | tf_op jit(solution)/shard_map/ppermute | solution.py:32
  48.3 2.7 %copy-start.8 = (f32[2,512,1024]{2,1,0:T(8,128)S(1)}, f32[2,512,1024]{2,1,0:T(8,128)}, u32[]{:S(2)}) copy-start(f32[2,512,1024]{2,1,0:T(8,128)} %copy-done.7) | copy-start | bytes 12582916
  48.9 2.1 %copy-start.4 = (bf16[100,1024]{1,0:T(8,128)(2,1)S(1)}, bf16[100,1024]{1,0:T(8,128)(2,1)}, u32[]{:S(2)}) copy-start(bf16[100,1024]{1,0:T(8,128)(2,1)} %param.8) | copy-start | bytes 614404
  51.0 1.8 %copy-start.6 = (bf16[2,1024,512]{2,1,0:T(8,128)(2,1)S(1)}, bf16[2,1024,512]{2,1,0:T(8,128)(2,1)}, u32[]{:S(2)}) copy-start(bf16[2,1024,512]{2,1,0:T(8,128)(2,1)} %copy-done.5) | copy-start | bytes 6291460
  52.8 2.4 %copy-start.9 = (bf16[2,512,1024]{2,1,0:T(8,128)(2,1)}, bf16[2,512,1024]{2,1,0:T(8,128)(2,1)S(1)}, u32[]{:S(2)}) copy-start(bf16[2,512,1024]{2,1,0:T(8,128)(2,1)S(1)} %multiply_convert_fusion) | copy-start | bytes 6291460
  55.2 1.3 %copy-start.1 = (bf16[1024,1024]{1,0:T(8,128)(2,1)}, bf16[1024,1024]{1,0:T(8,128)(2,1)S(1)}, u32[]{:S(2)}) copy-start(bf16[1024,1024]{1,0:T(8,128)(2,1)S(1)} %bitcast_convert_fusion) | copy-start | bytes 6291460
  56.6 2.9 %collective-permute-start.4 = (bf16[1024,512]{1,0:T(8,128)(2,1)S(1)}, bf16[1024,512]{1,0:T(8,128)(2,1)}, u32[]{:S(2)}, u32[]{:S(2)}) collective-permute-start(bf16[1024,512]{1,0:T(8,128)(2,1)S(1)} %broadcast_select_fusion), channel_id=1, source_target_pairs={{0,64},{64,0},{1,65},{65,1},{2,66},{66,2},{3,67},{67,3},{4,68},{68... | collective-permute-start | bytes 3145736 | tf_op jit(solution)/shard_map/ppermute | solution.py:32
  62.6 7.8 %collective-permute-start.7 = (bf16[256,512]{1,0:T(8,128)(2,1)}, bf16[256,512]{1,0:T(8,128)(2,1)}, u32[]{:S(2)}, u32[]{:S(2)}) collective-permute-start(bf16[256,512]{1,0:T(8,128)(2,1)} %get-tuple-element.15), channel_id=1, source_target_pairs={{0,48},{16,0},{32,16},{48,32},{1,49},{17,1},{33,17},{49,33},{2,50}... | collective-permute-start | bytes 786440 | tf_op jit(solution)/shard_map/ppermute | solution.py:32
  63.1 9.1 %collective-permute-start.6 = (bf16[256,512]{1,0:T(8,128)(2,1)}, bf16[256,512]{1,0:T(8,128)(2,1)}, u32[]{:S(2)}, u32[]{:S(2)}) collective-permute-start(bf16[256,512]{1,0:T(8,128)(2,1)} %get-tuple-element.16), channel_id=1, source_target_pairs={{0,32},{16,48},{32,0},{48,16},{1,33},{17,49},{33,1},{49,17},{2,34}... | collective-permute-start | bytes 786440 | tf_op jit(solution)/shard_map/ppermute | solution.py:32
  63.4 15.3 %collective-permute-start.5 = (bf16[256,512]{1,0:T(8,128)(2,1)S(1)}, bf16[256,512]{1,0:T(8,128)(2,1)}, u32[]{:S(2)}, u32[]{:S(2)}) collective-permute-start(bf16[256,512]{1,0:T(8,128)(2,1)S(1)} %get-tuple-element.14), channel_id=1, source_target_pairs={{0,16},{16,32},{32,48},{48,0},{1,17},{17,33},{33,49},{49,1},{2,18}... | collective-permute-start | bytes 786440 | tf_op jit(solution)/shard_map/ppermute | solution.py:32
  80.9 28.3 %all-to-all-start = ((bf16[32,16,256]{2,1,0:T(8,128)(2,1)}), bf16[32,16,256]{2,1,0:T(8,128)(2,1)S(1)}, u32[]{:S(2)}, u32[]{:S(2)}) async-start(bf16[32,16,256]{2,1,0:T(8,128)(2,1)} %bitcast.16), calls=%async_computation | async-start | bytes 524288 | tf_op jit(solution)/shard_map/all_to_all | solution.py:69
  101.9 27.4 %collective-permute-start.11 = (bf16[2,128,1024]{1,2,0:T(8,128)(2,1)}, bf16[2,128,1024]{1,2,0:T(8,128)(2,1)S(1)}, u32[]{:S(2)}, u32[]{:S(2)}) collective-permute-start(bf16[2,128,1024]{1,2,0:T(8,128)(2,1)} %get-tuple-element.13), channel_id=1, source_target_pairs={{0,1},{1,2},{2,3},{3,4},{4,5},{5,6},{6,7},{7,8},{8,9},{9,10},{10,1... | collective-permute-start | bytes 1572872 | tf_op jit(solution)/shard_map/ppermute | solution.py:32
  104.5 26.1 %collective-permute-start.10 = (bf16[2,128,1024]{1,2,0:T(8,128)(2,1)}, bf16[2,128,1024]{1,2,0:T(8,128)(2,1)}, u32[]{:S(2)}, u32[]{:S(2)}) collective-permute-start(bf16[2,128,1024]{1,2,0:T(8,128)(2,1)} %get-tuple-element.12), channel_id=1, source_target_pairs={{0,63},{1,0},{2,1},{3,2},{4,3},{5,4},{6,5},{7,6},{8,7},{9,8},{10,9... | collective-permute-start | bytes 1572872 | tf_op jit(solution)/shard_map/ppermute | solution.py:32
  109.2 18.1 %collective-permute-start.8 = (bf16[16,256]{1,0:T(8,128)(2,1)S(1)}, bf16[16,256]{1,0:T(8,128)(2,1)S(1)}, u32[]{:S(2)}, u32[]{:S(2)}) collective-permute-start(bf16[16,256]{1,0:T(8,128)(2,1)S(1)} %reduce_sum.22), channel_id=1, source_target_pairs={{0,128},{128,0},{1,129},{129,1},{2,130},{130,2},{3,131},{131,3},{4... | collective-permute-start | bytes 24584 | tf_op jit(solution)/shard_map/ppermute | solution.py:32
  127.3 5.9 %collective-permute-start.9 = (bf16[16,512]{1,0:T(8,128)(2,1)S(1)}, bf16[16,512]{1,0:T(8,128)(2,1)S(1)}, u32[]{:S(2)}, u32[]{:S(2)}) collective-permute-start(bf16[16,512]{1,0:T(8,128)(2,1)S(1)} %pad_maximum_fusion.1), channel_id=1, source_target_pairs={{0,64},{64,0},{1,65},{65,1},{2,66},{66,2},{3,67},{67,3},{4,68},{68... | collective-permute-start | bytes 49160 | tf_op jit(solution)/shard_map/ppermute | solution.py:32

commit v2 on v1

v2 whole, which is shorter than its diff:
```python
import functools
import itertools

import jax
import jax.numpy as jnp
from jax import lax
from jax.experimental import pallas as pl
from jax.experimental.pallas import tpu as pltpu
from jax.sharding import Mesh
from jax.sharding import PartitionSpec as P

NAMES = ("xl", "c", "y", "z", "xh")
MEMBER = ("xl", "c")
SPACE = ("y", "z", "xh")
BF16 = jnp.bfloat16
F32 = jnp.float32
VMEM = pl.BlockSpec(memory_space=pltpu.VMEM)
SMEM = pl.BlockSpec(memory_space=pltpu.SMEM)
grant = 16 << 20

fair_eps = 0.05
smooth_sq = 0.01
chunk = 256


def permute(value, axes, moved):
    sizes = [lax.axis_size(a) for a in axes]
    pairs = []
    for at in itertools.product(*[range(s) for s in sizes]):
        source = target = 0
        for size, a, b in zip(sizes, at, moved(*at)):
            source, target = source * size + a, target * size + b % size
        pairs.append((source, target))
    return lax.ppermute(value, axes if len(axes) > 1 else axes[0], pairs)


def shifted(value, axis, steps):
    return permute(value, (axis,), lambda i: (i + steps,))


def relayed(value, sign):
    n_y, n_z = lax.axis_size("y"), lax.axis_size("z")

    def moved(y, z, xh):
        k = (y * n_z + z + (sign if xh == 0 else -sign)) % (n_y * n_z)
        return (k // n_z, k % n_z, xh)

    return permute(value, SPACE, moved)


def call(kernel, out_shape, *args, scalars=0, final=False):
    on_chip = [pltpu.with_memory_space_constraint(a, pltpu.VMEM) for a in args[scalars:]]
    return pl.pallas_call(
        kernel,
        out_shape=[
            jax.ShapeDtypeStruct(*s) if final else pltpu.VMEM(*s) for s in out_shape
        ],
        in_specs=[SMEM] * scalars + [VMEM] * len(on_chip),
        out_specs=[VMEM] * len(out_shape),
        compiler_params=pltpu.CompilerParams(vmem_limit_bytes=grant),
    )(*args[:scalars], *on_chip)


def dot(a, b, ca=1, cb=0):
    return lax.dot_general(a, b, (((ca,), (cb,)), ((), ())), preferred_element_type=F32)


def stage_kernel(slots_ref, *refs):
    sources, (counts_ref, flipped_ref, *targets, sems) = refs[:3], refs[3:]
    copies = [
        pltpu.make_async_copy(a, b, sems.at[k]) for k, (a, b) in enumerate(zip(sources, targets))
    ]
    for copy in copies:
        copy.start()
    n, g = flipped_ref.shape
    xh = lax.axis_index("xh")
    at = lax.broadcasted_iota(jnp.int32, (n, g), 0)
    width = n // 3
    far = jnp.where(xh == 0, 0, 2 * width)
    near = jnp.where(xh == 0, 2 * width, 0)
    start = jnp.where(at < width, width, jnp.where(at < 2 * width, near - width, far - 2 * width))
    moved = at + start
    total = jnp.zeros((n, g), F32)
    for k in range(3):
        total = total + jnp.where(slots_ref[k : k + 1, :] == moved, 1.0, 0.0)
    flipped_ref[...] = total.astype(BF16)
    counts_ref[...] = total.T.astype(BF16)
    for copy in copies:
        copy.wait()


def staged(slots, sources, grid_rows, nodes):
    shapes = [((grid_rows, nodes), BF16), ((nodes, grid_rows), BF16)]
    shapes += [(a.shape, a.dtype) for a in sources]
    return pl.pallas_call(
        stage_kernel,
        out_shape=[pltpu.VMEM(shape, dtype) for shape, dtype in shapes],
        in_specs=[VMEM] + [pl.BlockSpec(memory_space=pl.ANY)] * len(sources),
        out_specs=[VMEM] * len(shapes),
        scratch_shapes=[pltpu.SemaphoreType.DMA((len(sources),))],
        compiler_params=pltpu.CompilerParams(vmem_limit_bytes=grant),
    )(slots, *sources)


def forward_kernel(counts_ref, own_ref, rec_ref, fwd_ref, w_ref, wo_ref, turned_ref, gate_ref, pred_ref):
    extended = jnp.concatenate([own_ref[...], rec_ref[...], fwd_ref[...]], axis=0)
    area = dot(counts_ref[...], extended).astype(BF16)
    turned_ref[...] = area.T
    total = None
    for n in range(0, w_ref.shape[1], chunk):
        pre = dot(area, w_ref[:, n : n + chunk])
        sig = 0.5 * jnp.tanh(0.5 * pre) + 0.5
        value = pre * sig
        gate_ref[:, n : n + chunk] = (sig * (1.0 + (pre - value))).astype(BF16)
        part = dot(wo_ref[:, n : n + chunk], value.astype(BF16), 1, 1)
        total = part if total is None else total + part
    pred_ref[...] = total.astype(BF16)


def smooth_sign(value):
    return value * lax.rsqrt(value * value + smooth_sq)


def half_slopes(start, half, wo_ref, gates, dps, slopes, turned, out):
    cols = pl.ds(pl.multiple_of(start, half), half)
    wo = wo_ref[:, cols]
    part = None
    for dp, gate, slope, area in zip(dps, gates, slopes, turned):
        value = (dot(dp[...], wo, 0, 0) * gate[:, cols].astype(F32)).astype(BF16)
        slope[...] = value
        more = dot(area[...], value)
        part = more if part is None else part + more
    out[...] = part.astype(out.dtype)


def give_kernel(total, len_ref, *refs):
    preds, (target_ref, wo_ref, t0, t1, gate0, gate1, dp0, dp1, s0, s1, out) = refs[:8], refs[8:]
    channels, _ = target_ref.shape
    scale = (1.0 - fair_eps) / (total * (total - 1))
    for r in range(0, channels, 16):
        rows = slice(r, min(r + 16, channels))
        own = [preds[0][rows].astype(F32), preds[1][rows].astype(F32)]
        truth = target_ref[rows].astype(F32)
        mutual = smooth_sign(own[0] - own[1])
        pairs = [mutual, -mutual]
        for ref in preds[2:]:
            other = ref[rows].astype(F32)
            pairs = [p + smooth_sign(v - other) for p, v in zip(pairs, own)]
        at = lax.broadcasted_iota(jnp.int32, truth.shape, 1)
        for ref, v, p in zip((dp0, dp1), own, pairs):
            value = smooth_sign(v - truth) * (1.0 / total) - scale * p
            ref[rows] = jnp.where(at < len_ref[0], value, 0.0).astype(BF16)
    half = out.shape[1]
    start = (1 - lax.axis_index("c")) * half
    half_slopes(start, half, wo_ref, (gate0, gate1), (dp0, dp1), (s0, s1), (t0, t1), out)


def keep_kernel(wo_ref, t0, t1, gate0, gate1, dp0, dp1, s0, s1, out):
    half = out.shape[1]
    start = lax.axis_index("c") * half
    half_slopes(start, half, wo_ref, (gate0, gate1), (dp0, dp1), (s0, s1), (t0, t1), out)


def cores_kernel(keep_ref, got_ref, own_ref, *outs):
    size = own_ref.shape[0]
    n_y = len(outs) + 1
    for s, out in enumerate((own_ref,) + outs):
        to = lax.rem(lax.axis_index("y") + s, n_y)
        rows = pl.ds(pl.multiple_of(to * size, size), size)
        out[...] = (keep_ref[rows, :].astype(F32) + got_ref[rows, :].astype(F32)).astype(out.dtype)


def total_kernel(first_ref, *refs):
    total = first_ref[...].astype(F32)
    for ref in refs[:-1]:
        total = total + ref[...].astype(F32)
    refs[-1][...] = total.astype(refs[-1].dtype)


def columns_kernel(parts_ref, mine_ref, theirs_ref):
    size = mine_ref.shape[0]
    xh = lax.axis_index("xh")
    total = parts_ref[0].astype(F32)
    for k in range(1, parts_ref.shape[0]):
        total = total + parts_ref[k].astype(F32)
    first, second = total[:size], total[size:]
    mine_ref[...] = jnp.where(xh == 0, first, second).astype(BF16)
    theirs_ref[...] = jnp.where(xh == 0, second, first).astype(BF16)


def place_kernel(mine_ref, other_ref, out_ref):
    half = mine_ref.shape[1]
    first = lax.axis_index("c") == 0
    mine, other = mine_ref[...].astype(F32), other_ref[...].astype(F32)
    out_ref[:, :half] = jnp.where(first, mine, other)
    out_ref[:, half:] = jnp.where(first, other, mine)


def backward_kernel(flipped_ref, w_ref, give_ref, keep_ref, own_ref, rec_ref, fwd_ref):
    half = give_ref.shape[1]
    width = own_ref.shape[0]
    c = lax.axis_index("c")
    give = pl.ds(pl.multiple_of((1 - c) * half, half), half)
    keep = pl.ds(pl.multiple_of(c * half, half), half)
    for n in range(0, w_ref.shape[0], chunk):
        rows = slice(n, n + chunk)
        darea = dot(give_ref[...], w_ref[rows, give], 1, 1) + dot(keep_ref[...], w_ref[rows, keep], 1, 1)
        dext = dot(flipped_ref[...], darea.astype(BF16))
        own_ref[:, rows] = dext[:width]
        rec_ref[:, rows] = dext[width : 2 * width]
        fwd_ref[:, rows] = dext[2 * width :].astype(BF16)


def step(mesh_latent, w_hidden, w_out, target, slots, lengths):
    members, width, wide = mesh_latent.shape
    channels, grid_rows = target.shape
    total = members * lax.axis_size(MEMBER)
    half = wide // 2
    n_y, n_z, n_x = (lax.axis_size(a) for a in SPACE)

    own = [mesh_latent[m] for m in range(members)]
    rec = []
    for v in own:
        rec.append(shifted(v, "xh", 1))
    fwd = [relayed(v, 1) for v in rec]
    counts, flipped, w_hidden, w_out, target = staged(
        slots, (w_hidden, w_out, target), grid_rows, 3 * width
    )
    area, gate, pred = [], [], []
    for m in range(members):
        a, p, q = call(
            forward_kernel,
            [((wide, grid_rows), BF16), ((grid_rows, wide), BF16), ((channels, grid_rows), BF16)],
            counts, own[m], rec[m], fwd[m], w_hidden, w_out,
        )
        area.append(a)
        gate.append(p)
        pred.append(q)
    others = []
    for q in pred:
        others += [
            shifted(q, "xl", 1), permute(q, MEMBER, lambda a, b: (1 - a, 1 - b)), shifted(q, "c", 1)
        ]

    slope = ((grid_rows, half), BF16)
    part = ((wide, half), BF16)
    dp = ((channels, grid_rows), BF16)
    dp0, dp1, g0, g1, give = call(
        functools.partial(give_kernel, total), [dp, dp, slope, slope, part],
        lengths, *pred, *others, target, w_out, *area, *gate, scalars=1,
    )
    got = shifted(give, "c", 1)
    k0, k1, keep = call(keep_kernel, [slope, slope, part], w_out, *area, *gate, dp0, dp1)
    rows_y = (wide // n_y, half)
    mine, *give = call(cores_kernel, [(rows_y, F32)] + [(rows_y, BF16)] * (n_y - 1), keep, got)
    got = []
    for s, g in enumerate(give):
        got.append(shifted(g, "y", s + 1))

    node = ((width, wide), F32)
    back = []
    for g, k in ((g0, k0), (g1, k1)):
        back.append(
            call(backward_kernel, [node, node, ((width, wide), BF16)], flipped, w_hidden, g, k)
        )
    far = [relayed(b[2], -1) for b in back]
    far = [call(total_kernel, [((width, wide), BF16)], b[1], f)[0] for b, f in zip(back, far)]

    (rows,) = call(total_kernel, [(rows_y, BF16)], mine, *got)
    rows, far[0] = lax.optimization_barrier((rows, far[0]))
    far = [shifted(f, "xh", 1) for f in far]
    rows = lax.all_to_all(rows.reshape(n_z, wide // (n_y * n_z), half), "z", 0, 0)
    out_rows = (wide // (n_y * n_z * n_x), half)
    mine, theirs = call(columns_kernel, [(out_rows, BF16)] * 2, rows)
    (mine,) = call(
        total_kernel, [(out_rows, BF16)],
        mine, shifted(mine, "xl", 1), shifted(theirs, "xh", 1),
        permute(theirs, ("xl", "xh"), lambda a, b: (1 - a, 1 - b)),
    )
    (grad_hidden,) = call(place_kernel, [((out_rows[0], wide), F32)], mine, shifted(mine, "c", 1), final=True)
    grad_mesh = jnp.stack([(b[0] + f.astype(F32)).astype(BF16) for b, f in zip(back, far)])
    return (grad_hidden, grad_mesh)


def solution(mesh):
    finer = Mesh(mesh.devices.reshape(2, 2, 4, 8, 2), NAMES)
    in_specs = (P(MEMBER, SPACE, None), P(), P(), P(None, SPACE), P(None, SPACE), P(SPACE))
    out_specs = (P(SPACE, None), P(MEMBER, SPACE, None))
    return jax.shard_map(step, mesh=finer, in_specs=in_specs, out_specs=out_specs, check_vma=False)
```

time: 134 us -> 111 us (0.83)
  waiting for transfers between devices: 57.8 us -> 24.5 us
  starting transfers between devices: 38.7 us -> 59.2 us
  Pallas kernels: 0 us -> 19 us
  matrix products: 16.6 us -> 0 us
  other arithmetic: 9.83 us -> 0.94 us
  local copies, waits for them, and re-layouts: 9.39 us -> 5.18 us
    ppermute x12 -> x22, waiting for transfers between devices: 57.8 us -> 21.1 us  [permute(): return lax.ppermute(value, axes if len(axes) > 1 else axes[0], pairs)]
    ppermute x12 -> x22, starting transfers between devices: 27.1 us -> 51.4 us  [permute(): return lax.ppermute(value, axes if len(axes) > 1 else axes[0], pairs)]
    pallas_call x0 -> x14, Pallas kernels: none -> 19 us  [the longest x13 18.1 us: call(): pl.pallas_call(kernel, out_shape=[jax.ShapeDtypeStruct(*s) if final else...]
    dot_general x6 -> x0, matrix products: 16.6 us -> none  [the longest x1 7.21 us: shards(): dext = jnp.einsum('gs,mgi->msi', counts, darea, preferred_element_type=F32)]
    convert_element_type x8 -> x0, other arithmetic: 7.09 us -> none  [the longest x1 2.28 us: reduce_rows(): (keep.astype(F32) + got.astype(F32)).astype(BF16)]
    all_to_all x1, starting transfers between devices: 11.6 us -> 7.85 us  [step(): lax.all_to_all(rows.reshape(n_z, wide // (n_y * n_z), half), 'z', 0, 0)]
    all_to_all x1, waiting for transfers between devices: 0.01 us -> 3.31 us  [step(): lax.all_to_all(rows.reshape(n_z, wide // (n_y * n_z), half), 'z', 0, 0)]
    slice x2 -> x0, local copies, waits for them, and re-layouts: 3.05 us -> none  [the longest x1 2.24 us: shards(): from_right = shifted(dext[:, :width].astype(BF16), SPACE, -1).astype(F32)]
  transfers between devices with their start and end apart: 13 -> 23, of which waited for: 10 -> 10; matrix products, arithmetic and copies ran while one was open for 10% -> 1% of each run, Pallas kernels for 0% -> 15%
where the time goes in v2:
time: 111 us; the launch traced here: 110 us
  starting transfers between devices  59.2 us (53%)
  waiting for transfers between devices  24.5 us (22%)
  Pallas kernels  19 us (17%)
  local copies, waits for them, and re-layouts  5.18 us (5%)
  between operations  1.43 us (1%)
    ppermute x22, starting transfers between devices, permute(): return lax.ppermute(value, axes if len(axes) > 1 else axes[0], pairs)  51.4 us
    ppermute x22, waiting for transfers between devices, permute(): return lax.ppermute(value, axes if len(axes) > 1 else axes[0], pairs)  21.1 us
    pallas_call x13, Pallas kernels, call(): pl.pallas_call(kernel, out_shape=[jax.ShapeDtypeStruct(*s) if final else...  18.1 us
    all_to_all x1, starting transfers between devices, step(): lax.all_to_all(rows.reshape(n_z, wide // (n_y * n_z), half), 'z', 0, 0)  7.85 us
    unnamed x8, local copies, waits for them, and re-layouts  4.11 us
    all_to_all x1, waiting for transfers between devices, step(): lax.all_to_all(rows.reshape(n_z, wide // (n_y * n_z), half), 'z', 0, 0)  3.31 us
  transfers between devices with their start and end apart: 23, of which 10 were waited for; matrix products, arithmetic and copies ran while one was open for 1% of the time, Pallas kernels for 15%

profile of v2, /device:TPU:1, one launch (start us, length us, event | category | flops | bytes accessed | tf_op | source)
XLA Modules:
  0.0 110.3 jit_solution(6188542973477037409)
XLA Ops:
  0.6 1.1 slice_bitcast_fusion
  1.7 3.6 %collective-permute-start.2 = (bf16[128,1024]{1,0:T(8,128)(2,1)S(1)}, bf16[128,1024]{1,0:T(8,128)(2,1)S(1)}, u32[]{:S(2)}, u32[]{:S(2)}) collective-permute-start(bf16[128,1024]{1,0:T(8,128)(2,1)S(1)} %get-tuple-element.68.own_ref), channel_id=1, source_target_pairs={{0,1},{1,0},{2,3},{3,2},{4,5},{5,4},{6,7},{7,6},{8,9},{9,8},{10,11... | collective-permute-start | bytes 786440 | tf_op jit(solution)/shard_map/ppermute | solution.py:34
  5.4 4.9 %collective-permute-done.2.rec_ref = bf16[128,1024]{1,0:T(8,128)(2,1)S(1)} collective-permute-done((bf16[128,1024]{1,0:T(8,128)(2,1)S(1)}, bf16[128,1024]{1,0:T(8,128)(2,1)S(1)}, u32[]{:S(2)}, u32[]{:S(2)}) %collective-permute-start.2) | collective-permute-done | bytes 262176 | tf_op jit(solution)/shard_map/ppermute | solution.py:34
  10.3 2.6 %collective-permute-start.3 = (bf16[128,1024]{1,0:T(8,128)(2,1)S(1)}, bf16[128,1024]{1,0:T(8,128)(2,1)S(1)}, u32[]{:S(2)}, u32[]{:S(2)}) collective-permute-start(bf16[128,1024]{1,0:T(8,128)(2,1)S(1)} %collective-permute-done.2.rec_ref), channel_id=1, source_target_pairs={{0,2},{1,63},{2,4},{3,1},{4,6},{5,3},{6,8},{7,5},{8,10},{9,7},{10,... | collective-permute-start | bytes 786440 | tf_op jit(solution)/shard_map/ppermute | solution.py:34
  12.9 3.0 %collective-permute-done.rec_ref = bf16[128,1024]{1,0:T(8,128)(2,1)S(1)} collective-permute-done((bf16[128,1024]{1,0:T(8,128)(2,1)S(1)}, bf16[128,1024]{1,0:T(8,128)(2,1)S(1)}, u32[]{:S(2)}, u32[]{:S(2)}) %collective-permute-start) | collective-permute-done | bytes 262176 | tf_op jit(solution)/shard_map/ppermute | solution.py:34
  16.0 2.6 %collective-permute-start.1 = (bf16[128,1024]{1,0:T(8,128)(2,1)S(1)}, bf16[128,1024]{1,0:T(8,128)(2,1)S(1)}, u32[]{:S(2)}, u32[]{:S(2)}) collective-permute-start(bf16[128,1024]{1,0:T(8,128)(2,1)S(1)} %collective-permute-done.rec_ref), channel_id=1, source_target_pairs={{0,2},{1,63},{2,4},{3,1},{4,6},{5,3},{6,8},{7,5},{8,10},{9,7},{10,... | collective-permute-start | bytes 786440 | tf_op jit(solution)/shard_map/ppermute | solution.py:34
  18.6 1.6 %copy-done = bf16[1024,1024]{1,0:T(8,128)(2,1)S(1)} copy-done((bf16[1024,1024]{1,0:T(8,128)(2,1)S(1)}, bf16[1024,1024]{1,0:T(8,128)(2,1)}, u32[]{:S(2)}) %copy-start) | copy-done | bytes 2097176
  23.6 3.1 %shard_map.79 = (bf16[1024,512]{1,0:T(8,128)(2,1)S(1)}, bf16[512,1024]{1,0:T(8,128)(2,1)S(1)}, bf16[100,512]{1,0:T(8,128)(2,1)S(1)}) custom-call(bf16[512,384]{1,0:T(8,128)(2,1)S(1)} %get-tuple-element.36.counts_ref, bf16[128,1024]{1,0:T(8,128)(2,1)S(1)} %get-tuple-element.68.own_ref, bf16[128,1024]{1,0:T(8,128)(2,1)S(1)} %collective-permute-done.2.rec_ref, ...), custom_call_target="tpu_custom_call" | custom-call | tf_op jit(solution)/shard_map/pallas_call | solution.py:53
  26.7 3.1 %collective-permute-start.9 = (bf16[100,512]{1,0:T(8,128)(2,1)S(1)}, bf16[100,512]{1,0:T(8,128)(2,1)S(1)}, u32[]{:S(2)}, u32[]{:S(2)}) collective-permute-start(bf16[100,512]{1,0:T(8,128)(2,1)S(1)} %get-tuple-element.43.refs_1_), channel_id=1, source_target_pairs={{0,64},{64,0},{1,65},{65,1},{2,66},{66,2},{3,67},{67,3},{4,68},{68... | collective-permute-start | bytes 307208 | tf_op jit(solution)/shard_map/ppermute | solution.py:34
  29.8 1.2 %collective-permute-start.8 = (bf16[100,512]{1,0:T(8,128)(2,1)S(1)}, bf16[100,512]{1,0:T(8,128)(2,1)S(1)}, u32[]{:S(2)}, u32[]{:S(2)}) collective-permute-start(bf16[100,512]{1,0:T(8,128)(2,1)S(1)} %get-tuple-element.43.refs_1_), channel_id=1, source_target_pairs={{0,192},{64,128},{128,64},{192,0},{1,193},{65,129},{129,65},{193,1... | collective-permute-start | bytes 307208 | tf_op jit(solution)/shard_map/ppermute | solution.py:34
  31.3 3.1 %shard_map.78 = (bf16[1024,512]{1,0:T(8,128)(2,1)S(1)}, bf16[512,1024]{1,0:T(8,128)(2,1)S(1)}, bf16[100,512]{1,0:T(8,128)(2,1)S(1)}) custom-call(bf16[512,384]{1,0:T(8,128)(2,1)S(1)} %get-tuple-element.36.counts_ref, bf16[128,1024]{1,0:T(8,128)(2,1)S(1)} %get-tuple-element.69.own_ref, bf16[128,1024]{1,0:T(8,128)(2,1)S(1)} %collective-permute-done.rec_ref, ...), custom_call_target="tpu_custom_call" | custom-call | tf_op jit(solution)/shard_map/pallas_call | solution.py:53
  34.3 1.1 collective-permute-start.6
  35.4 1.2 %collective-permute-start.5 = (bf16[100,512]{1,0:T(8,128)(2,1)S(1)}, bf16[100,512]{1,0:T(8,128)(2,1)S(1)}, u32[]{:S(2)}, u32[]{:S(2)}) collective-permute-start(bf16[100,512]{1,0:T(8,128)(2,1)S(1)} %get-tuple-element.42.refs_0_), channel_id=1, source_target_pairs={{0,192},{64,128},{128,64},{192,0},{1,193},{65,129},{129,65},{193,1... | collective-permute-start | bytes 307208 | tf_op jit(solution)/shard_map/ppermute | solution.py:34
  37.5 3.1 %collective-permute-done.5.refs_3_ = bf16[100,512]{1,0:T(8,128)(2,1)S(1)} collective-permute-done((bf16[100,512]{1,0:T(8,128)(2,1)S(1)}, bf16[100,512]{1,0:T(8,128)(2,1)S(1)}, u32[]{:S(2)}, u32[]{:S(2)}) %collective-permute-start.5) | collective-permute-done | bytes 102432 | tf_op jit(solution)/shard_map/ppermute | solution.py:34
  40.7 1.4 %collective-permute-done.4.refs_2_ = bf16[100,512]{1,0:T(8,128)(2,1)S(1)} collective-permute-done((bf16[100,512]{1,0:T(8,128)(2,1)S(1)}, bf16[100,512]{1,0:T(8,128)(2,1)S(1)}, u32[]{:S(2)}, u32[]{:S(2)}) %collective-permute-start.4) | collective-permute-done | bytes 102432 | tf_op jit(solution)/shard_map/ppermute | solution.py:34
  42.1 2.3 %shard_map.80 = (bf16[100,512]{1,0:T(8,128)(2,1)S(1)}, bf16[100,512]{1,0:T(8,128)(2,1)S(1)}, bf16[512,512]{1,0:T(8,128)(2,1)S(1)}, bf16[512,512]{1,0:T(8,128)(2,1)S(1)}, bf16[1024,512]{1,0:T(8,128)(2,1)S(1)}) custom-call(s32[1]{0:T(128)S(6)} %copy.8.len_ref, bf16[100,512]{1,0:T(8,128)(2,1)S(1)} %get-tuple-element.42.refs_0_, ...), custom_call_target="tpu_custom_call" | custom-call | tf_op jit(solution)/shard_map/pallas_call | solution.py:53
  45.4 1.6 %shard_map.81 = (bf16[512,512]{1,0:T(8,128)(2,1)S(1)}, bf16[512,512]{1,0:T(8,128)(2,1)S(1)}, bf16[1024,512]{1,0:T(8,128)(2,1)S(1)}) custom-call(bf16[100,1024]{1,0:T(8,128)(2,1)S(1)} %get-tuple-element.35.wo_ref.refs_9_, bf16[1024,512]{1,0:T(8,128)(2,1)S(1)} %get-tuple-element.38.refs_10_.t0, bf16[1024,512]{1,0:T(8,128)(2,1)S(1)} %get-tuple-element.39.refs_11_.t1, ...), custom_call_target="tpu_custom_call" | custom-call | tf_op jit(solution)/shard_map/pallas_call | solution.py:53
  47.0 3.1 %shard_map.89 = (f32[128,1024]{1,0:T(8,128)S(1)}, f32[128,1024]{1,0:T(8,128)S(1)}, bf16[128,1024]{1,0:T(8,128)(2,1)S(1)}) custom-call(bf16[384,512]{1,0:T(8,128)(2,1)S(1)} %get-tuple-element.53.flipped_ref, bf16[1024,1024]{1,0:T(8,128)(2,1)S(1)} %get-tuple-element.37.w_ref, bf16[512,512]{1,0:T(8,128)(2,1)S(1)} %get-tuple-element.63.give_ref, ...), custom_call_target="tpu_custom_call" | custom-call | tf_op jit(solution)/shard_map/pallas_call | solution.py:53
  50.1 4.7 %collective-permute-start.20 = (bf16[128,1024]{1,0:T(8,128)(2,1)S(1)}, bf16[128,1024]{1,0:T(8,128)(2,1)S(1)}, u32[]{:S(2)}, u32[]{:S(2)}) collective-permute-start(bf16[128,1024]{1,0:T(8,128)(2,1)S(1)} %get-tuple-element.67), channel_id=1, source_target_pairs={{0,62},{1,3},{2,0},{3,5},{4,2},{5,7},{6,4},{7,9},{8,6},{9,11},{10,... | collective-permute-start | bytes 786440 | tf_op jit(solution)/shard_map/ppermute | solution.py:34
  54.8 3.1 %shard_map.84 = (f32[128,1024]{1,0:T(8,128)S(1)}, f32[128,1024]{1,0:T(8,128)S(1)}, bf16[128,1024]{1,0:T(8,128)(2,1)S(1)}) custom-call(bf16[384,512]{1,0:T(8,128)(2,1)S(1)} %get-tuple-element.53.flipped_ref, bf16[1024,1024]{1,0:T(8,128)(2,1)S(1)} %get-tuple-element.37.w_ref, bf16[512,512]{1,0:T(8,128)(2,1)S(1)} %get-tuple-element.54.give_ref, ...), custom_call_target="tpu_custom_call" | custom-call | tf_op jit(solution)/shard_map/pallas_call | solution.py:53
  57.9 1.8 %collective-permute-start.14 = (bf16[128,1024]{1,0:T(8,128)(2,1)S(1)}, bf16[128,1024]{1,0:T(8,128)(2,1)S(1)}, u32[]{:S(2)}, u32[]{:S(2)}) collective-permute-start(bf16[128,1024]{1,0:T(8,128)(2,1)S(1)} %get-tuple-element.57), channel_id=1, source_target_pairs={{0,62},{1,3},{2,0},{3,5},{4,2},{5,7},{6,4},{7,9},{8,6},{9,11},{10,... | collective-permute-start | bytes 786440 | tf_op jit(solution)/shard_map/ppermute | solution.py:34
  60.1 1.6 %collective-permute-start.12 = (bf16[256,512]{1,0:T(8,128)(2,1)S(1)}, bf16[256,512]{1,0:T(8,128)(2,1)S(1)}, u32[]{:S(2)}, u32[]{:S(2)}) collective-permute-start(bf16[256,512]{1,0:T(8,128)(2,1)S(1)} %get-tuple-element.51), channel_id=1, source_target_pairs={{0,32},{16,48},{32,0},{48,16},{1,33},{17,49},{33,1},{49,17},{2,34}... | collective-permute-start | bytes 786440 | tf_op jit(solution)/shard_map/ppermute | solution.py:34
  62.8 6.4 %collective-permute-start.21 = (bf16[128,1024]{1,0:T(8,128)(2,1)S(1)}, bf16[128,1024]{1,0:T(8,128)(2,1)S(1)}, u32[]{:S(2)}, u32[]{:S(2)}) collective-permute-start(bf16[128,1024]{1,0:T(8,128)(2,1)S(1)} %shard_map.90), channel_id=1, source_target_pairs={{0,1},{1,0},{2,3},{3,2},{4,5},{5,4},{6,7},{7,6},{8,9},{9,8},{10,11... | collective-permute-start | bytes 786440 | tf_op jit(solution)/shard_map/ppermute | solution.py:34
  69.6 3.6 %collective-permute-done.12.refs_1_ = bf16[256,512]{1,0:T(8,128)(2,1)S(1)} collective-permute-done((bf16[256,512]{1,0:T(8,128)(2,1)S(1)}, bf16[256,512]{1,0:T(8,128)(2,1)S(1)}, u32[]{:S(2)}, u32[]{:S(2)}) %collective-permute-start.12) | collective-permute-done | bytes 262176 | tf_op jit(solution)/shard_map/ppermute | solution.py:34
  73.2 1.4 %collective-permute-done.13.refs_2_ = bf16[256,512]{1,0:T(8,128)(2,1)S(1)} collective-permute-done((bf16[256,512]{1,0:T(8,128)(2,1)S(1)}, bf16[256,512]{1,0:T(8,128)(2,1)S(1)}, u32[]{:S(2)}, u32[]{:S(2)}) %collective-permute-start.13) | collective-permute-done | bytes 262176 | tf_op jit(solution)/shard_map/ppermute | solution.py:34
  75.4 7.8 %all-to-all-start = ((bf16[8,32,512]{2,1,0:T(8,128)(2,1)}), bf16[8,32,512]{2,1,0:T(8,128)(2,1)S(1)}, u32[]{:S(2)}, u32[]{:S(2)}) async-start(bf16[8,32,512]{2,1,0:T(8,128)(2,1)} %bitcast.2), calls=%async_computation | async-start | bytes 524288 | tf_op jit(solution)/shard_map/all_to_all | solution.py:272
  83.2 7.4 %collective-permute-start.19 = (bf16[128,1024]{1,0:T(8,128)(2,1)S(1)}, bf16[128,1024]{1,0:T(8,128)(2,1)S(1)}, u32[]{:S(2)}, u32[]{:S(2)}) collective-permute-start(bf16[128,1024]{1,0:T(8,128)(2,1)S(1)} %shard_map.85), channel_id=1, source_target_pairs={{0,1},{1,0},{2,3},{3,2},{4,5},{5,4},{6,7},{7,6},{8,9},{9,8},{10,11... | collective-permute-start | bytes 786440 | tf_op jit(solution)/shard_map/ppermute | solution.py:34
  90.7 3.3 %all-to-all-done.parts_ref = bf16[8,32,512]{2,1,0:T(8,128)(2,1)S(1)} async-done(((bf16[8,32,512]{2,1,0:T(8,128)(2,1)}), bf16[8,32,512]{2,1,0:T(8,128)(2,1)S(1)}, u32[]{:S(2)}, u32[]{:S(2)}) %all-to-all-start) | async-done | bytes 262176 | tf_op jit(solution)/shard_map/all_to_all | solution.py:272
  94.0 8.5 %collective-permute-start.17 = (bf16[16,512]{1,0:T(8,128)(2,1)S(1)}, bf16[16,512]{1,0:T(8,128)(2,1)S(1)}, u32[]{:S(2)}, u32[]{:S(2)}) collective-permute-start(bf16[16,512]{1,0:T(8,128)(2,1)S(1)} %get-tuple-element.60), channel_id=1, source_target_pairs={{0,129},{1,128},{128,1},{129,0},{2,131},{3,130},{130,3},{131,2},{4... | collective-permute-start | bytes 49160 | tf_op jit(solution)/shard_map/ppermute | solution.py:34
  103.3 2.3 %collective-permute-done.15.refs_0_ = bf16[16,512]{1,0:T(8,128)(2,1)S(1)} collective-permute-done((bf16[16,512]{1,0:T(8,128)(2,1)S(1)}, bf16[16,512]{1,0:T(8,128)(2,1)S(1)}, u32[]{:S(2)}, u32[]{:S(2)}) %collective-permute-start.15) | collective-permute-done | bytes 16416 | tf_op jit(solution)/shard_map/ppermute | solution.py:34
  105.6 1.1 collective-permute-done.16.refs_1_
  106.7 2.1 %collective-permute-start.18 = (bf16[16,512]{1,0:T(8,128)(2,1)S(1)}, bf16[16,512]{1,0:T(8,128)(2,1)S(1)}, u32[]{:S(2)}, u32[]{:S(2)}) collective-permute-start(bf16[16,512]{1,0:T(8,128)(2,1)S(1)} %shard_map.87.mine_ref), channel_id=1, source_target_pairs={{0,64},{64,0},{1,65},{65,1},{2,66},{66,2},{3,67},{67,3},{4,68},{68... | collective-permute-start | bytes 49160 | tf_op jit(solution)/shard_map/ppermute | solution.py:34
  (40 shorter events, 10.0 us)
Async XLA Ops:
  1.7 8.6 %collective-permute-start.2 = (bf16[128,1024]{1,0:T(8,128)(2,1)S(1)}, bf16[128,1024]{1,0:T(8,128)(2,1)S(1)}, u32[]{:S(2)}, u32[]{:S(2)}) collective-permute-start(bf16[128,1024]{1,0:T(8,128)(2,1)S(1)} %get-tuple-element.68.own_ref), channel_id=1, source_target_pairs={{0,1},{1,0},{2,3},{3,2},{4,5},{5,4},{6,7},{7,6},{8,9},{9,8},{10,11... | collective-permute-start | bytes 786440 | tf_op jit(solution)/shard_map/ppermute | solution.py:34
  5.3 10.6 %collective-permute-start = (bf16[128,1024]{1,0:T(8,128)(2,1)S(1)}, bf16[128,1024]{1,0:T(8,128)(2,1)S(1)}, u32[]{:S(2)}, u32[]{:S(2)}) collective-permute-start(bf16[128,1024]{1,0:T(8,128)(2,1)S(1)} %get-tuple-element.69.own_ref), channel_id=1, source_target_pairs={{0,1},{1,0},{2,3},{3,2},{4,5},{5,4},{6,7},{7,6},{8,9},{9,8},{10,11... | collective-permute-start | bytes 786440 | tf_op jit(solution)/shard_map/ppermute | solution.py:34
  10.3 13.2 %collective-permute-start.3 = (bf16[128,1024]{1,0:T(8,128)(2,1)S(1)}, bf16[128,1024]{1,0:T(8,128)(2,1)S(1)}, u32[]{:S(2)}, u32[]{:S(2)}) collective-permute-start(bf16[128,1024]{1,0:T(8,128)(2,1)S(1)} %collective-permute-done.2.rec_ref), channel_id=1, source_target_pairs={{0,2},{1,63},{2,4},{3,1},{4,6},{5,3},{6,8},{7,5},{8,10},{9,7},{10,... | collective-permute-start | bytes 786440 | tf_op jit(solution)/shard_map/ppermute | solution.py:34
  16.0 15.3 %collective-permute-start.1 = (bf16[128,1024]{1,0:T(8,128)(2,1)S(1)}, bf16[128,1024]{1,0:T(8,128)(2,1)S(1)}, u32[]{:S(2)}, u32[]{:S(2)}) collective-permute-start(bf16[128,1024]{1,0:T(8,128)(2,1)S(1)} %collective-permute-done.rec_ref), channel_id=1, source_target_pairs={{0,2},{1,63},{2,4},{3,1},{4,6},{5,3},{6,8},{7,5},{8,10},{9,7},{10,... | collective-permute-start | bytes 786440 | tf_op jit(solution)/shard_map/ppermute | solution.py:34
  18.6 1.6 %copy-start = (bf16[1024,1024]{1,0:T(8,128)(2,1)S(1)}, bf16[1024,1024]{1,0:T(8,128)(2,1)}, u32[]{:S(2)}) copy-start(bf16[1024,1024]{1,0:T(8,128)(2,1)} %refs_0_.1) | copy-start | bytes 6291460
  20.1 0.9 copy-start.1
  21.1 0.9 copy-start.2
  22.0 0.7 copy-start.3
  26.7 9.9 %collective-permute-start.9 = (bf16[100,512]{1,0:T(8,128)(2,1)S(1)}, bf16[100,512]{1,0:T(8,128)(2,1)S(1)}, u32[]{:S(2)}, u32[]{:S(2)}) collective-permute-start(bf16[100,512]{1,0:T(8,128)(2,1)S(1)} %get-tuple-element.43.refs_1_), channel_id=1, source_target_pairs={{0,64},{64,0},{1,65},{65,1},{2,66},{66,2},{3,67},{67,3},{4,68},{68... | collective-permute-start | bytes 307208 | tf_op jit(solution)/shard_map/ppermute | solution.py:34
  29.8 7.7 %collective-permute-start.8 = (bf16[100,512]{1,0:T(8,128)(2,1)S(1)}, bf16[100,512]{1,0:T(8,128)(2,1)S(1)}, u32[]{:S(2)}, u32[]{:S(2)}) collective-permute-start(bf16[100,512]{1,0:T(8,128)(2,1)S(1)} %get-tuple-element.43.refs_1_), channel_id=1, source_target_pairs={{0,192},{64,128},{128,64},{192,0},{1,193},{65,129},{129,65},{193,1... | collective-permute-start | bytes 307208 | tf_op jit(solution)/shard_map/ppermute | solution.py:34
  31.0 6.5 %collective-permute-start.7 = (bf16[100,512]{1,0:T(8,128)(2,1)S(1)}, bf16[100,512]{1,0:T(8,128)(2,1)S(1)}, u32[]{:S(2)}, u32[]{:S(2)}) collective-permute-start(bf16[100,512]{1,0:T(8,128)(2,1)S(1)} %get-tuple-element.43.refs_1_), channel_id=1, source_target_pairs={{0,128},{128,0},{1,129},{129,1},{2,130},{130,2},{3,131},{131,3},{4... | collective-permute-start | bytes 307208 | tf_op jit(solution)/shard_map/ppermute | solution.py:34
  34.3 3.2 %collective-permute-start.6 = (bf16[100,512]{1,0:T(8,128)(2,1)S(1)}, bf16[100,512]{1,0:T(8,128)(2,1)S(1)}, u32[]{:S(2)}, u32[]{:S(2)}) collective-permute-start(bf16[100,512]{1,0:T(8,128)(2,1)S(1)} %get-tuple-element.42.refs_0_), channel_id=1, source_target_pairs={{0,64},{64,0},{1,65},{65,1},{2,66},{66,2},{3,67},{67,3},{4,68},{68... | collective-permute-start | bytes 307208 | tf_op jit(solution)/shard_map/ppermute | solution.py:34
  35.4 5.3 %collective-permute-start.5 = (bf16[100,512]{1,0:T(8,128)(2,1)S(1)}, bf16[100,512]{1,0:T(8,128)(2,1)S(1)}, u32[]{:S(2)}, u32[]{:S(2)}) collective-permute-start(bf16[100,512]{1,0:T(8,128)(2,1)S(1)} %get-tuple-element.42.refs_0_), channel_id=1, source_target_pairs={{0,192},{64,128},{128,64},{192,0},{1,193},{65,129},{129,65},{193,1... | collective-permute-start | bytes 307208 | tf_op jit(solution)/shard_map/ppermute | solution.py:34
  36.6 5.5 %collective-permute-start.4 = (bf16[100,512]{1,0:T(8,128)(2,1)S(1)}, bf16[100,512]{1,0:T(8,128)(2,1)S(1)}, u32[]{:S(2)}, u32[]{:S(2)}) collective-permute-start(bf16[100,512]{1,0:T(8,128)(2,1)S(1)} %get-tuple-element.42.refs_0_), channel_id=1, source_target_pairs={{0,128},{128,0},{1,129},{129,1},{2,130},{130,2},{3,131},{131,3},{4... | collective-permute-start | bytes 307208 | tf_op jit(solution)/shard_map/ppermute | solution.py:34
  44.4 15.4 %collective-permute-start.10 = (bf16[1024,512]{1,0:T(8,128)(2,1)S(1)}, bf16[1024,512]{1,0:T(8,128)(2,1)S(1)}, u32[]{:S(2)}, u32[]{:S(2)}) collective-permute-start(bf16[1024,512]{1,0:T(8,128)(2,1)S(1)} %get-tuple-element.48), channel_id=1, source_target_pairs={{0,64},{64,0},{1,65},{65,1},{2,66},{66,2},{3,67},{67,3},{4,68},{68... | collective-permute-start | bytes 3145736 | tf_op jit(solution)/shard_map/ppermute | solution.py:34
  50.1 12.6 %collective-permute-start.20 = (bf16[128,1024]{1,0:T(8,128)(2,1)S(1)}, bf16[128,1024]{1,0:T(8,128)(2,1)S(1)}, u32[]{:S(2)}, u32[]{:S(2)}) collective-permute-start(bf16[128,1024]{1,0:T(8,128)(2,1)S(1)} %get-tuple-element.67), channel_id=1, source_target_pairs={{0,62},{1,3},{2,0},{3,5},{4,2},{5,7},{6,4},{7,9},{8,6},{9,11},{10,... | collective-permute-start | bytes 786440 | tf_op jit(solution)/shard_map/ppermute | solution.py:34
  57.9 11.3 %collective-permute-start.14 = (bf16[128,1024]{1,0:T(8,128)(2,1)S(1)}, bf16[128,1024]{1,0:T(8,128)(2,1)S(1)}, u32[]{:S(2)}, u32[]{:S(2)}) collective-permute-start(bf16[128,1024]{1,0:T(8,128)(2,1)S(1)} %get-tuple-element.57), channel_id=1, source_target_pairs={{0,62},{1,3},{2,0},{3,5},{4,2},{5,7},{6,4},{7,9},{8,6},{9,11},{10,... | collective-permute-start | bytes 786440 | tf_op jit(solution)/shard_map/ppermute | solution.py:34
  60.0 9.6 %collective-permute-start.11 = (bf16[256,512]{1,0:T(8,128)(2,1)S(1)}, bf16[256,512]{1,0:T(8,128)(2,1)S(1)}, u32[]{:S(2)}, u32[]{:S(2)}) collective-permute-start(bf16[256,512]{1,0:T(8,128)(2,1)S(1)} %get-tuple-element.50), channel_id=1, source_target_pairs={{0,16},{16,32},{32,48},{48,0},{1,17},{17,33},{33,49},{49,1},{2,18}... | collective-permute-start | bytes 786440 | tf_op jit(solution)/shard_map/ppermute | solution.py:34
  60.1 13.1 %collective-permute-start.12 = (bf16[256,512]{1,0:T(8,128)(2,1)S(1)}, bf16[256,512]{1,0:T(8,128)(2,1)S(1)}, u32[]{:S(2)}, u32[]{:S(2)}) collective-permute-start(bf16[256,512]{1,0:T(8,128)(2,1)S(1)} %get-tuple-element.51), channel_id=1, source_target_pairs={{0,32},{16,48},{32,0},{48,16},{1,33},{17,49},{33,1},{49,17},{2,34}... | collective-permute-start | bytes 786440 | tf_op jit(solution)/shard_map/ppermute | solution.py:34
  61.7 12.9 %collective-permute-start.13 = (bf16[256,512]{1,0:T(8,128)(2,1)S(1)}, bf16[256,512]{1,0:T(8,128)(2,1)S(1)}, u32[]{:S(2)}, u32[]{:S(2)}) collective-permute-start(bf16[256,512]{1,0:T(8,128)(2,1)S(1)} %get-tuple-element.52), channel_id=1, source_target_pairs={{0,48},{16,0},{32,16},{48,32},{1,49},{17,1},{33,17},{49,33},{2,50}... | collective-permute-start | bytes 786440 | tf_op jit(solution)/shard_map/ppermute | solution.py:34
  62.8 27.8 %collective-permute-start.21 = (bf16[128,1024]{1,0:T(8,128)(2,1)S(1)}, bf16[128,1024]{1,0:T(8,128)(2,1)S(1)}, u32[]{:S(2)}, u32[]{:S(2)}) collective-permute-start(bf16[128,1024]{1,0:T(8,128)(2,1)S(1)} %shard_map.90), channel_id=1, source_target_pairs={{0,1},{1,0},{2,3},{3,2},{4,5},{5,4},{6,7},{7,6},{8,9},{9,8},{10,11... | collective-permute-start | bytes 786440 | tf_op jit(solution)/shard_map/ppermute | solution.py:34
  75.4 18.6 %all-to-all-start = ((bf16[8,32,512]{2,1,0:T(8,128)(2,1)}), bf16[8,32,512]{2,1,0:T(8,128)(2,1)S(1)}, u32[]{:S(2)}, u32[]{:S(2)}) async-start(bf16[8,32,512]{2,1,0:T(8,128)(2,1)} %bitcast.2), calls=%async_computation | async-start | bytes 524288 | tf_op jit(solution)/shard_map/all_to_all | solution.py:272
  83.2 20.0 %collective-permute-start.19 = (bf16[128,1024]{1,0:T(8,128)(2,1)S(1)}, bf16[128,1024]{1,0:T(8,128)(2,1)S(1)}, u32[]{:S(2)}, u32[]{:S(2)}) collective-permute-start(bf16[128,1024]{1,0:T(8,128)(2,1)S(1)} %shard_map.85), channel_id=1, source_target_pairs={{0,1},{1,0},{2,3},{3,2},{4,5},{5,4},{6,7},{7,6},{8,9},{9,8},{10,11... | collective-permute-start | bytes 786440 | tf_op jit(solution)/shard_map/ppermute | solution.py:34
  94.0 11.6 %collective-permute-start.17 = (bf16[16,512]{1,0:T(8,128)(2,1)S(1)}, bf16[16,512]{1,0:T(8,128)(2,1)S(1)}, u32[]{:S(2)}, u32[]{:S(2)}) collective-permute-start(bf16[16,512]{1,0:T(8,128)(2,1)S(1)} %get-tuple-element.60), channel_id=1, source_target_pairs={{0,129},{1,128},{128,1},{129,0},{2,131},{3,130},{130,3},{131,2},{4... | collective-permute-start | bytes 49160 | tf_op jit(solution)/shard_map/ppermute | solution.py:34
  102.6 4.1 %collective-permute-start.16 = (bf16[16,512]{1,0:T(8,128)(2,1)S(1)}, bf16[16,512]{1,0:T(8,128)(2,1)S(1)}, u32[]{:S(2)}, u32[]{:S(2)}) collective-permute-start(bf16[16,512]{1,0:T(8,128)(2,1)S(1)} %get-tuple-element.60), channel_id=1, source_target_pairs={{0,1},{1,0},{2,3},{3,2},{4,5},{5,4},{6,7},{7,6},{8,9},{9,8},{10,11... | collective-permute-start | bytes 49160 | tf_op jit(solution)/shard_map/ppermute | solution.py:34
  102.9 2.6 %collective-permute-start.15 = (bf16[16,512]{1,0:T(8,128)(2,1)S(1)}, bf16[16,512]{1,0:T(8,128)(2,1)S(1)}, u32[]{:S(2)}, u32[]{:S(2)}) collective-permute-start(bf16[16,512]{1,0:T(8,128)(2,1)S(1)} %get-tuple-element.59.first_ref), channel_id=1, source_target_pairs={{0,128},{128,0},{1,129},{129,1},{2,130},{130,2},{3,131},{131,3},{4... | collective-permute-start | bytes 49160 | tf_op jit(solution)/shard_map/ppermute | solution.py:34
  106.7 2.9 %collective-permute-start.18 = (bf16[16,512]{1,0:T(8,128)(2,1)S(1)}, bf16[16,512]{1,0:T(8,128)(2,1)S(1)}, u32[]{:S(2)}, u32[]{:S(2)}) collective-permute-start(bf16[16,512]{1,0:T(8,128)(2,1)S(1)} %shard_map.87.mine_ref), channel_id=1, source_target_pairs={{0,64},{64,0},{1,65},{65,1},{2,66},{66,2},{3,67},{67,3},{4,68},{68... | collective-permute-start | bytes 49160 | tf_op jit(solution)/shard_map/ppermute | solution.py:34

commit v3 on v2

--- a/solution.py
+++ b/solution.py
@@ -130,7 +130,7 @@
         slope[...] = value
         more = dot(area[...], value)
         part = more if part is None else part + more
-    out[...] = part.astype(out.dtype)
+    out[...] = part.astype(out.dtype).reshape(out.shape)
 
 
 def give_kernel(total, len_ref, *refs):
@@ -150,24 +150,38 @@
         for ref, v, p in zip((dp0, dp1), own, pairs):
             value = smooth_sign(v - truth) * (1.0 / total) - scale * p
             ref[rows] = jnp.where(at < len_ref[0], value, 0.0).astype(BF16)
-    half = out.shape[1]
+    half = out.shape[-1]
     start = (1 - lax.axis_index("c")) * half
     half_slopes(start, half, wo_ref, (gate0, gate1), (dp0, dp1), (s0, s1), (t0, t1), out)
 
 
 def keep_kernel(wo_ref, t0, t1, gate0, gate1, dp0, dp1, s0, s1, out):
-    half = out.shape[1]
+    half = out.shape[-1]
     start = lax.axis_index("c") * half
     half_slopes(start, half, wo_ref, (gate0, gate1), (dp0, dp1), (s0, s1), (t0, t1), out)
 
 
 def cores_kernel(keep_ref, got_ref, own_ref, *outs):
+    wide = own_ref.shape[-1]
+    for out, (a, b) in zip((own_ref,) + outs, ((0, 0), (0, 1), (1, 0), (1, 1))):
+        xh = lax.rem(lax.axis_index("xh") + a, 2)
+        xl = lax.rem(lax.axis_index("xl") + b, 2)
+        cols = pl.ds(pl.multiple_of(xl * wide, wide), wide)
+        out[...] = (
+            keep_ref[:, xh, :, cols].astype(F32) + got_ref[:, xh, :, cols].astype(F32)
+        ).astype(out.dtype)
+
+
+def cut_kernel(first_ref, second_ref, third_ref, fourth_ref, own_ref, *outs):
     size = own_ref.shape[0]
     n_y = len(outs) + 1
     for s, out in enumerate((own_ref,) + outs):
         to = lax.rem(lax.axis_index("y") + s, n_y)
-        rows = pl.ds(pl.multiple_of(to * size, size), size)
-        out[...] = (keep_ref[rows, :].astype(F32) + got_ref[rows, :].astype(F32)).astype(out.dtype)
+        at = pl.ds(to * size, size)
+        total = first_ref[at]
+        for ref in (second_ref, third_ref, fourth_ref):
+            total = total + ref[at].astype(F32)
+        out[...] = total.astype(out.dtype)
 
 
 def total_kernel(first_ref, *refs):
@@ -177,23 +191,25 @@
     refs[-1][...] = total.astype(refs[-1].dtype)
 
 
-def columns_kernel(parts_ref, mine_ref, theirs_ref):
-    size = mine_ref.shape[0]
-    xh = lax.axis_index("xh")
+def sum_kernel(parts_ref, out_ref):
     total = parts_ref[0].astype(F32)
     for k in range(1, parts_ref.shape[0]):
         total = total + parts_ref[k].astype(F32)
-    first, second = total[:size], total[size:]
-    mine_ref[...] = jnp.where(xh == 0, first, second).astype(BF16)
-    theirs_ref[...] = jnp.where(xh == 0, second, first).astype(BF16)
-
-
-def place_kernel(mine_ref, other_ref, out_ref):
-    half = mine_ref.shape[1]
-    first = lax.axis_index("c") == 0
-    mine, other = mine_ref[...].astype(F32), other_ref[...].astype(F32)
-    out_ref[:, :half] = jnp.where(first, mine, other)
-    out_ref[:, half:] = jnp.where(first, other, mine)
+    out_ref[...] = total.astype(out_ref.dtype)
+
+
+def place_kernel(mine_ref, x_ref, c_ref, both_ref, out_ref):
+    wide = mine_ref.shape[1]
+    c, xl = lax.axis_index("c"), lax.axis_index("xl")
+    for k, ref in enumerate((mine_ref, x_ref, c_ref, both_ref)):
+        at = lax.rem(c + k // 2, 2) * 2 + lax.rem(xl + k, 2)
+        cols = pl.ds(pl.multiple_of(at * wide, wide), wide)
+        out_ref[:, cols] = ref[...].astype(F32)
+
+
+def nodes_kernel(own0_ref, own1_ref, far0_ref, far1_ref, out_ref):
+    out_ref[0] = (own0_ref[...] + far0_ref[...].astype(F32)).astype(BF16)
+    out_ref[1] = (own1_ref[...] + far1_ref[...].astype(F32)).astype(BF16)
 
 
 def backward_kernel(flipped_ref, w_ref, give_ref, keep_ref, own_ref, rec_ref, fwd_ref):
@@ -243,7 +259,8 @@
         ]
 
     slope = ((grid_rows, half), BF16)
-    part = ((wide, half), BF16)
+    out_rows = wide // (n_y * n_z * n_x)
+    part = ((n_y * n_z, n_x, out_rows, half), BF16)
     dp = ((channels, grid_rows), BF16)
     dp0, dp1, g0, g1, give = call(
         functools.partial(give_kernel, total), [dp, dp, slope, slope, part],
@@ -251,11 +268,17 @@
     )
     got = shifted(give, "c", 1)
     k0, k1, keep = call(keep_kernel, [slope, slope, part], w_out, *area, *gate, dp0, dp1)
-    rows_y = (wide // n_y, half)
-    mine, *give = call(cores_kernel, [(rows_y, F32)] + [(rows_y, BF16)] * (n_y - 1), keep, got)
+    part = ((n_y * n_z, out_rows, half // 2), BF16)
+    mine, *give = call(cores_kernel, [(part[0], F32)] + [part] * 3, keep, got)
     got = []
-    for s, g in enumerate(give):
-        got.append(shifted(g, "y", s + 1))
+    for axes, g in zip((("xl",), ("xh",), ("xl", "xh")), give):
+        got.append(permute(g, axes, lambda *at: tuple(1 - i for i in at)))
+    part = ((n_z, out_rows, half // 2), BF16)
+    mine, *give = call(cut_kernel, [(part[0], F32)] + [part] * (n_y - 1), mine, *got)
+    got = []
+    for s in (2, 1, 3):
+        got.append(shifted(give[s - 1], "y", s))
+    (rows,) = call(total_kernel, [part], mine, *got)
 
     node = ((width, wide), F32)
     back = []
@@ -263,22 +286,23 @@
         back.append(
             call(backward_kernel, [node, node, ((width, wide), BF16)], flipped, w_hidden, g, k)
         )
-    far = [relayed(b[2], -1) for b in back]
-    far = [call(total_kernel, [((width, wide), BF16)], b[1], f)[0] for b, f in zip(back, far)]
-
-    (rows,) = call(total_kernel, [(rows_y, BF16)], mine, *got)
-    rows, far[0] = lax.optimization_barrier((rows, far[0]))
-    far = [shifted(f, "xh", 1) for f in far]
-    rows = lax.all_to_all(rows.reshape(n_z, wide // (n_y * n_z), half), "z", 0, 0)
-    out_rows = (wide // (n_y * n_z * n_x), half)
-    mine, theirs = call(columns_kernel, [(out_rows, BF16)] * 2, rows)
-    (mine,) = call(
-        total_kernel, [(out_rows, BF16)],
-        mine, shifted(mine, "xl", 1), shifted(theirs, "xh", 1),
-        permute(theirs, ("xl", "xh"), lambda a, b: (1 - a, 1 - b)),
+    far = []
+    for b in back:
+        moved = relayed(b[2], -1)
+        far.append(call(total_kernel, [((width, wide), BF16)], b[1], moved)[0])
+
+    for m in range(members):
+        far[m] = shifted(far[m], "xh", 1)
+    rows = lax.all_to_all(rows, "z", 0, 0)
+    (mine,) = call(sum_kernel, [((out_rows, half // 2), BF16)], rows)
+    (grad_hidden,) = call(
+        place_kernel, [((out_rows, wide), F32)],
+        mine, shifted(mine, "xl", 1), shifted(mine, "c", 1),
+        permute(mine, MEMBER, lambda a, b: (1 - a, 1 - b)), final=True,
     )
-    (grad_hidden,) = call(place_kernel, [((out_rows[0], wide), F32)], mine, shifted(mine, "c", 1), final=True)
-    grad_mesh = jnp.stack([(b[0] + f.astype(F32)).astype(BF16) for b, f in zip(back, far)])
+    (grad_mesh,) = call(
+        nodes_kernel, [((members, width, wide), BF16)], *[b[0] for b in back], *far, final=True
+    )
     return (grad_hidden, grad_mesh)
 
 

time: 111 us -> 115 us (1.036)
  blocking collectives: 0 us -> 12.7 us
  starting transfers between devices: 59.2 us -> 47.5 us
  waiting for transfers between devices: 24.5 us -> 28.2 us
    all_to_all x0 -> x1, blocking collectives: none -> 12.7 us  [step(): rows = lax.all_to_all(rows, 'z', 0, 0)]
    all_to_all x1 -> x0, starting transfers between devices: 7.85 us -> none  [step(): lax.all_to_all(rows.reshape(n_z, wide // (n_y * n_z), half), 'z', 0, 0)]
    ppermute x22 -> x24, waiting for transfers between devices: 21.1 us -> 28.2 us  [permute(): return lax.ppermute(value, axes if len(axes) > 1 else axes[0], pairs)]
    ppermute x22 -> x24, starting transfers between devices: 51.4 us -> 47.5 us  [permute(): return lax.ppermute(value, axes if len(axes) > 1 else axes[0], pairs)]
    all_to_all x1 -> x0, waiting for transfers between devices: 3.31 us -> none  [step(): lax.all_to_all(rows.reshape(n_z, wide // (n_y * n_z), half), 'z', 0, 0)]
    pallas_call x13 -> x14, Pallas kernels: 18.1 us -> 18.3 us  [call(): pl.pallas_call(kernel, out_shape=[jax.ShapeDtypeStruct(*s) if final else...]
  transfers between devices with their start and end apart: 23 -> 24, of which waited for: 10 -> 8; matrix products, arithmetic and copies ran while one was open for 1% -> 0% of each run, Pallas kernels for 15% -> 14%
where the time goes in v3:
time: 115 us; the launch traced here: 114 us
  starting transfers between devices  47.5 us (41%)
  waiting for transfers between devices  28.2 us (25%)
  Pallas kernels  19.2 us (17%)
  blocking collectives  12.7 us (11%)
  local copies, waits for them, and re-layouts  5.18 us (5%)
  between operations  1.41 us (1%)
    ppermute x24, starting transfers between devices, permute(): return lax.ppermute(value, axes if len(axes) > 1 else axes[0], pairs)  47.5 us
    ppermute x24, waiting for transfers between devices, permute(): return lax.ppermute(value, axes if len(axes) > 1 else axes[0], pairs)  28.2 us
    pallas_call x14, Pallas kernels, call(): pl.pallas_call(kernel, out_shape=[jax.ShapeDtypeStruct(*s) if final else...  18.3 us
    all_to_all x1, blocking collectives, step(): rows = lax.all_to_all(rows, 'z', 0, 0)  12.7 us
    unnamed x8, local copies, waits for them, and re-layouts  4.11 us
  transfers between devices with their start and end apart: 24, of which 8 were waited for; matrix products, arithmetic and copies ran while one was open for 0% of the time, Pallas kernels for 14%

profile of v3, /device:TPU:1, one launch (start us, length us, event | category | flops | bytes accessed | tf_op | source)
XLA Modules:
  0.0 114.1 jit_solution(4631710206880985110)
XLA Ops:
  0.6 1.1 slice_bitcast_fusion
  1.7 3.6 %collective-permute-start.2 = (bf16[128,1024]{1,0:T(8,128)(2,1)S(1)}, bf16[128,1024]{1,0:T(8,128)(2,1)S(1)}, u32[]{:S(2)}, u32[]{:S(2)}) collective-permute-start(bf16[128,1024]{1,0:T(8,128)(2,1)S(1)} %get-tuple-element.68.own_ref), channel_id=1, source_target_pairs={{0,1},{1,0},{2,3},{3,2},{4,5},{5,4},{6,7},{7,6},{8,9},{9,8},{10,11... | collective-permute-start | bytes 786440 | tf_op jit(solution)/shard_map/ppermute | solution.py:34
  5.4 4.9 %collective-permute-done.2.rec_ref = bf16[128,1024]{1,0:T(8,128)(2,1)S(1)} collective-permute-done((bf16[128,1024]{1,0:T(8,128)(2,1)S(1)}, bf16[128,1024]{1,0:T(8,128)(2,1)S(1)}, u32[]{:S(2)}, u32[]{:S(2)}) %collective-permute-start.2) | collective-permute-done | bytes 262176 | tf_op jit(solution)/shard_map/ppermute | solution.py:34
  10.3 2.6 %collective-permute-start.3 = (bf16[128,1024]{1,0:T(8,128)(2,1)S(1)}, bf16[128,1024]{1,0:T(8,128)(2,1)S(1)}, u32[]{:S(2)}, u32[]{:S(2)}) collective-permute-start(bf16[128,1024]{1,0:T(8,128)(2,1)S(1)} %collective-permute-done.2.rec_ref), channel_id=1, source_target_pairs={{0,2},{1,63},{2,4},{3,1},{4,6},{5,3},{6,8},{7,5},{8,10},{9,7},{10,... | collective-permute-start | bytes 786440 | tf_op jit(solution)/shard_map/ppermute | solution.py:34
  12.9 3.0 %collective-permute-done.rec_ref = bf16[128,1024]{1,0:T(8,128)(2,1)S(1)} collective-permute-done((bf16[128,1024]{1,0:T(8,128)(2,1)S(1)}, bf16[128,1024]{1,0:T(8,128)(2,1)S(1)}, u32[]{:S(2)}, u32[]{:S(2)}) %collective-permute-start) | collective-permute-done | bytes 262176 | tf_op jit(solution)/shard_map/ppermute | solution.py:34
  16.0 2.6 %collective-permute-start.1 = (bf16[128,1024]{1,0:T(8,128)(2,1)S(1)}, bf16[128,1024]{1,0:T(8,128)(2,1)S(1)}, u32[]{:S(2)}, u32[]{:S(2)}) collective-permute-start(bf16[128,1024]{1,0:T(8,128)(2,1)S(1)} %collective-permute-done.rec_ref), channel_id=1, source_target_pairs={{0,2},{1,63},{2,4},{3,1},{4,6},{5,3},{6,8},{7,5},{8,10},{9,7},{10,... | collective-permute-start | bytes 786440 | tf_op jit(solution)/shard_map/ppermute | solution.py:34
  18.6 1.6 %copy-done = bf16[1024,1024]{1,0:T(8,128)(2,1)S(1)} copy-done((bf16[1024,1024]{1,0:T(8,128)(2,1)S(1)}, bf16[1024,1024]{1,0:T(8,128)(2,1)}, u32[]{:S(2)}) %copy-start) | copy-done | bytes 2097176
  23.6 3.1 %shard_map.79 = (bf16[1024,512]{1,0:T(8,128)(2,1)S(1)}, bf16[512,1024]{1,0:T(8,128)(2,1)S(1)}, bf16[100,512]{1,0:T(8,128)(2,1)S(1)}) custom-call(bf16[512,384]{1,0:T(8,128)(2,1)S(1)} %get-tuple-element.36.counts_ref, bf16[128,1024]{1,0:T(8,128)(2,1)S(1)} %get-tuple-element.68.own_ref, bf16[128,1024]{1,0:T(8,128)(2,1)S(1)} %collective-permute-done.2.rec_ref, ...), custom_call_target="tpu_custom_call" | custom-call | tf_op jit(solution)/shard_map/pallas_call | solution.py:53
  26.7 3.1 %collective-permute-start.9 = (bf16[100,512]{1,0:T(8,128)(2,1)S(1)}, bf16[100,512]{1,0:T(8,128)(2,1)S(1)}, u32[]{:S(2)}, u32[]{:S(2)}) collective-permute-start(bf16[100,512]{1,0:T(8,128)(2,1)S(1)} %get-tuple-element.43.refs_1_), channel_id=1, source_target_pairs={{0,64},{64,0},{1,65},{65,1},{2,66},{66,2},{3,67},{67,3},{4,68},{68... | collective-permute-start | bytes 307208 | tf_op jit(solution)/shard_map/ppermute | solution.py:34
  29.8 1.2 %collective-permute-start.8 = (bf16[100,512]{1,0:T(8,128)(2,1)S(1)}, bf16[100,512]{1,0:T(8,128)(2,1)S(1)}, u32[]{:S(2)}, u32[]{:S(2)}) collective-permute-start(bf16[100,512]{1,0:T(8,128)(2,1)S(1)} %get-tuple-element.43.refs_1_), channel_id=1, source_target_pairs={{0,192},{64,128},{128,64},{192,0},{1,193},{65,129},{129,65},{193,1... | collective-permute-start | bytes 307208 | tf_op jit(solution)/shard_map/ppermute | solution.py:34
  31.3 3.1 %shard_map.78 = (bf16[1024,512]{1,0:T(8,128)(2,1)S(1)}, bf16[512,1024]{1,0:T(8,128)(2,1)S(1)}, bf16[100,512]{1,0:T(8,128)(2,1)S(1)}) custom-call(bf16[512,384]{1,0:T(8,128)(2,1)S(1)} %get-tuple-element.36.counts_ref, bf16[128,1024]{1,0:T(8,128)(2,1)S(1)} %get-tuple-element.69.own_ref, bf16[128,1024]{1,0:T(8,128)(2,1)S(1)} %collective-permute-done.rec_ref, ...), custom_call_target="tpu_custom_call" | custom-call | tf_op jit(solution)/shard_map/pallas_call | solution.py:53
  34.3 1.1 collective-permute-start.6
  35.4 1.2 %collective-permute-start.5 = (bf16[100,512]{1,0:T(8,128)(2,1)S(1)}, bf16[100,512]{1,0:T(8,128)(2,1)S(1)}, u32[]{:S(2)}, u32[]{:S(2)}) collective-permute-start(bf16[100,512]{1,0:T(8,128)(2,1)S(1)} %get-tuple-element.42.refs_0_), channel_id=1, source_target_pairs={{0,192},{64,128},{128,64},{192,0},{1,193},{65,129},{129,65},{193,1... | collective-permute-start | bytes 307208 | tf_op jit(solution)/shard_map/ppermute | solution.py:34
  37.5 3.1 %collective-permute-done.5.refs_3_ = bf16[100,512]{1,0:T(8,128)(2,1)S(1)} collective-permute-done((bf16[100,512]{1,0:T(8,128)(2,1)S(1)}, bf16[100,512]{1,0:T(8,128)(2,1)S(1)}, u32[]{:S(2)}, u32[]{:S(2)}) %collective-permute-start.5) | collective-permute-done | bytes 102432 | tf_op jit(solution)/shard_map/ppermute | solution.py:34
  40.7 1.4 %collective-permute-done.4.refs_2_ = bf16[100,512]{1,0:T(8,128)(2,1)S(1)} collective-permute-done((bf16[100,512]{1,0:T(8,128)(2,1)S(1)}, bf16[100,512]{1,0:T(8,128)(2,1)S(1)}, u32[]{:S(2)}, u32[]{:S(2)}) %collective-permute-start.4) | collective-permute-done | bytes 102432 | tf_op jit(solution)/shard_map/ppermute | solution.py:34
  42.1 2.3 %shard_map.80 = (bf16[100,512]{1,0:T(8,128)(2,1)S(1)}, bf16[100,512]{1,0:T(8,128)(2,1)S(1)}, bf16[512,512]{1,0:T(8,128)(2,1)S(1)}, bf16[512,512]{1,0:T(8,128)(2,1)S(1)}, bf16[32,2,16,512]{3,2,1,0:T(8,128)(2,1)S(1)}) custom-call(s32[1]{0:T(128)S(6)} %copy.8.len_ref, bf16[100,512]{1,0:T(8,128)(2,1)S(1)} %get-tuple-element.42.refs_0_, ...), custom_call_target="tpu_custom_call" | custom-call | tf_op jit(solution)/shard_map/pallas_call | solution.py:53
  45.4 1.6 %shard_map.81 = (bf16[512,512]{1,0:T(8,128)(2,1)S(1)}, bf16[512,512]{1,0:T(8,128)(2,1)S(1)}, bf16[32,2,16,512]{3,2,1,0:T(8,128)(2,1)S(1)}) custom-call(bf16[100,1024]{1,0:T(8,128)(2,1)S(1)} %get-tuple-element.35.wo_ref.refs_9_, bf16[1024,512]{1,0:T(8,128)(2,1)S(1)} %get-tuple-element.38.refs_10_.t0, bf16[1024,512]{1,0:T(8,128)(2,1)S(1)} %get-tuple-element.39.refs_11_.t1, ...), custom_call_target="tpu_custom_call" | custom-call | tf_op jit(solution)/shard_map/pallas_call | solution.py:53
  47.0 3.1 %shard_map.87 = (f32[128,1024]{1,0:T(8,128)S(1)}, f32[128,1024]{1,0:T(8,128)S(1)}, bf16[128,1024]{1,0:T(8,128)(2,1)S(1)}) custom-call(bf16[384,512]{1,0:T(8,128)(2,1)S(1)} %get-tuple-element.57.flipped_ref, bf16[1024,1024]{1,0:T(8,128)(2,1)S(1)} %get-tuple-element.37.w_ref, bf16[512,512]{1,0:T(8,128)(2,1)S(1)} %get-tuple-element.58.give_ref, ...), custom_call_target="tpu_custom_call" | custom-call | tf_op jit(solution)/shard_map/pallas_call | solution.py:53
  50.1 4.7 %collective-permute-start.20 = (bf16[128,1024]{1,0:T(8,128)(2,1)S(1)}, bf16[128,1024]{1,0:T(8,128)(2,1)S(1)}, u32[]{:S(2)}, u32[]{:S(2)}) collective-permute-start(bf16[128,1024]{1,0:T(8,128)(2,1)S(1)} %get-tuple-element.65), channel_id=1, source_target_pairs={{0,62},{1,3},{2,0},{3,5},{4,2},{5,7},{6,4},{7,9},{8,6},{9,11},{10,... | collective-permute-start | bytes 786440 | tf_op jit(solution)/shard_map/ppermute | solution.py:34
  54.8 3.1 %shard_map.88 = (f32[128,1024]{1,0:T(8,128)S(1)}, f32[128,1024]{1,0:T(8,128)S(1)}, bf16[128,1024]{1,0:T(8,128)(2,1)S(1)}) custom-call(bf16[384,512]{1,0:T(8,128)(2,1)S(1)} %get-tuple-element.57.flipped_ref, bf16[1024,1024]{1,0:T(8,128)(2,1)S(1)} %get-tuple-element.37.w_ref, bf16[512,512]{1,0:T(8,128)(2,1)S(1)} %get-tuple-element.61.give_ref, ...), custom_call_target="tpu_custom_call" | custom-call | tf_op jit(solution)/shard_map/pallas_call | solution.py:53
  57.9 1.8 %collective-permute-start.22 = (bf16[128,1024]{1,0:T(8,128)(2,1)S(1)}, bf16[128,1024]{1,0:T(8,128)(2,1)S(1)}, u32[]{:S(2)}, u32[]{:S(2)}) collective-permute-start(bf16[128,1024]{1,0:T(8,128)(2,1)S(1)} %get-tuple-element.67), channel_id=1, source_target_pairs={{0,62},{1,3},{2,0},{3,5},{4,2},{5,7},{6,4},{7,9},{8,6},{9,11},{10,... | collective-permute-start | bytes 786440 | tf_op jit(solution)/shard_map/ppermute | solution.py:34
  60.0 1.3 %collective-permute-start.11 = (bf16[32,16,256]{2,1,0:T(8,128)(2,1)S(1)}, bf16[32,16,256]{2,1,0:T(8,128)(2,1)S(1)}, u32[]{:S(2)}, u32[]{:S(2)}) collective-permute-start(bf16[32,16,256]{2,1,0:T(8,128)(2,1)S(1)} %get-tuple-element.50), channel_id=1, source_target_pairs={{0,128},{128,0},{1,129},{129,1},{2,130},{130,2},{3,131},{131,3},{4... | collective-permute-start | bytes 786440 | tf_op jit(solution)/shard_map/ppermute | solution.py:34
  62.4 1.6 %collective-permute-start.13 = (bf16[32,16,256]{2,1,0:T(8,128)(2,1)S(1)}, bf16[32,16,256]{2,1,0:T(8,128)(2,1)S(1)}, u32[]{:S(2)}, u32[]{:S(2)}) collective-permute-start(bf16[32,16,256]{2,1,0:T(8,128)(2,1)S(1)} %get-tuple-element.52), channel_id=1, source_target_pairs={{0,129},{1,128},{128,1},{129,0},{2,131},{3,130},{130,3},{131,2},{4... | collective-permute-start | bytes 786440 | tf_op jit(solution)/shard_map/ppermute | solution.py:34
  64.0 5.1 %collective-permute-start.21 = (bf16[128,1024]{1,0:T(8,128)(2,1)S(1)}, bf16[128,1024]{1,0:T(8,128)(2,1)S(1)}, u32[]{:S(2)}, u32[]{:S(2)}) collective-permute-start(bf16[128,1024]{1,0:T(8,128)(2,1)S(1)} %shard_map.89), channel_id=1, source_target_pairs={{0,1},{1,0},{2,3},{3,2},{4,5},{5,4},{6,7},{7,6},{8,9},{9,8},{10,11... | collective-permute-start | bytes 786440 | tf_op jit(solution)/shard_map/ppermute | solution.py:34
  69.2 5.5 %collective-permute-start.23 = (bf16[128,1024]{1,0:T(8,128)(2,1)S(1)}, bf16[128,1024]{1,0:T(8,128)(2,1)S(1)}, u32[]{:S(2)}, u32[]{:S(2)}) collective-permute-start(bf16[128,1024]{1,0:T(8,128)(2,1)S(1)} %shard_map.90), channel_id=1, source_target_pairs={{0,1},{1,0},{2,3},{3,2},{4,5},{5,4},{6,7},{7,6},{8,9},{9,8},{10,11... | collective-permute-start | bytes 786440 | tf_op jit(solution)/shard_map/ppermute | solution.py:34
  74.8 13.0 %collective-permute-done.13.fourth_ref = bf16[32,16,256]{2,1,0:T(8,128)(2,1)S(1)} collective-permute-done((bf16[32,16,256]{2,1,0:T(8,128)(2,1)S(1)}, bf16[32,16,256]{2,1,0:T(8,128)(2,1)S(1)}, u32[]{:S(2)}, u32[]{:S(2)}) %collective-permute-start.13) | collective-permute-done | bytes 262176 | tf_op jit(solution)/shard_map/ppermute | solution.py:34
  89.0 2.0 %collective-permute-start.16 = (bf16[8,16,256]{2,1,0:T(8,128)(2,1)S(1)}, bf16[8,16,256]{2,1,0:T(8,128)(2,1)S(1)}, u32[]{:S(2)}, u32[]{:S(2)}) collective-permute-start(bf16[8,16,256]{2,1,0:T(8,128)(2,1)S(1)} %get-tuple-element.56), channel_id=1, source_target_pairs={{0,48},{16,0},{32,16},{48,32},{1,49},{17,1},{33,17},{49,33},{2,50}... | collective-permute-start | bytes 196616 | tf_op jit(solution)/shard_map/ppermute | solution.py:34
  91.0 1.7 %collective-permute-done.14.refs_0_ = bf16[8,16,256]{2,1,0:T(8,128)(2,1)S(1)} collective-permute-done((bf16[8,16,256]{2,1,0:T(8,128)(2,1)S(1)}, bf16[8,16,256]{2,1,0:T(8,128)(2,1)S(1)}, u32[]{:S(2)}, u32[]{:S(2)}) %collective-permute-start.14) | collective-permute-done | bytes 65568 | tf_op jit(solution)/shard_map/ppermute | solution.py:34
  93.3 12.7 %all_to_all.5.parts_ref = bf16[8,16,256]{2,1,0:T(8,128)(2,1)S(1)} all-to-all(bf16[8,16,256]{2,1,0:T(8,128)(2,1)S(1)} %shard_map.84), channel_id=1, replica_groups=mesh['xl'=2,'c'=2,'y'=4,'z'=8,'xh'=2] {'z'}, dimensions={0} | all-to-all | bytes 131072 | tf_op jit(solution)/shard_map/all_to_all | solution.py:296
  106.0 3.4 %collective-permute-start.19 = (bf16[16,256]{1,0:T(8,128)(2,1)S(1)}, bf16[16,256]{1,0:T(8,128)(2,1)S(1)}, u32[]{:S(2)}, u32[]{:S(2)}) collective-permute-start(bf16[16,256]{1,0:T(8,128)(2,1)S(1)} %shard_map.85.mine_ref), channel_id=1, source_target_pairs={{0,192},{64,128},{128,64},{192,0},{1,193},{65,129},{129,65},{193,1... | collective-permute-start | bytes 24584 | tf_op jit(solution)/shard_map/ppermute | solution.py:34
  109.4 1.5 %collective-permute-start.18 = (bf16[16,256]{1,0:T(8,128)(2,1)S(1)}, bf16[16,256]{1,0:T(8,128)(2,1)S(1)}, u32[]{:S(2)}, u32[]{:S(2)}) collective-permute-start(bf16[16,256]{1,0:T(8,128)(2,1)S(1)} %shard_map.85.mine_ref), channel_id=1, source_target_pairs={{0,64},{64,0},{1,65},{65,1},{2,66},{66,2},{3,67},{67,3},{4,68},{68... | collective-permute-start | bytes 24584 | tf_op jit(solution)/shard_map/ppermute | solution.py:34
  110.9 1.3 %collective-permute-start.17 = (bf16[16,256]{1,0:T(8,128)(2,1)S(1)}, bf16[16,256]{1,0:T(8,128)(2,1)S(1)}, u32[]{:S(2)}, u32[]{:S(2)}) collective-permute-start(bf16[16,256]{1,0:T(8,128)(2,1)S(1)} %shard_map.85.mine_ref), channel_id=1, source_target_pairs={{0,128},{128,0},{1,129},{129,1},{2,130},{130,2},{3,131},{131,3},{4... | collective-permute-start | bytes 24584 | tf_op jit(solution)/shard_map/ppermute | solution.py:34
  (41 shorter events, 10.4 us)
Async XLA Ops:
  1.7 8.6 %collective-permute-start.2 = (bf16[128,1024]{1,0:T(8,128)(2,1)S(1)}, bf16[128,1024]{1,0:T(8,128)(2,1)S(1)}, u32[]{:S(2)}, u32[]{:S(2)}) collective-permute-start(bf16[128,1024]{1,0:T(8,128)(2,1)S(1)} %get-tuple-element.68.own_ref), channel_id=1, source_target_pairs={{0,1},{1,0},{2,3},{3,2},{4,5},{5,4},{6,7},{7,6},{8,9},{9,8},{10,11... | collective-permute-start | bytes 786440 | tf_op jit(solution)/shard_map/ppermute | solution.py:34
  5.3 10.6 %collective-permute-start = (bf16[128,1024]{1,0:T(8,128)(2,1)S(1)}, bf16[128,1024]{1,0:T(8,128)(2,1)S(1)}, u32[]{:S(2)}, u32[]{:S(2)}) collective-permute-start(bf16[128,1024]{1,0:T(8,128)(2,1)S(1)} %get-tuple-element.69.own_ref), channel_id=1, source_target_pairs={{0,1},{1,0},{2,3},{3,2},{4,5},{5,4},{6,7},{7,6},{8,9},{9,8},{10,11... | collective-permute-start | bytes 786440 | tf_op jit(solution)/shard_map/ppermute | solution.py:34
  10.3 13.2 %collective-permute-start.3 = (bf16[128,1024]{1,0:T(8,128)(2,1)S(1)}, bf16[128,1024]{1,0:T(8,128)(2,1)S(1)}, u32[]{:S(2)}, u32[]{:S(2)}) collective-permute-start(bf16[128,1024]{1,0:T(8,128)(2,1)S(1)} %collective-permute-done.2.rec_ref), channel_id=1, source_target_pairs={{0,2},{1,63},{2,4},{3,1},{4,6},{5,3},{6,8},{7,5},{8,10},{9,7},{10,... | collective-permute-start | bytes 786440 | tf_op jit(solution)/shard_map/ppermute | solution.py:34
  16.0 15.3 %collective-permute-start.1 = (bf16[128,1024]{1,0:T(8,128)(2,1)S(1)}, bf16[128,1024]{1,0:T(8,128)(2,1)S(1)}, u32[]{:S(2)}, u32[]{:S(2)}) collective-permute-start(bf16[128,1024]{1,0:T(8,128)(2,1)S(1)} %collective-permute-done.rec_ref), channel_id=1, source_target_pairs={{0,2},{1,63},{2,4},{3,1},{4,6},{5,3},{6,8},{7,5},{8,10},{9,7},{10,... | collective-permute-start | bytes 786440 | tf_op jit(solution)/shard_map/ppermute | solution.py:34
  18.6 1.6 %copy-start = (bf16[1024,1024]{1,0:T(8,128)(2,1)S(1)}, bf16[1024,1024]{1,0:T(8,128)(2,1)}, u32[]{:S(2)}) copy-start(bf16[1024,1024]{1,0:T(8,128)(2,1)} %refs_0_.1) | copy-start | bytes 6291460
  20.1 0.9 copy-start.1
  21.1 0.9 copy-start.2
  22.0 0.7 copy-start.3
  26.7 9.9 %collective-permute-start.9 = (bf16[100,512]{1,0:T(8,128)(2,1)S(1)}, bf16[100,512]{1,0:T(8,128)(2,1)S(1)}, u32[]{:S(2)}, u32[]{:S(2)}) collective-permute-start(bf16[100,512]{1,0:T(8,128)(2,1)S(1)} %get-tuple-element.43.refs_1_), channel_id=1, source_target_pairs={{0,64},{64,0},{1,65},{65,1},{2,66},{66,2},{3,67},{67,3},{4,68},{68... | collective-permute-start | bytes 307208 | tf_op jit(solution)/shard_map/ppermute | solution.py:34
  29.8 7.7 %collective-permute-start.8 = (bf16[100,512]{1,0:T(8,128)(2,1)S(1)}, bf16[100,512]{1,0:T(8,128)(2,1)S(1)}, u32[]{:S(2)}, u32[]{:S(2)}) collective-permute-start(bf16[100,512]{1,0:T(8,128)(2,1)S(1)} %get-tuple-element.43.refs_1_), channel_id=1, source_target_pairs={{0,192},{64,128},{128,64},{192,0},{1,193},{65,129},{129,65},{193,1... | collective-permute-start | bytes 307208 | tf_op jit(solution)/shard_map/ppermute | solution.py:34
  31.0 6.5 %collective-permute-start.7 = (bf16[100,512]{1,0:T(8,128)(2,1)S(1)}, bf16[100,512]{1,0:T(8,128)(2,1)S(1)}, u32[]{:S(2)}, u32[]{:S(2)}) collective-permute-start(bf16[100,512]{1,0:T(8,128)(2,1)S(1)} %get-tuple-element.43.refs_1_), channel_id=1, source_target_pairs={{0,128},{128,0},{1,129},{129,1},{2,130},{130,2},{3,131},{131,3},{4... | collective-permute-start | bytes 307208 | tf_op jit(solution)/shard_map/ppermute | solution.py:34
  34.3 3.2 %collective-permute-start.6 = (bf16[100,512]{1,0:T(8,128)(2,1)S(1)}, bf16[100,512]{1,0:T(8,128)(2,1)S(1)}, u32[]{:S(2)}, u32[]{:S(2)}) collective-permute-start(bf16[100,512]{1,0:T(8,128)(2,1)S(1)} %get-tuple-element.42.refs_0_), channel_id=1, source_target_pairs={{0,64},{64,0},{1,65},{65,1},{2,66},{66,2},{3,67},{67,3},{4,68},{68... | collective-permute-start | bytes 307208 | tf_op jit(solution)/shard_map/ppermute | solution.py:34
  35.4 5.3 %collective-permute-start.5 = (bf16[100,512]{1,0:T(8,128)(2,1)S(1)}, bf16[100,512]{1,0:T(8,128)(2,1)S(1)}, u32[]{:S(2)}, u32[]{:S(2)}) collective-permute-start(bf16[100,512]{1,0:T(8,128)(2,1)S(1)} %get-tuple-element.42.refs_0_), channel_id=1, source_target_pairs={{0,192},{64,128},{128,64},{192,0},{1,193},{65,129},{129,65},{193,1... | collective-permute-start | bytes 307208 | tf_op jit(solution)/shard_map/ppermute | solution.py:34
  36.6 5.5 %collective-permute-start.4 = (bf16[100,512]{1,0:T(8,128)(2,1)S(1)}, bf16[100,512]{1,0:T(8,128)(2,1)S(1)}, u32[]{:S(2)}, u32[]{:S(2)}) collective-permute-start(bf16[100,512]{1,0:T(8,128)(2,1)S(1)} %get-tuple-element.42.refs_0_), channel_id=1, source_target_pairs={{0,128},{128,0},{1,129},{129,1},{2,130},{130,2},{3,131},{131,3},{4... | collective-permute-start | bytes 307208 | tf_op jit(solution)/shard_map/ppermute | solution.py:34
  44.4 15.4 %collective-permute-start.10 = (bf16[32,2,16,512]{3,2,1,0:T(8,128)(2,1)S(1)}, bf16[32,2,16,512]{3,2,1,0:T(8,128)(2,1)S(1)}, u32[]{:S(2)}, u32[]{:S(2)}) collective-permute-start(bf16[32,2,16,512]{3,2,1,0:T(8,128)(2,1)S(1)} %get-tuple-element.48), channel_id=1, source_target_pairs={{0,64},{64,0},{1,65},{65,1},{2,66},{66,2},{3,67},{67,3},{4,68},{68... | collective-permute-start | bytes 3145736 | tf_op jit(solution)/shard_map/ppermute | solution.py:34
  50.1 13.8 %collective-permute-start.20 = (bf16[128,1024]{1,0:T(8,128)(2,1)S(1)}, bf16[128,1024]{1,0:T(8,128)(2,1)S(1)}, u32[]{:S(2)}, u32[]{:S(2)}) collective-permute-start(bf16[128,1024]{1,0:T(8,128)(2,1)S(1)} %get-tuple-element.65), channel_id=1, source_target_pairs={{0,62},{1,3},{2,0},{3,5},{4,2},{5,7},{6,4},{7,9},{8,6},{9,11},{10,... | collective-permute-start | bytes 786440 | tf_op jit(solution)/shard_map/ppermute | solution.py:34
  57.9 11.2 %collective-permute-start.22 = (bf16[128,1024]{1,0:T(8,128)(2,1)S(1)}, bf16[128,1024]{1,0:T(8,128)(2,1)S(1)}, u32[]{:S(2)}, u32[]{:S(2)}) collective-permute-start(bf16[128,1024]{1,0:T(8,128)(2,1)S(1)} %get-tuple-element.67), channel_id=1, source_target_pairs={{0,62},{1,3},{2,0},{3,5},{4,2},{5,7},{6,4},{7,9},{8,6},{9,11},{10,... | collective-permute-start | bytes 786440 | tf_op jit(solution)/shard_map/ppermute | solution.py:34
  60.0 14.7 %collective-permute-start.11 = (bf16[32,16,256]{2,1,0:T(8,128)(2,1)S(1)}, bf16[32,16,256]{2,1,0:T(8,128)(2,1)S(1)}, u32[]{:S(2)}, u32[]{:S(2)}) collective-permute-start(bf16[32,16,256]{2,1,0:T(8,128)(2,1)S(1)} %get-tuple-element.50), channel_id=1, source_target_pairs={{0,128},{128,0},{1,129},{129,1},{2,130},{130,2},{3,131},{131,3},{4... | collective-permute-start | bytes 786440 | tf_op jit(solution)/shard_map/ppermute | solution.py:34
  61.3 13.4 %collective-permute-start.12 = (bf16[32,16,256]{2,1,0:T(8,128)(2,1)S(1)}, bf16[32,16,256]{2,1,0:T(8,128)(2,1)S(1)}, u32[]{:S(2)}, u32[]{:S(2)}) collective-permute-start(bf16[32,16,256]{2,1,0:T(8,128)(2,1)S(1)} %get-tuple-element.51), channel_id=1, source_target_pairs={{0,1},{1,0},{2,3},{3,2},{4,5},{5,4},{6,7},{7,6},{8,9},{9,8},{10,11... | collective-permute-start | bytes 786440 | tf_op jit(solution)/shard_map/ppermute | solution.py:34
  62.4 25.4 %collective-permute-start.13 = (bf16[32,16,256]{2,1,0:T(8,128)(2,1)S(1)}, bf16[32,16,256]{2,1,0:T(8,128)(2,1)S(1)}, u32[]{:S(2)}, u32[]{:S(2)}) collective-permute-start(bf16[32,16,256]{2,1,0:T(8,128)(2,1)S(1)} %get-tuple-element.52), channel_id=1, source_target_pairs={{0,129},{1,128},{128,1},{129,0},{2,131},{3,130},{130,3},{131,2},{4... | collective-permute-start | bytes 786440 | tf_op jit(solution)/shard_map/ppermute | solution.py:34
  64.0 48.1 %collective-permute-start.21 = (bf16[128,1024]{1,0:T(8,128)(2,1)S(1)}, bf16[128,1024]{1,0:T(8,128)(2,1)S(1)}, u32[]{:S(2)}, u32[]{:S(2)}) collective-permute-start(bf16[128,1024]{1,0:T(8,128)(2,1)S(1)} %shard_map.89), channel_id=1, source_target_pairs={{0,1},{1,0},{2,3},{3,2},{4,5},{5,4},{6,7},{7,6},{8,9},{9,8},{10,11... | collective-permute-start | bytes 786440 | tf_op jit(solution)/shard_map/ppermute | solution.py:34
  69.2 43.0 %collective-permute-start.23 = (bf16[128,1024]{1,0:T(8,128)(2,1)S(1)}, bf16[128,1024]{1,0:T(8,128)(2,1)S(1)}, u32[]{:S(2)}, u32[]{:S(2)}) collective-permute-start(bf16[128,1024]{1,0:T(8,128)(2,1)S(1)} %shard_map.90), channel_id=1, source_target_pairs={{0,1},{1,0},{2,3},{3,2},{4,5},{5,4},{6,7},{7,6},{8,9},{9,8},{10,11... | collective-permute-start | bytes 786440 | tf_op jit(solution)/shard_map/ppermute | solution.py:34
  87.8 4.8 %collective-permute-start.14 = (bf16[8,16,256]{2,1,0:T(8,128)(2,1)S(1)}, bf16[8,16,256]{2,1,0:T(8,128)(2,1)S(1)}, u32[]{:S(2)}, u32[]{:S(2)}) collective-permute-start(bf16[8,16,256]{2,1,0:T(8,128)(2,1)S(1)} %get-tuple-element.54), channel_id=1, source_target_pairs={{0,32},{16,48},{32,0},{48,16},{1,33},{17,49},{33,1},{49,17},{2,34}... | collective-permute-start | bytes 196616 | tf_op jit(solution)/shard_map/ppermute | solution.py:34
  88.3 5.0 %collective-permute-start.15 = (bf16[8,16,256]{2,1,0:T(8,128)(2,1)S(1)}, bf16[8,16,256]{2,1,0:T(8,128)(2,1)S(1)}, u32[]{:S(2)}, u32[]{:S(2)}) collective-permute-start(bf16[8,16,256]{2,1,0:T(8,128)(2,1)S(1)} %get-tuple-element.55), channel_id=1, source_target_pairs={{0,16},{16,32},{32,48},{48,0},{1,17},{17,33},{33,49},{49,1},{2,18}... | collective-permute-start | bytes 196616 | tf_op jit(solution)/shard_map/ppermute | solution.py:34
  89.0 4.3 %collective-permute-start.16 = (bf16[8,16,256]{2,1,0:T(8,128)(2,1)S(1)}, bf16[8,16,256]{2,1,0:T(8,128)(2,1)S(1)}, u32[]{:S(2)}, u32[]{:S(2)}) collective-permute-start(bf16[8,16,256]{2,1,0:T(8,128)(2,1)S(1)} %get-tuple-element.56), channel_id=1, source_target_pairs={{0,48},{16,0},{32,16},{48,32},{1,49},{17,1},{33,17},{49,33},{2,50}... | collective-permute-start | bytes 196616 | tf_op jit(solution)/shard_map/ppermute | solution.py:34
  106.0 7.1 %collective-permute-start.19 = (bf16[16,256]{1,0:T(8,128)(2,1)S(1)}, bf16[16,256]{1,0:T(8,128)(2,1)S(1)}, u32[]{:S(2)}, u32[]{:S(2)}) collective-permute-start(bf16[16,256]{1,0:T(8,128)(2,1)S(1)} %shard_map.85.mine_ref), channel_id=1, source_target_pairs={{0,192},{64,128},{128,64},{192,0},{1,193},{65,129},{129,65},{193,1... | collective-permute-start | bytes 24584 | tf_op jit(solution)/shard_map/ppermute | solution.py:34
  109.4 3.7 %collective-permute-start.18 = (bf16[16,256]{1,0:T(8,128)(2,1)S(1)}, bf16[16,256]{1,0:T(8,128)(2,1)S(1)}, u32[]{:S(2)}, u32[]{:S(2)}) collective-permute-start(bf16[16,256]{1,0:T(8,128)(2,1)S(1)} %shard_map.85.mine_ref), channel_id=1, source_target_pairs={{0,64},{64,0},{1,65},{65,1},{2,66},{66,2},{3,67},{67,3},{4,68},{68... | collective-permute-start | bytes 24584 | tf_op jit(solution)/shard_map/ppermute | solution.py:34
  110.9 2.6 %collective-permute-start.17 = (bf16[16,256]{1,0:T(8,128)(2,1)S(1)}, bf16[16,256]{1,0:T(8,128)(2,1)S(1)}, u32[]{:S(2)}, u32[]{:S(2)}) collective-permute-start(bf16[16,256]{1,0:T(8,128)(2,1)S(1)} %shard_map.85.mine_ref), channel_id=1, source_target_pairs={{0,128},{128,0},{1,129},{129,1},{2,130},{130,2},{3,131},{131,3},{4... | collective-permute-start | bytes 24584 | tf_op jit(solution)/shard_map/ppermute | solution.py:34

commit v4 on v3

--- a/solution.py
+++ b/solution.py
@@ -106,15 +106,15 @@
     extended = jnp.concatenate([own_ref[...], rec_ref[...], fwd_ref[...]], axis=0)
     area = dot(counts_ref[...], extended).astype(BF16)
     turned_ref[...] = area.T
-    total = None
-    for n in range(0, w_ref.shape[1], chunk):
-        pre = dot(area, w_ref[:, n : n + chunk])
+    hidden = []
+    for n in range(0, w_ref.shape[1], 2 * chunk):
+        cols = slice(n, n + 2 * chunk)
+        pre = dot(area, w_ref[:, cols])
         sig = 0.5 * jnp.tanh(0.5 * pre) + 0.5
         value = pre * sig
-        gate_ref[:, n : n + chunk] = (sig * (1.0 + (pre - value))).astype(BF16)
-        part = dot(wo_ref[:, n : n + chunk], value.astype(BF16), 1, 1)
-        total = part if total is None else total + part
-    pred_ref[...] = total.astype(BF16)
+        gate_ref[:, cols] = (sig * (1.0 + (pre - value))).astype(BF16)
+        hidden.append(value.astype(BF16))
+    pred_ref[...] = dot(wo_ref[...], jnp.concatenate(hidden, axis=1), 1, 1).astype(BF16)
 
 
 def smooth_sign(value):
@@ -207,9 +207,14 @@
         out_ref[:, cols] = ref[...].astype(F32)
 
 
-def nodes_kernel(own0_ref, own1_ref, far0_ref, far1_ref, out_ref):
-    out_ref[0] = (own0_ref[...] + far0_ref[...].astype(F32)).astype(BF16)
-    out_ref[1] = (own1_ref[...] + far1_ref[...].astype(F32)).astype(BF16)
+def join_kernel(rec0_ref, rec1_ref, far0_ref, far1_ref, out_ref):
+    out_ref[0] = (rec0_ref[...] + far0_ref[...].astype(F32)).astype(BF16)
+    out_ref[1] = (rec1_ref[...] + far1_ref[...].astype(F32)).astype(BF16)
+
+
+def nodes_kernel(own0_ref, own1_ref, far_ref, out_ref):
+    out_ref[0] = (own0_ref[...] + far_ref[0].astype(F32)).astype(BF16)
+    out_ref[1] = (own1_ref[...] + far_ref[1].astype(F32)).astype(BF16)
 
 
 def backward_kernel(flipped_ref, w_ref, give_ref, keep_ref, own_ref, rec_ref, fwd_ref):
@@ -252,11 +257,12 @@
         area.append(a)
         gate.append(p)
         pred.append(q)
-    others = []
-    for q in pred:
-        others += [
-            shifted(q, "xl", 1), permute(q, MEMBER, lambda a, b: (1 - a, 1 - b)), shifted(q, "c", 1)
-        ]
+    near, mate, last = [], [], []
+    for m, q in enumerate(pred):
+        near.append(shifted(q, "xl", 1))
+        mate.append(shifted(q, "c", 1))
+        last.append(shifted(near[m], "c", 1))
+    others = near + mate + last
 
     slope = ((grid_rows, half), BF16)
     out_rows = wide // (n_y * n_z * n_x)
@@ -288,11 +294,9 @@
         )
     far = []
     for b in back:
-        moved = relayed(b[2], -1)
-        far.append(call(total_kernel, [((width, wide), BF16)], b[1], moved)[0])
-
-    for m in range(members):
-        far[m] = shifted(far[m], "xh", 1)
+        far.append(relayed(b[2], -1))
+    (far,) = call(join_kernel, [((members, width, wide), BF16)], *[b[1] for b in back], *far)
+    far = shifted(far, "xh", 1)
     rows = lax.all_to_all(rows, "z", 0, 0)
     (mine,) = call(sum_kernel, [((out_rows, half // 2), BF16)], rows)
     (grad_hidden,) = call(
@@ -301,7 +305,7 @@
         permute(mine, MEMBER, lambda a, b: (1 - a, 1 - b)), final=True,
     )
     (grad_mesh,) = call(
-        nodes_kernel, [((members, width, wide), BF16)], *[b[0] for b in back], *far, final=True
+        nodes_kernel, [((members, width, wide), BF16)], *[b[0] for b in back], far, final=True
     )
     return (grad_hidden, grad_mesh)
 

time: 115 us -> 117 us (1.017)
  waiting for transfers between devices: 28.2 us -> 38.4 us
  starting transfers between devices: 47.5 us -> 43.3 us
  blocking collectives: 12.7 us -> 9.7 us
  Pallas kernels: 19.2 us -> 17.8 us
    ppermute x24 -> x23, waiting for transfers between devices: 28.2 us -> 38.4 us  [permute(): return lax.ppermute(value, axes if len(axes) > 1 else axes[0], pairs)]
    ppermute x24 -> x23, starting transfers between devices: 47.5 us -> 43.3 us  [permute(): return lax.ppermute(value, axes if len(axes) > 1 else axes[0], pairs)]
    all_to_all x1, blocking collectives: 12.7 us -> 9.7 us  [step(): rows = lax.all_to_all(rows, 'z', 0, 0)]
    pallas_call x14 -> x13, Pallas kernels: 18.3 us -> 16.9 us  [call(): pl.pallas_call(kernel, out_shape=[jax.ShapeDtypeStruct(*s) if final else...]
  transfers between devices with their start and end apart: 24 -> 23, of which waited for: 8 -> 11; matrix products, arithmetic and copies ran while one was open for 0% -> 0% of each run, Pallas kernels for 14% -> 13%
where the time goes in v4:
time: 117 us; the launch traced here: 116 us
  starting transfers between devices  43.3 us (37%)
  waiting for transfers between devices  38.4 us (33%)
  Pallas kernels  17.8 us (15%)
  blocking collectives  9.7 us (8%)
  local copies, waits for them, and re-layouts  5.18 us (4%)
  between operations  1.43 us (1%)
    ppermute x23, starting transfers between devices, permute(): return lax.ppermute(value, axes if len(axes) > 1 else axes[0], pairs)  43.3 us
    ppermute x23, waiting for transfers between devices, permute(): return lax.ppermute(value, axes if len(axes) > 1 else axes[0], pairs)  38.4 us
    pallas_call x13, Pallas kernels, call(): pl.pallas_call(kernel, out_shape=[jax.ShapeDtypeStruct(*s) if final else...  16.9 us
    all_to_all x1, blocking collectives, step(): rows = lax.all_to_all(rows, 'z', 0, 0)  9.7 us
    unnamed x8, local copies, waits for them, and re-layouts  4.11 us
  transfers between devices with their start and end apart: 23, of which 11 were waited for; matrix products, arithmetic and copies ran while one was open for 0% of the time, Pallas kernels for 13%

profile of v4, /device:TPU:1, one launch (start us, length us, event | category | flops | bytes accessed | tf_op | source)
XLA Modules:
  0.0 115.8 jit_solution(5673931093252500872)
XLA Ops:
  0.6 1.1 slice_bitcast_fusion
  1.7 3.6 %collective-permute-start.2 = (bf16[128,1024]{1,0:T(8,128)(2,1)S(1)}, bf16[128,1024]{1,0:T(8,128)(2,1)S(1)}, u32[]{:S(2)}, u32[]{:S(2)}) collective-permute-start(bf16[128,1024]{1,0:T(8,128)(2,1)S(1)} %get-tuple-element.68.own_ref), channel_id=1, source_target_pairs={{0,1},{1,0},{2,3},{3,2},{4,5},{5,4},{6,7},{7,6},{8,9},{9,8},{10,11... | collective-permute-start | bytes 786440 | tf_op jit(solution)/shard_map/ppermute | solution.py:34
  5.4 4.9 %collective-permute-done.2.rec_ref = bf16[128,1024]{1,0:T(8,128)(2,1)S(1)} collective-permute-done((bf16[128,1024]{1,0:T(8,128)(2,1)S(1)}, bf16[128,1024]{1,0:T(8,128)(2,1)S(1)}, u32[]{:S(2)}, u32[]{:S(2)}) %collective-permute-start.2) | collective-permute-done | bytes 262176 | tf_op jit(solution)/shard_map/ppermute | solution.py:34
  10.3 2.6 %collective-permute-start.3 = (bf16[128,1024]{1,0:T(8,128)(2,1)S(1)}, bf16[128,1024]{1,0:T(8,128)(2,1)S(1)}, u32[]{:S(2)}, u32[]{:S(2)}) collective-permute-start(bf16[128,1024]{1,0:T(8,128)(2,1)S(1)} %collective-permute-done.2.rec_ref), channel_id=1, source_target_pairs={{0,2},{1,63},{2,4},{3,1},{4,6},{5,3},{6,8},{7,5},{8,10},{9,7},{10,... | collective-permute-start | bytes 786440 | tf_op jit(solution)/shard_map/ppermute | solution.py:34
  12.9 3.0 %collective-permute-done.rec_ref = bf16[128,1024]{1,0:T(8,128)(2,1)S(1)} collective-permute-done((bf16[128,1024]{1,0:T(8,128)(2,1)S(1)}, bf16[128,1024]{1,0:T(8,128)(2,1)S(1)}, u32[]{:S(2)}, u32[]{:S(2)}) %collective-permute-start) | collective-permute-done | bytes 262176 | tf_op jit(solution)/shard_map/ppermute | solution.py:34
  16.0 2.6 %collective-permute-start.1 = (bf16[128,1024]{1,0:T(8,128)(2,1)S(1)}, bf16[128,1024]{1,0:T(8,128)(2,1)S(1)}, u32[]{:S(2)}, u32[]{:S(2)}) collective-permute-start(bf16[128,1024]{1,0:T(8,128)(2,1)S(1)} %collective-permute-done.rec_ref), channel_id=1, source_target_pairs={{0,2},{1,63},{2,4},{3,1},{4,6},{5,3},{6,8},{7,5},{8,10},{9,7},{10,... | collective-permute-start | bytes 786440 | tf_op jit(solution)/shard_map/ppermute | solution.py:34
  18.6 1.6 %copy-done = bf16[1024,1024]{1,0:T(8,128)(2,1)S(1)} copy-done((bf16[1024,1024]{1,0:T(8,128)(2,1)S(1)}, bf16[1024,1024]{1,0:T(8,128)(2,1)}, u32[]{:S(2)}) %copy-start) | copy-done | bytes 2097176
  20.1 0.9 copy-done.1
  22.7 0.9 shard_map.77
  23.6 2.4 %shard_map.79 = (bf16[1024,512]{1,0:T(8,128)(2,1)S(1)}, bf16[512,1024]{1,0:T(8,128)(2,1)S(1)}, bf16[100,512]{1,0:T(8,128)(2,1)S(1)}) custom-call(bf16[512,384]{1,0:T(8,128)(2,1)S(1)} %get-tuple-element.36.counts_ref, bf16[128,1024]{1,0:T(8,128)(2,1)S(1)} %get-tuple-element.68.own_ref, bf16[128,1024]{1,0:T(8,128)(2,1)S(1)} %collective-permute-done.2.rec_ref, ...), custom_call_target="tpu_custom_call" | custom-call | tf_op jit(solution)/shard_map/pallas_call | solution.py:53
  26.0 1.3 %collective-permute-start.5 = (bf16[100,512]{1,0:T(8,128)(2,1)S(1)}, bf16[100,512]{1,0:T(8,128)(2,1)S(1)}, u32[]{:S(2)}, u32[]{:S(2)}) collective-permute-start(bf16[100,512]{1,0:T(8,128)(2,1)S(1)} %get-tuple-element.43.refs_1_), channel_id=1, source_target_pairs={{0,128},{128,0},{1,129},{129,1},{2,130},{130,2},{3,131},{131,3},{4... | collective-permute-start | bytes 307208 | tf_op jit(solution)/shard_map/ppermute | solution.py:34
  27.3 2.8 %collective-permute-done.1.fwd_ref = bf16[128,1024]{1,0:T(8,128)(2,1)S(1)} collective-permute-done((bf16[128,1024]{1,0:T(8,128)(2,1)S(1)}, bf16[128,1024]{1,0:T(8,128)(2,1)S(1)}, u32[]{:S(2)}, u32[]{:S(2)}) %collective-permute-start.1) | collective-permute-done | bytes 262176 | tf_op jit(solution)/shard_map/ppermute | solution.py:34
  30.2 2.4 %shard_map.78 = (bf16[1024,512]{1,0:T(8,128)(2,1)S(1)}, bf16[512,1024]{1,0:T(8,128)(2,1)S(1)}, bf16[100,512]{1,0:T(8,128)(2,1)S(1)}) custom-call(bf16[512,384]{1,0:T(8,128)(2,1)S(1)} %get-tuple-element.36.counts_ref, bf16[128,1024]{1,0:T(8,128)(2,1)S(1)} %get-tuple-element.69.own_ref, bf16[128,1024]{1,0:T(8,128)(2,1)S(1)} %collective-permute-done.rec_ref, ...), custom_call_target="tpu_custom_call" | custom-call | tf_op jit(solution)/shard_map/pallas_call | solution.py:53
  32.6 1.3 %collective-permute-start.4 = (bf16[100,512]{1,0:T(8,128)(2,1)S(1)}, bf16[100,512]{1,0:T(8,128)(2,1)S(1)}, u32[]{:S(2)}, u32[]{:S(2)}) collective-permute-start(bf16[100,512]{1,0:T(8,128)(2,1)S(1)} %get-tuple-element.42.refs_0_), channel_id=1, source_target_pairs={{0,128},{128,0},{1,129},{129,1},{2,130},{130,2},{3,131},{131,3},{4... | collective-permute-start | bytes 307208 | tf_op jit(solution)/shard_map/ppermute | solution.py:34
  33.9 2.4 %collective-permute-start.7 = (bf16[100,512]{1,0:T(8,128)(2,1)S(1)}, bf16[100,512]{1,0:T(8,128)(2,1)S(1)}, u32[]{:S(2)}, u32[]{:S(2)}) collective-permute-start(bf16[100,512]{1,0:T(8,128)(2,1)S(1)} %get-tuple-element.43.refs_1_), channel_id=1, source_target_pairs={{0,64},{64,0},{1,65},{65,1},{2,66},{66,2},{3,67},{67,3},{4,68},{68... | collective-permute-start | bytes 307208 | tf_op jit(solution)/shard_map/ppermute | solution.py:34
  36.7 2.7 %collective-permute-start.8 = (bf16[100,512]{1,0:T(8,128)(2,1)S(1)}, bf16[100,512]{1,0:T(8,128)(2,1)S(1)}, u32[]{:S(2)}, u32[]{:S(2)}) collective-permute-start(bf16[100,512]{1,0:T(8,128)(2,1)S(1)} %collective-permute-done.4.refs_2_), channel_id=1, source_target_pairs={{0,64},{64,0},{1,65},{65,1},{2,66},{66,2},{3,67},{67,3},{4,68},{68... | collective-permute-start | bytes 307208 | tf_op jit(solution)/shard_map/ppermute | solution.py:34
  40.4 2.3 %shard_map.80 = (bf16[100,512]{1,0:T(8,128)(2,1)S(1)}, bf16[100,512]{1,0:T(8,128)(2,1)S(1)}, bf16[512,512]{1,0:T(8,128)(2,1)S(1)}, bf16[512,512]{1,0:T(8,128)(2,1)S(1)}, bf16[32,2,16,512]{3,2,1,0:T(8,128)(2,1)S(1)}) custom-call(s32[1]{0:T(128)S(6)} %copy.8.len_ref, bf16[100,512]{1,0:T(8,128)(2,1)S(1)} %get-tuple-element.42.refs_0_, ...), custom_call_target="tpu_custom_call" | custom-call | tf_op jit(solution)/shard_map/pallas_call | solution.py:53
  43.3 1.6 %shard_map.81 = (bf16[512,512]{1,0:T(8,128)(2,1)S(1)}, bf16[512,512]{1,0:T(8,128)(2,1)S(1)}, bf16[32,2,16,512]{3,2,1,0:T(8,128)(2,1)S(1)}) custom-call(bf16[100,1024]{1,0:T(8,128)(2,1)S(1)} %get-tuple-element.35.wo_ref.refs_9_, bf16[1024,512]{1,0:T(8,128)(2,1)S(1)} %get-tuple-element.38.refs_10_.t0, bf16[1024,512]{1,0:T(8,128)(2,1)S(1)} %get-tuple-element.39.refs_11_.t1, ...), custom_call_target="tpu_custom_call" | custom-call | tf_op jit(solution)/shard_map/pallas_call | solution.py:53
  44.9 3.1 %shard_map.87 = (f32[128,1024]{1,0:T(8,128)S(1)}, f32[128,1024]{1,0:T(8,128)S(1)}, bf16[128,1024]{1,0:T(8,128)(2,1)S(1)}) custom-call(bf16[384,512]{1,0:T(8,128)(2,1)S(1)} %get-tuple-element.57.flipped_ref, bf16[1024,1024]{1,0:T(8,128)(2,1)S(1)} %get-tuple-element.37.w_ref, bf16[512,512]{1,0:T(8,128)(2,1)S(1)} %get-tuple-element.58.give_ref, ...), custom_call_target="tpu_custom_call" | custom-call | tf_op jit(solution)/shard_map/pallas_call | solution.py:53
  48.0 3.4 %collective-permute-start.20 = (bf16[128,1024]{1,0:T(8,128)(2,1)S(1)}, bf16[128,1024]{1,0:T(8,128)(2,1)S(1)}, u32[]{:S(2)}, u32[]{:S(2)}) collective-permute-start(bf16[128,1024]{1,0:T(8,128)(2,1)S(1)} %get-tuple-element.66), channel_id=1, source_target_pairs={{0,62},{1,3},{2,0},{3,5},{4,2},{5,7},{6,4},{7,9},{8,6},{9,11},{10,... | collective-permute-start | bytes 786440 | tf_op jit(solution)/shard_map/ppermute | solution.py:34
  51.4 3.1 %shard_map.88 = (f32[128,1024]{1,0:T(8,128)S(1)}, f32[128,1024]{1,0:T(8,128)S(1)}, bf16[128,1024]{1,0:T(8,128)(2,1)S(1)}) custom-call(bf16[384,512]{1,0:T(8,128)(2,1)S(1)} %get-tuple-element.57.flipped_ref, bf16[1024,1024]{1,0:T(8,128)(2,1)S(1)} %get-tuple-element.37.w_ref, bf16[512,512]{1,0:T(8,128)(2,1)S(1)} %get-tuple-element.61.give_ref, ...), custom_call_target="tpu_custom_call" | custom-call | tf_op jit(solution)/shard_map/pallas_call | solution.py:53
  54.5 1.8 %collective-permute-start.21 = (bf16[128,1024]{1,0:T(8,128)(2,1)S(1)}, bf16[128,1024]{1,0:T(8,128)(2,1)S(1)}, u32[]{:S(2)}, u32[]{:S(2)}) collective-permute-start(bf16[128,1024]{1,0:T(8,128)(2,1)S(1)} %get-tuple-element.67), channel_id=1, source_target_pairs={{0,62},{1,3},{2,0},{3,5},{4,2},{5,7},{6,4},{7,9},{8,6},{9,11},{10,... | collective-permute-start | bytes 786440 | tf_op jit(solution)/shard_map/ppermute | solution.py:34
  56.9 5.6 %collective-permute-done.21.far1_ref = bf16[128,1024]{1,0:T(8,128)(2,1)S(1)} collective-permute-done((bf16[128,1024]{1,0:T(8,128)(2,1)S(1)}, bf16[128,1024]{1,0:T(8,128)(2,1)S(1)}, u32[]{:S(2)}, u32[]{:S(2)}) %collective-permute-start.21) | collective-permute-done | bytes 262176 | tf_op jit(solution)/shard_map/ppermute | solution.py:34
  62.6 8.3 %collective-permute-start.22 = (bf16[2,128,1024]{2,1,0:T(8,128)(2,1)S(1)}, bf16[2,128,1024]{2,1,0:T(8,128)(2,1)S(1)}, u32[]{:S(2)}, u32[]{:S(2)}) collective-permute-start(bf16[2,128,1024]{2,1,0:T(8,128)(2,1)S(1)} %shard_map.89), channel_id=1, source_target_pairs={{0,1},{1,0},{2,3},{3,2},{4,5},{5,4},{6,7},{7,6},{8,9},{9,8},{10,11... | collective-permute-start | bytes 1572872 | tf_op jit(solution)/shard_map/ppermute | solution.py:34
  71.9 3.3 %collective-permute-start.13 = (bf16[32,16,256]{2,1,0:T(8,128)(2,1)S(1)}, bf16[32,16,256]{2,1,0:T(8,128)(2,1)S(1)}, u32[]{:S(2)}, u32[]{:S(2)}) collective-permute-start(bf16[32,16,256]{2,1,0:T(8,128)(2,1)S(1)} %get-tuple-element.52), channel_id=1, source_target_pairs={{0,129},{1,128},{128,1},{129,0},{2,131},{3,130},{130,3},{131,2},{4... | collective-permute-start | bytes 786440 | tf_op jit(solution)/shard_map/ppermute | solution.py:34
  75.2 12.4 %collective-permute-done.11.second_ref = bf16[32,16,256]{2,1,0:T(8,128)(2,1)S(1)} collective-permute-done((bf16[32,16,256]{2,1,0:T(8,128)(2,1)S(1)}, bf16[32,16,256]{2,1,0:T(8,128)(2,1)S(1)}, u32[]{:S(2)}, u32[]{:S(2)}) %collective-permute-start.11) | collective-permute-done | bytes 262176 | tf_op jit(solution)/shard_map/ppermute | solution.py:34
  87.6 6.0 %collective-permute-done.12.third_ref = bf16[32,16,256]{2,1,0:T(8,128)(2,1)S(1)} collective-permute-done((bf16[32,16,256]{2,1,0:T(8,128)(2,1)S(1)}, bf16[32,16,256]{2,1,0:T(8,128)(2,1)S(1)}, u32[]{:S(2)}, u32[]{:S(2)}) %collective-permute-start.12) | collective-permute-done | bytes 262176 | tf_op jit(solution)/shard_map/ppermute | solution.py:34
  93.8 2.7 %collective-permute-start.16 = (bf16[8,16,256]{2,1,0:T(8,128)(2,1)S(1)}, bf16[8,16,256]{2,1,0:T(8,128)(2,1)S(1)}, u32[]{:S(2)}, u32[]{:S(2)}) collective-permute-start(bf16[8,16,256]{2,1,0:T(8,128)(2,1)S(1)} %get-tuple-element.56), channel_id=1, source_target_pairs={{0,48},{16,0},{32,16},{48,32},{1,49},{17,1},{33,17},{49,33},{2,50}... | collective-permute-start | bytes 196616 | tf_op jit(solution)/shard_map/ppermute | solution.py:34
  96.5 2.0 %collective-permute-done.14.refs_0_ = bf16[8,16,256]{2,1,0:T(8,128)(2,1)S(1)} collective-permute-done((bf16[8,16,256]{2,1,0:T(8,128)(2,1)S(1)}, bf16[8,16,256]{2,1,0:T(8,128)(2,1)S(1)}, u32[]{:S(2)}, u32[]{:S(2)}) %collective-permute-start.14) | collective-permute-done | bytes 65568 | tf_op jit(solution)/shard_map/ppermute | solution.py:34
  98.9 9.7 %all_to_all.5.parts_ref = bf16[8,16,256]{2,1,0:T(8,128)(2,1)S(1)} all-to-all(bf16[8,16,256]{2,1,0:T(8,128)(2,1)S(1)} %shard_map.84), channel_id=1, replica_groups=mesh['xl'=2,'c'=2,'y'=4,'z'=8,'xh'=2] {'z'}, dimensions={0} | all-to-all | bytes 131072 | tf_op jit(solution)/shard_map/all_to_all | solution.py:300
  108.6 3.7 %collective-permute-start.19 = (bf16[16,256]{1,0:T(8,128)(2,1)S(1)}, bf16[16,256]{1,0:T(8,128)(2,1)S(1)}, u32[]{:S(2)}, u32[]{:S(2)}) collective-permute-start(bf16[16,256]{1,0:T(8,128)(2,1)S(1)} %shard_map.85.mine_ref), channel_id=1, source_target_pairs={{0,192},{64,128},{128,64},{192,0},{1,193},{65,129},{129,65},{193,1... | collective-permute-start | bytes 24584 | tf_op jit(solution)/shard_map/ppermute | solution.py:34
  112.6 1.3 %collective-permute-start.17 = (bf16[16,256]{1,0:T(8,128)(2,1)S(1)}, bf16[16,256]{1,0:T(8,128)(2,1)S(1)}, u32[]{:S(2)}, u32[]{:S(2)}) collective-permute-start(bf16[16,256]{1,0:T(8,128)(2,1)S(1)} %shard_map.85.mine_ref), channel_id=1, source_target_pairs={{0,128},{128,0},{1,129},{129,1},{2,130},{130,2},{3,131},{131,3},{4... | collective-permute-start | bytes 24584 | tf_op jit(solution)/shard_map/ppermute | solution.py:34
  (38 shorter events, 7.7 us)
Async XLA Ops:
  1.7 8.6 %collective-permute-start.2 = (bf16[128,1024]{1,0:T(8,128)(2,1)S(1)}, bf16[128,1024]{1,0:T(8,128)(2,1)S(1)}, u32[]{:S(2)}, u32[]{:S(2)}) collective-permute-start(bf16[128,1024]{1,0:T(8,128)(2,1)S(1)} %get-tuple-element.68.own_ref), channel_id=1, source_target_pairs={{0,1},{1,0},{2,3},{3,2},{4,5},{5,4},{6,7},{7,6},{8,9},{9,8},{10,11... | collective-permute-start | bytes 786440 | tf_op jit(solution)/shard_map/ppermute | solution.py:34
  5.3 10.6 %collective-permute-start = (bf16[128,1024]{1,0:T(8,128)(2,1)S(1)}, bf16[128,1024]{1,0:T(8,128)(2,1)S(1)}, u32[]{:S(2)}, u32[]{:S(2)}) collective-permute-start(bf16[128,1024]{1,0:T(8,128)(2,1)S(1)} %get-tuple-element.69.own_ref), channel_id=1, source_target_pairs={{0,1},{1,0},{2,3},{3,2},{4,5},{5,4},{6,7},{7,6},{8,9},{9,8},{10,11... | collective-permute-start | bytes 786440 | tf_op jit(solution)/shard_map/ppermute | solution.py:34
  10.3 13.2 %collective-permute-start.3 = (bf16[128,1024]{1,0:T(8,128)(2,1)S(1)}, bf16[128,1024]{1,0:T(8,128)(2,1)S(1)}, u32[]{:S(2)}, u32[]{:S(2)}) collective-permute-start(bf16[128,1024]{1,0:T(8,128)(2,1)S(1)} %collective-permute-done.2.rec_ref), channel_id=1, source_target_pairs={{0,2},{1,63},{2,4},{3,1},{4,6},{5,3},{6,8},{7,5},{8,10},{9,7},{10,... | collective-permute-start | bytes 786440 | tf_op jit(solution)/shard_map/ppermute | solution.py:34
  16.0 14.2 %collective-permute-start.1 = (bf16[128,1024]{1,0:T(8,128)(2,1)S(1)}, bf16[128,1024]{1,0:T(8,128)(2,1)S(1)}, u32[]{:S(2)}, u32[]{:S(2)}) collective-permute-start(bf16[128,1024]{1,0:T(8,128)(2,1)S(1)} %collective-permute-done.rec_ref), channel_id=1, source_target_pairs={{0,2},{1,63},{2,4},{3,1},{4,6},{5,3},{6,8},{7,5},{8,10},{9,7},{10,... | collective-permute-start | bytes 786440 | tf_op jit(solution)/shard_map/ppermute | solution.py:34
  18.6 1.6 %copy-start = (bf16[1024,1024]{1,0:T(8,128)(2,1)S(1)}, bf16[1024,1024]{1,0:T(8,128)(2,1)}, u32[]{:S(2)}) copy-start(bf16[1024,1024]{1,0:T(8,128)(2,1)} %refs_0_.1) | copy-start | bytes 6291460
  20.1 0.9 copy-start.1
  21.1 0.9 copy-start.2
  22.0 0.7 copy-start.3
  26.0 10.2 %collective-permute-start.5 = (bf16[100,512]{1,0:T(8,128)(2,1)S(1)}, bf16[100,512]{1,0:T(8,128)(2,1)S(1)}, u32[]{:S(2)}, u32[]{:S(2)}) collective-permute-start(bf16[100,512]{1,0:T(8,128)(2,1)S(1)} %get-tuple-element.43.refs_1_), channel_id=1, source_target_pairs={{0,128},{128,0},{1,129},{129,1},{2,130},{130,2},{3,131},{131,3},{4... | collective-permute-start | bytes 307208 | tf_op jit(solution)/shard_map/ppermute | solution.py:34
  32.6 4.2 %collective-permute-start.4 = (bf16[100,512]{1,0:T(8,128)(2,1)S(1)}, bf16[100,512]{1,0:T(8,128)(2,1)S(1)}, u32[]{:S(2)}, u32[]{:S(2)}) collective-permute-start(bf16[100,512]{1,0:T(8,128)(2,1)S(1)} %get-tuple-element.42.refs_0_), channel_id=1, source_target_pairs={{0,128},{128,0},{1,129},{129,1},{2,130},{130,2},{3,131},{131,3},{4... | collective-permute-start | bytes 307208 | tf_op jit(solution)/shard_map/ppermute | solution.py:34
  33.9 6.2 %collective-permute-start.7 = (bf16[100,512]{1,0:T(8,128)(2,1)S(1)}, bf16[100,512]{1,0:T(8,128)(2,1)S(1)}, u32[]{:S(2)}, u32[]{:S(2)}) collective-permute-start(bf16[100,512]{1,0:T(8,128)(2,1)S(1)} %get-tuple-element.43.refs_1_), channel_id=1, source_target_pairs={{0,64},{64,0},{1,65},{65,1},{2,66},{66,2},{3,67},{67,3},{4,68},{68... | collective-permute-start | bytes 307208 | tf_op jit(solution)/shard_map/ppermute | solution.py:34
  36.2 3.9 %collective-permute-start.6 = (bf16[100,512]{1,0:T(8,128)(2,1)S(1)}, bf16[100,512]{1,0:T(8,128)(2,1)S(1)}, u32[]{:S(2)}, u32[]{:S(2)}) collective-permute-start(bf16[100,512]{1,0:T(8,128)(2,1)S(1)} %get-tuple-element.42.refs_0_), channel_id=1, source_target_pairs={{0,64},{64,0},{1,65},{65,1},{2,66},{66,2},{3,67},{67,3},{4,68},{68... | collective-permute-start | bytes 307208 | tf_op jit(solution)/shard_map/ppermute | solution.py:34
  36.2 3.9 %collective-permute-start.9 = (bf16[100,512]{1,0:T(8,128)(2,1)S(1)}, bf16[100,512]{1,0:T(8,128)(2,1)S(1)}, u32[]{:S(2)}, u32[]{:S(2)}) collective-permute-start(bf16[100,512]{1,0:T(8,128)(2,1)S(1)} %collective-permute-done.5.refs_3_), channel_id=1, source_target_pairs={{0,64},{64,0},{1,65},{65,1},{2,66},{66,2},{3,67},{67,3},{4,68},{68... | collective-permute-start | bytes 307208 | tf_op jit(solution)/shard_map/ppermute | solution.py:34
  36.7 3.7 %collective-permute-start.8 = (bf16[100,512]{1,0:T(8,128)(2,1)S(1)}, bf16[100,512]{1,0:T(8,128)(2,1)S(1)}, u32[]{:S(2)}, u32[]{:S(2)}) collective-permute-start(bf16[100,512]{1,0:T(8,128)(2,1)S(1)} %collective-permute-done.4.refs_2_), channel_id=1, source_target_pairs={{0,64},{64,0},{1,65},{65,1},{2,66},{66,2},{3,67},{67,3},{4,68},{68... | collective-permute-start | bytes 307208 | tf_op jit(solution)/shard_map/ppermute | solution.py:34
  42.7 28.3 %collective-permute-start.10 = (bf16[32,2,16,512]{3,2,1,0:T(8,128)(2,1)S(1)}, bf16[32,2,16,512]{3,2,1,0:T(8,128)(2,1)S(1)}, u32[]{:S(2)}, u32[]{:S(2)}) collective-permute-start(bf16[32,2,16,512]{3,2,1,0:T(8,128)(2,1)S(1)} %get-tuple-element.48), channel_id=1, source_target_pairs={{0,64},{64,0},{1,65},{65,1},{2,66},{66,2},{3,67},{67,3},{4,68},{68... | collective-permute-start | bytes 3145736 | tf_op jit(solution)/shard_map/ppermute | solution.py:34
  48.0 8.9 %collective-permute-start.20 = (bf16[128,1024]{1,0:T(8,128)(2,1)S(1)}, bf16[128,1024]{1,0:T(8,128)(2,1)S(1)}, u32[]{:S(2)}, u32[]{:S(2)}) collective-permute-start(bf16[128,1024]{1,0:T(8,128)(2,1)S(1)} %get-tuple-element.66), channel_id=1, source_target_pairs={{0,62},{1,3},{2,0},{3,5},{4,2},{5,7},{6,4},{7,9},{8,6},{9,11},{10,... | collective-permute-start | bytes 786440 | tf_op jit(solution)/shard_map/ppermute | solution.py:34
  54.5 8.0 %collective-permute-start.21 = (bf16[128,1024]{1,0:T(8,128)(2,1)S(1)}, bf16[128,1024]{1,0:T(8,128)(2,1)S(1)}, u32[]{:S(2)}, u32[]{:S(2)}) collective-permute-start(bf16[128,1024]{1,0:T(8,128)(2,1)S(1)} %get-tuple-element.67), channel_id=1, source_target_pairs={{0,62},{1,3},{2,0},{3,5},{4,2},{5,7},{6,4},{7,9},{8,6},{9,11},{10,... | collective-permute-start | bytes 786440 | tf_op jit(solution)/shard_map/ppermute | solution.py:34
  62.6 51.2 %collective-permute-start.22 = (bf16[2,128,1024]{2,1,0:T(8,128)(2,1)S(1)}, bf16[2,128,1024]{2,1,0:T(8,128)(2,1)S(1)}, u32[]{:S(2)}, u32[]{:S(2)}) collective-permute-start(bf16[2,128,1024]{2,1,0:T(8,128)(2,1)S(1)} %shard_map.89), channel_id=1, source_target_pairs={{0,1},{1,0},{2,3},{3,2},{4,5},{5,4},{6,7},{7,6},{8,9},{9,8},{10,11... | collective-permute-start | bytes 1572872 | tf_op jit(solution)/shard_map/ppermute | solution.py:34
  71.2 16.3 %collective-permute-start.11 = (bf16[32,16,256]{2,1,0:T(8,128)(2,1)S(1)}, bf16[32,16,256]{2,1,0:T(8,128)(2,1)S(1)}, u32[]{:S(2)}, u32[]{:S(2)}) collective-permute-start(bf16[32,16,256]{2,1,0:T(8,128)(2,1)S(1)} %get-tuple-element.50), channel_id=1, source_target_pairs={{0,128},{128,0},{1,129},{129,1},{2,130},{130,2},{3,131},{131,3},{4... | collective-permute-start | bytes 786440 | tf_op jit(solution)/shard_map/ppermute | solution.py:34
  71.3 22.2 %collective-permute-start.12 = (bf16[32,16,256]{2,1,0:T(8,128)(2,1)S(1)}, bf16[32,16,256]{2,1,0:T(8,128)(2,1)S(1)}, u32[]{:S(2)}, u32[]{:S(2)}) collective-permute-start(bf16[32,16,256]{2,1,0:T(8,128)(2,1)S(1)} %get-tuple-element.51), channel_id=1, source_target_pairs={{0,1},{1,0},{2,3},{3,2},{4,5},{5,4},{6,7},{7,6},{8,9},{9,8},{10,11... | collective-permute-start | bytes 786440 | tf_op jit(solution)/shard_map/ppermute | solution.py:34
  71.9 21.6 %collective-permute-start.13 = (bf16[32,16,256]{2,1,0:T(8,128)(2,1)S(1)}, bf16[32,16,256]{2,1,0:T(8,128)(2,1)S(1)}, u32[]{:S(2)}, u32[]{:S(2)}) collective-permute-start(bf16[32,16,256]{2,1,0:T(8,128)(2,1)S(1)} %get-tuple-element.52), channel_id=1, source_target_pairs={{0,129},{1,128},{128,1},{129,0},{2,131},{3,130},{130,3},{131,2},{4... | collective-permute-start | bytes 786440 | tf_op jit(solution)/shard_map/ppermute | solution.py:34
  93.7 4.8 %collective-permute-start.14 = (bf16[8,16,256]{2,1,0:T(8,128)(2,1)S(1)}, bf16[8,16,256]{2,1,0:T(8,128)(2,1)S(1)}, u32[]{:S(2)}, u32[]{:S(2)}) collective-permute-start(bf16[8,16,256]{2,1,0:T(8,128)(2,1)S(1)} %get-tuple-element.54), channel_id=1, source_target_pairs={{0,32},{16,48},{32,0},{48,16},{1,33},{17,49},{33,1},{49,17},{2,34}... | collective-permute-start | bytes 196616 | tf_op jit(solution)/shard_map/ppermute | solution.py:34
  93.8 5.1 %collective-permute-start.15 = (bf16[8,16,256]{2,1,0:T(8,128)(2,1)S(1)}, bf16[8,16,256]{2,1,0:T(8,128)(2,1)S(1)}, u32[]{:S(2)}, u32[]{:S(2)}) collective-permute-start(bf16[8,16,256]{2,1,0:T(8,128)(2,1)S(1)} %get-tuple-element.55), channel_id=1, source_target_pairs={{0,16},{16,32},{32,48},{48,0},{1,17},{17,33},{33,49},{49,1},{2,18}... | collective-permute-start | bytes 196616 | tf_op jit(solution)/shard_map/ppermute | solution.py:34
  93.8 5.0 %collective-permute-start.16 = (bf16[8,16,256]{2,1,0:T(8,128)(2,1)S(1)}, bf16[8,16,256]{2,1,0:T(8,128)(2,1)S(1)}, u32[]{:S(2)}, u32[]{:S(2)}) collective-permute-start(bf16[8,16,256]{2,1,0:T(8,128)(2,1)S(1)} %get-tuple-element.56), channel_id=1, source_target_pairs={{0,48},{16,0},{32,16},{48,32},{1,49},{17,1},{33,17},{49,33},{2,50}... | collective-permute-start | bytes 196616 | tf_op jit(solution)/shard_map/ppermute | solution.py:34
  108.6 6.1 %collective-permute-start.19 = (bf16[16,256]{1,0:T(8,128)(2,1)S(1)}, bf16[16,256]{1,0:T(8,128)(2,1)S(1)}, u32[]{:S(2)}, u32[]{:S(2)}) collective-permute-start(bf16[16,256]{1,0:T(8,128)(2,1)S(1)} %shard_map.85.mine_ref), channel_id=1, source_target_pairs={{0,192},{64,128},{128,64},{192,0},{1,193},{65,129},{129,65},{193,1... | collective-permute-start | bytes 24584 | tf_op jit(solution)/shard_map/ppermute | solution.py:34
  112.3 2.4 %collective-permute-start.18 = (bf16[16,256]{1,0:T(8,128)(2,1)S(1)}, bf16[16,256]{1,0:T(8,128)(2,1)S(1)}, u32[]{:S(2)}, u32[]{:S(2)}) collective-permute-start(bf16[16,256]{1,0:T(8,128)(2,1)S(1)} %shard_map.85.mine_ref), channel_id=1, source_target_pairs={{0,64},{64,0},{1,65},{65,1},{2,66},{66,2},{3,67},{67,3},{4,68},{68... | collective-permute-start | bytes 24584 | tf_op jit(solution)/shard_map/ppermute | solution.py:34
  112.6 2.6 %collective-permute-start.17 = (bf16[16,256]{1,0:T(8,128)(2,1)S(1)}, bf16[16,256]{1,0:T(8,128)(2,1)S(1)}, u32[]{:S(2)}, u32[]{:S(2)}) collective-permute-start(bf16[16,256]{1,0:T(8,128)(2,1)S(1)} %shard_map.85.mine_ref), channel_id=1, source_target_pairs={{0,128},{128,0},{1,129},{129,1},{2,130},{130,2},{3,131},{131,3},{4... | collective-permute-start | bytes 24584 | tf_op jit(solution)/shard_map/ppermute | solution.py:34

commit v5 on v4

--- a/solution.py
+++ b/solution.py
@@ -223,8 +223,8 @@
     c = lax.axis_index("c")
     give = pl.ds(pl.multiple_of((1 - c) * half, half), half)
     keep = pl.ds(pl.multiple_of(c * half, half), half)
-    for n in range(0, w_ref.shape[0], chunk):
-        rows = slice(n, n + chunk)
+    for n in range(0, w_ref.shape[0], 2 * chunk):
+        rows = slice(n, n + 2 * chunk)
         darea = dot(give_ref[...], w_ref[rows, give], 1, 1) + dot(keep_ref[...], w_ref[rows, keep], 1, 1)
         dext = dot(flipped_ref[...], darea.astype(BF16))
         own_ref[:, rows] = dext[:width]
@@ -277,7 +277,8 @@
     part = ((n_y * n_z, out_rows, half // 2), BF16)
     mine, *give = call(cores_kernel, [(part[0], F32)] + [part] * 3, keep, got)
     got = []
-    for axes, g in zip((("xl",), ("xh",), ("xl", "xh")), give):
+    give = (give[1], give[0], give[2])
+    for axes, g in zip((("xh",), ("xl",), ("xl", "xh")), give):
         got.append(permute(g, axes, lambda *at: tuple(1 - i for i in at)))
     part = ((n_z, out_rows, half // 2), BF16)
     mine, *give = call(cut_kernel, [(part[0], F32)] + [part] * (n_y - 1), mine, *got)
@@ -299,10 +300,11 @@
     far = shifted(far, "xh", 1)
     rows = lax.all_to_all(rows, "z", 0, 0)
     (mine,) = call(sum_kernel, [((out_rows, half // 2), BF16)], rows)
+    quarters = []
+    for axes in (("xl",), ("c",), MEMBER):
+        quarters.append(permute(mine, axes, lambda *at: tuple(1 - i for i in at)))
     (grad_hidden,) = call(
-        place_kernel, [((out_rows, wide), F32)],
-        mine, shifted(mine, "xl", 1), shifted(mine, "c", 1),
-        permute(mine, MEMBER, lambda a, b: (1 - a, 1 - b)), final=True,
+        place_kernel, [((out_rows, wide), F32)], mine, *quarters, final=True
     )
     (grad_mesh,) = call(
         nodes_kernel, [((members, width, wide), BF16)], *[b[0] for b in back], far, final=True

time: 117 us -> 116 us (level)
  waiting for transfers between devices: 38.4 us -> 43.4 us
  Pallas kernels: 17.8 us -> 15.3 us
  starting transfers between devices: 43.3 us -> 40.8 us
    ppermute x23, waiting for transfers between devices: 38.4 us -> 43.4 us  [permute(): return lax.ppermute(value, axes if len(axes) > 1 else axes[0], pairs)]
    pallas_call x13, Pallas kernels: 16.9 us -> 14.4 us  [call(): pl.pallas_call(kernel, out_shape=[jax.ShapeDtypeStruct(*s) if final else...]
    ppermute x23, starting transfers between devices: 43.3 us -> 40.8 us  [permute(): return lax.ppermute(value, axes if len(axes) > 1 else axes[0], pairs)]
  transfers between devices with their start and end apart: 23 -> 23, of which waited for: 11 -> 12; matrix products, arithmetic and copies ran while one was open for 0% -> 0% of each run, Pallas kernels for 13% -> 11%
where the time goes in v5:
time: 116 us
  waiting for transfers between devices  43.4 us (37%)
  starting transfers between devices  40.8 us (35%)
  Pallas kernels  15.3 us (13%)
  blocking collectives  9.6 us (8%)
  local copies, waits for them, and re-layouts  5.18 us (4%)
  between operations  1.43 us (1%)
    ppermute x23, waiting for transfers between devices, permute(): return lax.ppermute(value, axes if len(axes) > 1 else axes[0], pairs)  43.4 us
    ppermute x23, starting transfers between devices, permute(): return lax.ppermute(value, axes if len(axes) > 1 else axes[0], pairs)  40.8 us
    pallas_call x13, Pallas kernels, call(): pl.pallas_call(kernel, out_shape=[jax.ShapeDtypeStruct(*s) if final else...  14.4 us
    all_to_all x1, blocking collectives, step(): rows = lax.all_to_all(rows, 'z', 0, 0)  9.6 us
    unnamed x8, local copies, waits for them, and re-layouts  4.11 us
  transfers between devices with their start and end apart: 23, of which 12 were waited for; matrix products, arithmetic and copies ran while one was open for 0% of the time, Pallas kernels for 11%

profile of v5, /device:TPU:1, one launch (start us, length us, event | category | flops | bytes accessed | tf_op | source)
XLA Modules:
  0.0 115.7 jit_solution(15503637844882816349)
XLA Ops:
  1.7 3.6 %collective-permute-start.2 = (bf16[128,1024]{1,0:T(8,128)(2,1)S(1)}, bf16[128,1024]{1,0:T(8,128)(2,1)S(1)}, u32[]{:S(2)}, u32[]{:S(2)}) collective-permute-start(bf16[128,1024]{1,0:T(8,128)(2,1)S(1)} %get-tuple-element.68.own_ref), channel_id=1, source_target_pairs={{0,1},{1,0},{2,3},{3,2},{4,5},{5,4},{6,7},{7,6},{8,9},{9,8},{10,11... | collective-permute-start | bytes 786440 | tf_op jit(solution)/shard_map/ppermute | solution.py:34
  5.4 4.9 %collective-permute-done.2.rec_ref = bf16[128,1024]{1,0:T(8,128)(2,1)S(1)} collective-permute-done((bf16[128,1024]{1,0:T(8,128)(2,1)S(1)}, bf16[128,1024]{1,0:T(8,128)(2,1)S(1)}, u32[]{:S(2)}, u32[]{:S(2)}) %collective-permute-start.2) | collective-permute-done | bytes 262176 | tf_op jit(solution)/shard_map/ppermute | solution.py:34
  10.3 2.6 %collective-permute-start.3 = (bf16[128,1024]{1,0:T(8,128)(2,1)S(1)}, bf16[128,1024]{1,0:T(8,128)(2,1)S(1)}, u32[]{:S(2)}, u32[]{:S(2)}) collective-permute-start(bf16[128,1024]{1,0:T(8,128)(2,1)S(1)} %collective-permute-done.2.rec_ref), channel_id=1, source_target_pairs={{0,2},{1,63},{2,4},{3,1},{4,6},{5,3},{6,8},{7,5},{8,10},{9,7},{10,... | collective-permute-start | bytes 786440 | tf_op jit(solution)/shard_map/ppermute | solution.py:34
  12.9 3.0 %collective-permute-done.rec_ref = bf16[128,1024]{1,0:T(8,128)(2,1)S(1)} collective-permute-done((bf16[128,1024]{1,0:T(8,128)(2,1)S(1)}, bf16[128,1024]{1,0:T(8,128)(2,1)S(1)}, u32[]{:S(2)}, u32[]{:S(2)}) %collective-permute-start) | collective-permute-done | bytes 262176 | tf_op jit(solution)/shard_map/ppermute | solution.py:34
  16.0 2.6 %collective-permute-start.1 = (bf16[128,1024]{1,0:T(8,128)(2,1)S(1)}, bf16[128,1024]{1,0:T(8,128)(2,1)S(1)}, u32[]{:S(2)}, u32[]{:S(2)}) collective-permute-start(bf16[128,1024]{1,0:T(8,128)(2,1)S(1)} %collective-permute-done.rec_ref), channel_id=1, source_target_pairs={{0,2},{1,63},{2,4},{3,1},{4,6},{5,3},{6,8},{7,5},{8,10},{9,7},{10,... | collective-permute-start | bytes 786440 | tf_op jit(solution)/shard_map/ppermute | solution.py:34
  18.6 1.6 %copy-done = bf16[1024,1024]{1,0:T(8,128)(2,1)S(1)} copy-done((bf16[1024,1024]{1,0:T(8,128)(2,1)S(1)}, bf16[1024,1024]{1,0:T(8,128)(2,1)}, u32[]{:S(2)}) %copy-start) | copy-done | bytes 2097176
  23.6 2.4 %shard_map.79 = (bf16[1024,512]{1,0:T(8,128)(2,1)S(1)}, bf16[512,1024]{1,0:T(8,128)(2,1)S(1)}, bf16[100,512]{1,0:T(8,128)(2,1)S(1)}) custom-call(bf16[512,384]{1,0:T(8,128)(2,1)S(1)} %get-tuple-element.36.counts_ref, bf16[128,1024]{1,0:T(8,128)(2,1)S(1)} %get-tuple-element.68.own_ref, bf16[128,1024]{1,0:T(8,128)(2,1)S(1)} %collective-permute-done.2.rec_ref, ...), custom_call_target="tpu_custom_call" | custom-call | tf_op jit(solution)/shard_map/pallas_call | solution.py:53
  26.0 1.3 %collective-permute-start.5 = (bf16[100,512]{1,0:T(8,128)(2,1)S(1)}, bf16[100,512]{1,0:T(8,128)(2,1)S(1)}, u32[]{:S(2)}, u32[]{:S(2)}) collective-permute-start(bf16[100,512]{1,0:T(8,128)(2,1)S(1)} %get-tuple-element.43.refs_1_), channel_id=1, source_target_pairs={{0,128},{128,0},{1,129},{129,1},{2,130},{130,2},{3,131},{131,3},{4... | collective-permute-start | bytes 307208 | tf_op jit(solution)/shard_map/ppermute | solution.py:34
  27.3 2.8 %collective-permute-done.1.fwd_ref = bf16[128,1024]{1,0:T(8,128)(2,1)S(1)} collective-permute-done((bf16[128,1024]{1,0:T(8,128)(2,1)S(1)}, bf16[128,1024]{1,0:T(8,128)(2,1)S(1)}, u32[]{:S(2)}, u32[]{:S(2)}) %collective-permute-start.1) | collective-permute-done | bytes 262176 | tf_op jit(solution)/shard_map/ppermute | solution.py:34
  30.2 2.4 %shard_map.78 = (bf16[1024,512]{1,0:T(8,128)(2,1)S(1)}, bf16[512,1024]{1,0:T(8,128)(2,1)S(1)}, bf16[100,512]{1,0:T(8,128)(2,1)S(1)}) custom-call(bf16[512,384]{1,0:T(8,128)(2,1)S(1)} %get-tuple-element.36.counts_ref, bf16[128,1024]{1,0:T(8,128)(2,1)S(1)} %get-tuple-element.69.own_ref, bf16[128,1024]{1,0:T(8,128)(2,1)S(1)} %collective-permute-done.rec_ref, ...), custom_call_target="tpu_custom_call" | custom-call | tf_op jit(solution)/shard_map/pallas_call | solution.py:53
  32.6 1.3 %collective-permute-start.4 = (bf16[100,512]{1,0:T(8,128)(2,1)S(1)}, bf16[100,512]{1,0:T(8,128)(2,1)S(1)}, u32[]{:S(2)}, u32[]{:S(2)}) collective-permute-start(bf16[100,512]{1,0:T(8,128)(2,1)S(1)} %get-tuple-element.42.refs_0_), channel_id=1, source_target_pairs={{0,128},{128,0},{1,129},{129,1},{2,130},{130,2},{3,131},{131,3},{4... | collective-permute-start | bytes 307208 | tf_op jit(solution)/shard_map/ppermute | solution.py:34
  33.9 2.4 %collective-permute-start.7 = (bf16[100,512]{1,0:T(8,128)(2,1)S(1)}, bf16[100,512]{1,0:T(8,128)(2,1)S(1)}, u32[]{:S(2)}, u32[]{:S(2)}) collective-permute-start(bf16[100,512]{1,0:T(8,128)(2,1)S(1)} %get-tuple-element.43.refs_1_), channel_id=1, source_target_pairs={{0,64},{64,0},{1,65},{65,1},{2,66},{66,2},{3,67},{67,3},{4,68},{68... | collective-permute-start | bytes 307208 | tf_op jit(solution)/shard_map/ppermute | solution.py:34
  36.7 2.7 %collective-permute-start.8 = (bf16[100,512]{1,0:T(8,128)(2,1)S(1)}, bf16[100,512]{1,0:T(8,128)(2,1)S(1)}, u32[]{:S(2)}, u32[]{:S(2)}) collective-permute-start(bf16[100,512]{1,0:T(8,128)(2,1)S(1)} %collective-permute-done.4.refs_2_), channel_id=1, source_target_pairs={{0,64},{64,0},{1,65},{65,1},{2,66},{66,2},{3,67},{67,3},{4,68},{68... | collective-permute-start | bytes 307208 | tf_op jit(solution)/shard_map/ppermute | solution.py:34
  40.4 2.3 %shard_map.80 = (bf16[100,512]{1,0:T(8,128)(2,1)S(1)}, bf16[100,512]{1,0:T(8,128)(2,1)S(1)}, bf16[512,512]{1,0:T(8,128)(2,1)S(1)}, bf16[512,512]{1,0:T(8,128)(2,1)S(1)}, bf16[32,2,16,512]{3,2,1,0:T(8,128)(2,1)S(1)}) custom-call(s32[1]{0:T(128)S(6)} %copy.8.len_ref, bf16[100,512]{1,0:T(8,128)(2,1)S(1)} %get-tuple-element.42.refs_0_, ...), custom_call_target="tpu_custom_call" | custom-call | tf_op jit(solution)/shard_map/pallas_call | solution.py:53
  43.3 1.6 %shard_map.81 = (bf16[512,512]{1,0:T(8,128)(2,1)S(1)}, bf16[512,512]{1,0:T(8,128)(2,1)S(1)}, bf16[32,2,16,512]{3,2,1,0:T(8,128)(2,1)S(1)}) custom-call(bf16[100,1024]{1,0:T(8,128)(2,1)S(1)} %get-tuple-element.35.wo_ref.refs_9_, bf16[1024,512]{1,0:T(8,128)(2,1)S(1)} %get-tuple-element.38.refs_10_.t0, bf16[1024,512]{1,0:T(8,128)(2,1)S(1)} %get-tuple-element.39.refs_11_.t1, ...), custom_call_target="tpu_custom_call" | custom-call | tf_op jit(solution)/shard_map/pallas_call | solution.py:53
  44.9 1.8 %shard_map.87 = (f32[128,1024]{1,0:T(8,128)S(1)}, f32[128,1024]{1,0:T(8,128)S(1)}, bf16[128,1024]{1,0:T(8,128)(2,1)S(1)}) custom-call(bf16[384,512]{1,0:T(8,128)(2,1)S(1)} %get-tuple-element.57.flipped_ref, bf16[1024,1024]{1,0:T(8,128)(2,1)S(1)} %get-tuple-element.37.w_ref, bf16[512,512]{1,0:T(8,128)(2,1)S(1)} %get-tuple-element.58.give_ref, ...), custom_call_target="tpu_custom_call" | custom-call | tf_op jit(solution)/shard_map/pallas_call | solution.py:53
  46.8 3.4 %collective-permute-start.20 = (bf16[128,1024]{1,0:T(8,128)(2,1)S(1)}, bf16[128,1024]{1,0:T(8,128)(2,1)S(1)}, u32[]{:S(2)}, u32[]{:S(2)}) collective-permute-start(bf16[128,1024]{1,0:T(8,128)(2,1)S(1)} %get-tuple-element.66), channel_id=1, source_target_pairs={{0,62},{1,3},{2,0},{3,5},{4,2},{5,7},{6,4},{7,9},{8,6},{9,11},{10,... | collective-permute-start | bytes 786440 | tf_op jit(solution)/shard_map/ppermute | solution.py:34
  50.1 1.8 %shard_map.88 = (f32[128,1024]{1,0:T(8,128)S(1)}, f32[128,1024]{1,0:T(8,128)S(1)}, bf16[128,1024]{1,0:T(8,128)(2,1)S(1)}) custom-call(bf16[384,512]{1,0:T(8,128)(2,1)S(1)} %get-tuple-element.57.flipped_ref, bf16[1024,1024]{1,0:T(8,128)(2,1)S(1)} %get-tuple-element.37.w_ref, bf16[512,512]{1,0:T(8,128)(2,1)S(1)} %get-tuple-element.61.give_ref, ...), custom_call_target="tpu_custom_call" | custom-call | tf_op jit(solution)/shard_map/pallas_call | solution.py:53
  51.9 1.8 %collective-permute-start.21 = (bf16[128,1024]{1,0:T(8,128)(2,1)S(1)}, bf16[128,1024]{1,0:T(8,128)(2,1)S(1)}, u32[]{:S(2)}, u32[]{:S(2)}) collective-permute-start(bf16[128,1024]{1,0:T(8,128)(2,1)S(1)} %get-tuple-element.67), channel_id=1, source_target_pairs={{0,62},{1,3},{2,0},{3,5},{4,2},{5,7},{6,4},{7,9},{8,6},{9,11},{10,... | collective-permute-start | bytes 786440 | tf_op jit(solution)/shard_map/ppermute | solution.py:34
  53.8 1.8 %collective-permute-done.20.far0_ref = bf16[128,1024]{1,0:T(8,128)(2,1)S(1)} collective-permute-done((bf16[128,1024]{1,0:T(8,128)(2,1)S(1)}, bf16[128,1024]{1,0:T(8,128)(2,1)S(1)}, u32[]{:S(2)}, u32[]{:S(2)}) %collective-permute-start.20) | collective-permute-done | bytes 262176 | tf_op jit(solution)/shard_map/ppermute | solution.py:34
  55.6 5.6 %collective-permute-done.21.far1_ref = bf16[128,1024]{1,0:T(8,128)(2,1)S(1)} collective-permute-done((bf16[128,1024]{1,0:T(8,128)(2,1)S(1)}, bf16[128,1024]{1,0:T(8,128)(2,1)S(1)}, u32[]{:S(2)}, u32[]{:S(2)}) %collective-permute-start.21) | collective-permute-done | bytes 262176 | tf_op jit(solution)/shard_map/ppermute | solution.py:34
  61.3 8.4 %collective-permute-start.22 = (bf16[2,128,1024]{2,1,0:T(8,128)(2,1)S(1)}, bf16[2,128,1024]{2,1,0:T(8,128)(2,1)S(1)}, u32[]{:S(2)}, u32[]{:S(2)}) collective-permute-start(bf16[2,128,1024]{2,1,0:T(8,128)(2,1)S(1)} %shard_map.89), channel_id=1, source_target_pairs={{0,1},{1,0},{2,3},{3,2},{4,5},{5,4},{6,7},{7,6},{8,9},{9,8},{10,11... | collective-permute-start | bytes 1572872 | tf_op jit(solution)/shard_map/ppermute | solution.py:34
  70.2 3.1 %collective-permute-start.13 = (bf16[32,16,256]{2,1,0:T(8,128)(2,1)S(1)}, bf16[32,16,256]{2,1,0:T(8,128)(2,1)S(1)}, u32[]{:S(2)}, u32[]{:S(2)}) collective-permute-start(bf16[32,16,256]{2,1,0:T(8,128)(2,1)S(1)} %get-tuple-element.52), channel_id=1, source_target_pairs={{0,129},{1,128},{128,1},{129,0},{2,131},{3,130},{130,3},{131,2},{4... | collective-permute-start | bytes 786440 | tf_op jit(solution)/shard_map/ppermute | solution.py:34
  73.3 13.3 %collective-permute-done.11.second_ref = bf16[32,16,256]{2,1,0:T(8,128)(2,1)S(1)} collective-permute-done((bf16[32,16,256]{2,1,0:T(8,128)(2,1)S(1)}, bf16[32,16,256]{2,1,0:T(8,128)(2,1)S(1)}, u32[]{:S(2)}, u32[]{:S(2)}) %collective-permute-start.11) | collective-permute-done | bytes 262176 | tf_op jit(solution)/shard_map/ppermute | solution.py:34
  86.7 5.3 %collective-permute-done.12.third_ref = bf16[32,16,256]{2,1,0:T(8,128)(2,1)S(1)} collective-permute-done((bf16[32,16,256]{2,1,0:T(8,128)(2,1)S(1)}, bf16[32,16,256]{2,1,0:T(8,128)(2,1)S(1)}, u32[]{:S(2)}, u32[]{:S(2)}) %collective-permute-start.12) | collective-permute-done | bytes 262176 | tf_op jit(solution)/shard_map/ppermute | solution.py:34
  91.9 1.4 %collective-permute-done.13.fourth_ref = bf16[32,16,256]{2,1,0:T(8,128)(2,1)S(1)} collective-permute-done((bf16[32,16,256]{2,1,0:T(8,128)(2,1)S(1)}, bf16[32,16,256]{2,1,0:T(8,128)(2,1)S(1)}, u32[]{:S(2)}, u32[]{:S(2)}) %collective-permute-start.13) | collective-permute-done | bytes 262176 | tf_op jit(solution)/shard_map/ppermute | solution.py:34
  93.6 2.7 %collective-permute-start.16 = (bf16[8,16,256]{2,1,0:T(8,128)(2,1)S(1)}, bf16[8,16,256]{2,1,0:T(8,128)(2,1)S(1)}, u32[]{:S(2)}, u32[]{:S(2)}) collective-permute-start(bf16[8,16,256]{2,1,0:T(8,128)(2,1)S(1)} %get-tuple-element.56), channel_id=1, source_target_pairs={{0,48},{16,0},{32,16},{48,32},{1,49},{17,1},{33,17},{49,33},{2,50}... | collective-permute-start | bytes 196616 | tf_op jit(solution)/shard_map/ppermute | solution.py:34
  96.3 2.0 %collective-permute-done.14.refs_0_ = bf16[8,16,256]{2,1,0:T(8,128)(2,1)S(1)} collective-permute-done((bf16[8,16,256]{2,1,0:T(8,128)(2,1)S(1)}, bf16[8,16,256]{2,1,0:T(8,128)(2,1)S(1)}, u32[]{:S(2)}, u32[]{:S(2)}) %collective-permute-start.14) | collective-permute-done | bytes 65568 | tf_op jit(solution)/shard_map/ppermute | solution.py:34
  98.2 1.8 %collective-permute-done.15.refs_1_ = bf16[8,16,256]{2,1,0:T(8,128)(2,1)S(1)} collective-permute-done((bf16[8,16,256]{2,1,0:T(8,128)(2,1)S(1)}, bf16[8,16,256]{2,1,0:T(8,128)(2,1)S(1)}, u32[]{:S(2)}, u32[]{:S(2)}) %collective-permute-start.15) | collective-permute-done | bytes 65568 | tf_op jit(solution)/shard_map/ppermute | solution.py:34
  100.1 9.6 %all_to_all.5.parts_ref = bf16[8,16,256]{2,1,0:T(8,128)(2,1)S(1)} all-to-all(bf16[8,16,256]{2,1,0:T(8,128)(2,1)S(1)} %shard_map.84), channel_id=1, replica_groups=mesh['xl'=2,'c'=2,'y'=4,'z'=8,'xh'=2] {'z'}, dimensions={0} | all-to-all | bytes 131072 | tf_op jit(solution)/shard_map/all_to_all | solution.py:301
  109.7 2.9 %collective-permute-start.19 = (bf16[16,256]{1,0:T(8,128)(2,1)S(1)}, bf16[16,256]{1,0:T(8,128)(2,1)S(1)}, u32[]{:S(2)}, u32[]{:S(2)}) collective-permute-start(bf16[16,256]{1,0:T(8,128)(2,1)S(1)} %shard_map.85.mine_ref), channel_id=1, source_target_pairs={{0,192},{64,128},{128,64},{192,0},{1,193},{65,129},{129,65},{193,1... | collective-permute-start | bytes 24584 | tf_op jit(solution)/shard_map/ppermute | solution.py:34
  113.9 1.2 %collective-permute-done.17.x_ref = bf16[16,256]{1,0:T(8,128)(2,1)S(1)} collective-permute-done((bf16[16,256]{1,0:T(8,128)(2,1)S(1)}, bf16[16,256]{1,0:T(8,128)(2,1)S(1)}, u32[]{:S(2)}, u32[]{:S(2)}) %collective-permute-start.17) | collective-permute-done | bytes 8224 | tf_op jit(solution)/shard_map/ppermute | solution.py:34
  (38 shorter events, 8.9 us)
Async XLA Ops:
  1.7 8.6 %collective-permute-start.2 = (bf16[128,1024]{1,0:T(8,128)(2,1)S(1)}, bf16[128,1024]{1,0:T(8,128)(2,1)S(1)}, u32[]{:S(2)}, u32[]{:S(2)}) collective-permute-start(bf16[128,1024]{1,0:T(8,128)(2,1)S(1)} %get-tuple-element.68.own_ref), channel_id=1, source_target_pairs={{0,1},{1,0},{2,3},{3,2},{4,5},{5,4},{6,7},{7,6},{8,9},{9,8},{10,11... | collective-permute-start | bytes 786440 | tf_op jit(solution)/shard_map/ppermute | solution.py:34
  5.3 10.6 %collective-permute-start = (bf16[128,1024]{1,0:T(8,128)(2,1)S(1)}, bf16[128,1024]{1,0:T(8,128)(2,1)S(1)}, u32[]{:S(2)}, u32[]{:S(2)}) collective-permute-start(bf16[128,1024]{1,0:T(8,128)(2,1)S(1)} %get-tuple-element.69.own_ref), channel_id=1, source_target_pairs={{0,1},{1,0},{2,3},{3,2},{4,5},{5,4},{6,7},{7,6},{8,9},{9,8},{10,11... | collective-permute-start | bytes 786440 | tf_op jit(solution)/shard_map/ppermute | solution.py:34
  10.3 13.2 %collective-permute-start.3 = (bf16[128,1024]{1,0:T(8,128)(2,1)S(1)}, bf16[128,1024]{1,0:T(8,128)(2,1)S(1)}, u32[]{:S(2)}, u32[]{:S(2)}) collective-permute-start(bf16[128,1024]{1,0:T(8,128)(2,1)S(1)} %collective-permute-done.2.rec_ref), channel_id=1, source_target_pairs={{0,2},{1,63},{2,4},{3,1},{4,6},{5,3},{6,8},{7,5},{8,10},{9,7},{10,... | collective-permute-start | bytes 786440 | tf_op jit(solution)/shard_map/ppermute | solution.py:34
  16.0 14.2 %collective-permute-start.1 = (bf16[128,1024]{1,0:T(8,128)(2,1)S(1)}, bf16[128,1024]{1,0:T(8,128)(2,1)S(1)}, u32[]{:S(2)}, u32[]{:S(2)}) collective-permute-start(bf16[128,1024]{1,0:T(8,128)(2,1)S(1)} %collective-permute-done.rec_ref), channel_id=1, source_target_pairs={{0,2},{1,63},{2,4},{3,1},{4,6},{5,3},{6,8},{7,5},{8,10},{9,7},{10,... | collective-permute-start | bytes 786440 | tf_op jit(solution)/shard_map/ppermute | solution.py:34
  18.6 1.6 %copy-start = (bf16[1024,1024]{1,0:T(8,128)(2,1)S(1)}, bf16[1024,1024]{1,0:T(8,128)(2,1)}, u32[]{:S(2)}) copy-start(bf16[1024,1024]{1,0:T(8,128)(2,1)} %refs_0_.1) | copy-start | bytes 6291460
  20.1 0.9 copy-start.1
  21.1 0.9 copy-start.2
  22.0 0.7 copy-start.3
  26.0 10.2 %collective-permute-start.5 = (bf16[100,512]{1,0:T(8,128)(2,1)S(1)}, bf16[100,512]{1,0:T(8,128)(2,1)S(1)}, u32[]{:S(2)}, u32[]{:S(2)}) collective-permute-start(bf16[100,512]{1,0:T(8,128)(2,1)S(1)} %get-tuple-element.43.refs_1_), channel_id=1, source_target_pairs={{0,128},{128,0},{1,129},{129,1},{2,130},{130,2},{3,131},{131,3},{4... | collective-permute-start | bytes 307208 | tf_op jit(solution)/shard_map/ppermute | solution.py:34
  32.6 4.2 %collective-permute-start.4 = (bf16[100,512]{1,0:T(8,128)(2,1)S(1)}, bf16[100,512]{1,0:T(8,128)(2,1)S(1)}, u32[]{:S(2)}, u32[]{:S(2)}) collective-permute-start(bf16[100,512]{1,0:T(8,128)(2,1)S(1)} %get-tuple-element.42.refs_0_), channel_id=1, source_target_pairs={{0,128},{128,0},{1,129},{129,1},{2,130},{130,2},{3,131},{131,3},{4... | collective-permute-start | bytes 307208 | tf_op jit(solution)/shard_map/ppermute | solution.py:34
  33.9 6.2 %collective-permute-start.7 = (bf16[100,512]{1,0:T(8,128)(2,1)S(1)}, bf16[100,512]{1,0:T(8,128)(2,1)S(1)}, u32[]{:S(2)}, u32[]{:S(2)}) collective-permute-start(bf16[100,512]{1,0:T(8,128)(2,1)S(1)} %get-tuple-element.43.refs_1_), channel_id=1, source_target_pairs={{0,64},{64,0},{1,65},{65,1},{2,66},{66,2},{3,67},{67,3},{4,68},{68... | collective-permute-start | bytes 307208 | tf_op jit(solution)/shard_map/ppermute | solution.py:34
  36.2 3.9 %collective-permute-start.6 = (bf16[100,512]{1,0:T(8,128)(2,1)S(1)}, bf16[100,512]{1,0:T(8,128)(2,1)S(1)}, u32[]{:S(2)}, u32[]{:S(2)}) collective-permute-start(bf16[100,512]{1,0:T(8,128)(2,1)S(1)} %get-tuple-element.42.refs_0_), channel_id=1, source_target_pairs={{0,64},{64,0},{1,65},{65,1},{2,66},{66,2},{3,67},{67,3},{4,68},{68... | collective-permute-start | bytes 307208 | tf_op jit(solution)/shard_map/ppermute | solution.py:34
  36.2 3.9 %collective-permute-start.9 = (bf16[100,512]{1,0:T(8,128)(2,1)S(1)}, bf16[100,512]{1,0:T(8,128)(2,1)S(1)}, u32[]{:S(2)}, u32[]{:S(2)}) collective-permute-start(bf16[100,512]{1,0:T(8,128)(2,1)S(1)} %collective-permute-done.5.refs_3_), channel_id=1, source_target_pairs={{0,64},{64,0},{1,65},{65,1},{2,66},{66,2},{3,67},{67,3},{4,68},{68... | collective-permute-start | bytes 307208 | tf_op jit(solution)/shard_map/ppermute | solution.py:34
  36.7 3.7 %collective-permute-start.8 = (bf16[100,512]{1,0:T(8,128)(2,1)S(1)}, bf16[100,512]{1,0:T(8,128)(2,1)S(1)}, u32[]{:S(2)}, u32[]{:S(2)}) collective-permute-start(bf16[100,512]{1,0:T(8,128)(2,1)S(1)} %collective-permute-done.4.refs_2_), channel_id=1, source_target_pairs={{0,64},{64,0},{1,65},{65,1},{2,66},{66,2},{3,67},{67,3},{4,68},{68... | collective-permute-start | bytes 307208 | tf_op jit(solution)/shard_map/ppermute | solution.py:34
  42.7 27.0 %collective-permute-start.10 = (bf16[32,2,16,512]{3,2,1,0:T(8,128)(2,1)S(1)}, bf16[32,2,16,512]{3,2,1,0:T(8,128)(2,1)S(1)}, u32[]{:S(2)}, u32[]{:S(2)}) collective-permute-start(bf16[32,2,16,512]{3,2,1,0:T(8,128)(2,1)S(1)} %get-tuple-element.48), channel_id=1, source_target_pairs={{0,64},{64,0},{1,65},{65,1},{2,66},{66,2},{3,67},{67,3},{4,68},{68... | collective-permute-start | bytes 3145736 | tf_op jit(solution)/shard_map/ppermute | solution.py:34
  46.8 8.8 %collective-permute-start.20 = (bf16[128,1024]{1,0:T(8,128)(2,1)S(1)}, bf16[128,1024]{1,0:T(8,128)(2,1)S(1)}, u32[]{:S(2)}, u32[]{:S(2)}) collective-permute-start(bf16[128,1024]{1,0:T(8,128)(2,1)S(1)} %get-tuple-element.66), channel_id=1, source_target_pairs={{0,62},{1,3},{2,0},{3,5},{4,2},{5,7},{6,4},{7,9},{8,6},{9,11},{10,... | collective-permute-start | bytes 786440 | tf_op jit(solution)/shard_map/ppermute | solution.py:34
  51.9 9.3 %collective-permute-start.21 = (bf16[128,1024]{1,0:T(8,128)(2,1)S(1)}, bf16[128,1024]{1,0:T(8,128)(2,1)S(1)}, u32[]{:S(2)}, u32[]{:S(2)}) collective-permute-start(bf16[128,1024]{1,0:T(8,128)(2,1)S(1)} %get-tuple-element.67), channel_id=1, source_target_pairs={{0,62},{1,3},{2,0},{3,5},{4,2},{5,7},{6,4},{7,9},{8,6},{9,11},{10,... | collective-permute-start | bytes 786440 | tf_op jit(solution)/shard_map/ppermute | solution.py:34
  61.3 51.7 %collective-permute-start.22 = (bf16[2,128,1024]{2,1,0:T(8,128)(2,1)S(1)}, bf16[2,128,1024]{2,1,0:T(8,128)(2,1)S(1)}, u32[]{:S(2)}, u32[]{:S(2)}) collective-permute-start(bf16[2,128,1024]{2,1,0:T(8,128)(2,1)S(1)} %shard_map.89), channel_id=1, source_target_pairs={{0,1},{1,0},{2,3},{3,2},{4,5},{5,4},{6,7},{7,6},{8,9},{9,8},{10,11... | collective-permute-start | bytes 1572872 | tf_op jit(solution)/shard_map/ppermute | solution.py:34
  70.0 16.7 %collective-permute-start.11 = (bf16[32,16,256]{2,1,0:T(8,128)(2,1)S(1)}, bf16[32,16,256]{2,1,0:T(8,128)(2,1)S(1)}, u32[]{:S(2)}, u32[]{:S(2)}) collective-permute-start(bf16[32,16,256]{2,1,0:T(8,128)(2,1)S(1)} %get-tuple-element.50), channel_id=1, source_target_pairs={{0,1},{1,0},{2,3},{3,2},{4,5},{5,4},{6,7},{7,6},{8,9},{9,8},{10,11... | collective-permute-start | bytes 786440 | tf_op jit(solution)/shard_map/ppermute | solution.py:34
  70.1 21.8 %collective-permute-start.12 = (bf16[32,16,256]{2,1,0:T(8,128)(2,1)S(1)}, bf16[32,16,256]{2,1,0:T(8,128)(2,1)S(1)}, u32[]{:S(2)}, u32[]{:S(2)}) collective-permute-start(bf16[32,16,256]{2,1,0:T(8,128)(2,1)S(1)} %get-tuple-element.51), channel_id=1, source_target_pairs={{0,128},{128,0},{1,129},{129,1},{2,130},{130,2},{3,131},{131,3},{4... | collective-permute-start | bytes 786440 | tf_op jit(solution)/shard_map/ppermute | solution.py:34
  70.2 23.1 %collective-permute-start.13 = (bf16[32,16,256]{2,1,0:T(8,128)(2,1)S(1)}, bf16[32,16,256]{2,1,0:T(8,128)(2,1)S(1)}, u32[]{:S(2)}, u32[]{:S(2)}) collective-permute-start(bf16[32,16,256]{2,1,0:T(8,128)(2,1)S(1)} %get-tuple-element.52), channel_id=1, source_target_pairs={{0,129},{1,128},{128,1},{129,0},{2,131},{3,130},{130,3},{131,2},{4... | collective-permute-start | bytes 786440 | tf_op jit(solution)/shard_map/ppermute | solution.py:34
  93.4 4.8 %collective-permute-start.14 = (bf16[8,16,256]{2,1,0:T(8,128)(2,1)S(1)}, bf16[8,16,256]{2,1,0:T(8,128)(2,1)S(1)}, u32[]{:S(2)}, u32[]{:S(2)}) collective-permute-start(bf16[8,16,256]{2,1,0:T(8,128)(2,1)S(1)} %get-tuple-element.54), channel_id=1, source_target_pairs={{0,32},{16,48},{32,0},{48,16},{1,33},{17,49},{33,1},{49,17},{2,34}... | collective-permute-start | bytes 196616 | tf_op jit(solution)/shard_map/ppermute | solution.py:34
  93.5 6.5 %collective-permute-start.15 = (bf16[8,16,256]{2,1,0:T(8,128)(2,1)S(1)}, bf16[8,16,256]{2,1,0:T(8,128)(2,1)S(1)}, u32[]{:S(2)}, u32[]{:S(2)}) collective-permute-start(bf16[8,16,256]{2,1,0:T(8,128)(2,1)S(1)} %get-tuple-element.55), channel_id=1, source_target_pairs={{0,16},{16,32},{32,48},{48,0},{1,17},{17,33},{33,49},{49,1},{2,18}... | collective-permute-start | bytes 196616 | tf_op jit(solution)/shard_map/ppermute | solution.py:34
  93.6 6.4 %collective-permute-start.16 = (bf16[8,16,256]{2,1,0:T(8,128)(2,1)S(1)}, bf16[8,16,256]{2,1,0:T(8,128)(2,1)S(1)}, u32[]{:S(2)}, u32[]{:S(2)}) collective-permute-start(bf16[8,16,256]{2,1,0:T(8,128)(2,1)S(1)} %get-tuple-element.56), channel_id=1, source_target_pairs={{0,48},{16,0},{32,16},{48,32},{1,49},{17,1},{33,17},{49,33},{2,50}... | collective-permute-start | bytes 196616 | tf_op jit(solution)/shard_map/ppermute | solution.py:34
  109.7 4.2 %collective-permute-start.19 = (bf16[16,256]{1,0:T(8,128)(2,1)S(1)}, bf16[16,256]{1,0:T(8,128)(2,1)S(1)}, u32[]{:S(2)}, u32[]{:S(2)}) collective-permute-start(bf16[16,256]{1,0:T(8,128)(2,1)S(1)} %shard_map.85.mine_ref), channel_id=1, source_target_pairs={{0,192},{64,128},{128,64},{192,0},{1,193},{65,129},{129,65},{193,1... | collective-permute-start | bytes 24584 | tf_op jit(solution)/shard_map/ppermute | solution.py:34
  112.6 1.3 %collective-permute-start.18 = (bf16[16,256]{1,0:T(8,128)(2,1)S(1)}, bf16[16,256]{1,0:T(8,128)(2,1)S(1)}, u32[]{:S(2)}, u32[]{:S(2)}) collective-permute-start(bf16[16,256]{1,0:T(8,128)(2,1)S(1)} %shard_map.85.mine_ref), channel_id=1, source_target_pairs={{0,64},{64,0},{1,65},{65,1},{2,66},{66,2},{3,67},{67,3},{4,68},{68... | collective-permute-start | bytes 24584 | tf_op jit(solution)/shard_map/ppermute | solution.py:34
  112.6 2.5 %collective-permute-start.17 = (bf16[16,256]{1,0:T(8,128)(2,1)S(1)}, bf16[16,256]{1,0:T(8,128)(2,1)S(1)}, u32[]{:S(2)}, u32[]{:S(2)}) collective-permute-start(bf16[16,256]{1,0:T(8,128)(2,1)S(1)} %shard_map.85.mine_ref), channel_id=1, source_target_pairs={{0,128},{128,0},{1,129},{129,1},{2,130},{130,2},{3,131},{131,3},{4... | collective-permute-start | bytes 24584 | tf_op jit(solution)/shard_map/ppermute | solution.py:34

commit v6 on v5

--- a/solution.py
+++ b/solution.py
@@ -133,16 +133,30 @@
     out[...] = part.astype(out.dtype).reshape(out.shape)
 
 
+def early_kernel(own0_ref, own1_ref, *refs):
+    others, outs = refs[:-2], refs[-2:]
+    for r in range(0, own0_ref.shape[0], 16):
+        rows = slice(r, min(r + 16, own0_ref.shape[0]))
+        own = [own0_ref[rows].astype(F32), own1_ref[rows].astype(F32)]
+        mutual = smooth_sign(own[0] - own[1])
+        pairs = [mutual, -mutual]
+        for ref in others:
+            other = ref[rows].astype(F32)
+            pairs = [p + smooth_sign(v - other) for p, v in zip(pairs, own)]
+        for ref, p in zip(outs, pairs):
+            ref[rows] = p
+
+
 def give_kernel(total, len_ref, *refs):
-    preds, (target_ref, wo_ref, t0, t1, gate0, gate1, dp0, dp1, s0, s1, out) = refs[:8], refs[8:]
+    sums, refs = refs[:2], refs[2:]
+    preds, (target_ref, wo_ref, t0, t1, gate0, gate1, dp0, dp1, s0, s1, out) = refs[:5], refs[5:]
     channels, _ = target_ref.shape
     scale = (1.0 - fair_eps) / (total * (total - 1))
     for r in range(0, channels, 16):
         rows = slice(r, min(r + 16, channels))
         own = [preds[0][rows].astype(F32), preds[1][rows].astype(F32)]
         truth = target_ref[rows].astype(F32)
-        mutual = smooth_sign(own[0] - own[1])
-        pairs = [mutual, -mutual]
+        pairs = [ref[rows] for ref in sums]
         for ref in preds[2:]:
             other = ref[rows].astype(F32)
             pairs = [p + smooth_sign(v - other) for p, v in zip(pairs, own)]
@@ -262,7 +276,8 @@
         near.append(shifted(q, "xl", 1))
         mate.append(shifted(q, "c", 1))
         last.append(shifted(near[m], "c", 1))
-    others = near + mate + last
+    sums = call(early_kernel, [((channels, grid_rows), F32)] * 2, *pred, near[0], *mate)
+    others = [near[1]] + last
 
     slope = ((grid_rows, half), BF16)
     out_rows = wide // (n_y * n_z * n_x)
@@ -270,7 +285,7 @@
     dp = ((channels, grid_rows), BF16)
     dp0, dp1, g0, g1, give = call(
         functools.partial(give_kernel, total), [dp, dp, slope, slope, part],
-        lengths, *pred, *others, target, w_out, *area, *gate, scalars=1,
+        lengths, *sums, *pred, *others, target, w_out, *area, *gate, scalars=1,
     )
     got = shifted(give, "c", 1)
     k0, k1, keep = call(keep_kernel, [slope, slope, part], w_out, *area, *gate, dp0, dp1)

time: 116 us -> 116 us (level)
    pallas_call x13 -> x14, Pallas kernels: 14.4 us -> 14.4 us  [call(): pl.pallas_call(kernel, out_shape=[jax.ShapeDtypeStruct(*s) if final else...]
  transfers between devices with their start and end apart: 23 -> 23, of which waited for: 12 -> 11; matrix products, arithmetic and copies ran while one was open for 0% -> 0% of each run, Pallas kernels for 11% -> 11%
where the time goes in v6:
time: 116 us; the launch traced here: 115 us
  waiting for transfers between devices  43.1 us (37%)
  starting transfers between devices  40.6 us (35%)
  Pallas kernels  15.3 us (13%)
  blocking collectives  9.6 us (8%)
  local copies, waits for them, and re-layouts  5.18 us (4%)
  between operations  1.45 us (1%)
    ppermute x23, waiting for transfers between devices, permute(): return lax.ppermute(value, axes if len(axes) > 1 else axes[0], pairs)  43.1 us
    ppermute x23, starting transfers between devices, permute(): return lax.ppermute(value, axes if len(axes) > 1 else axes[0], pairs)  40.6 us
    pallas_call x14, Pallas kernels, call(): pl.pallas_call(kernel, out_shape=[jax.ShapeDtypeStruct(*s) if final else...  14.4 us
    all_to_all x1, blocking collectives, step(): rows = lax.all_to_all(rows, 'z', 0, 0)  9.6 us
    unnamed x8, local copies, waits for them, and re-layouts  4.11 us
  transfers between devices with their start and end apart: 23, of which 11 were waited for; matrix products, arithmetic and copies ran while one was open for 0% of the time, Pallas kernels for 11%

profile of v6, /device:TPU:1, one launch (start us, length us, event | category | flops | bytes accessed | tf_op | source)
XLA Modules:
  0.0 115.2 jit_solution(12468479474460472766)
XLA Ops:
  1.7 3.6 %collective-permute-start.2 = (bf16[128,1024]{1,0:T(8,128)(2,1)S(1)}, bf16[128,1024]{1,0:T(8,128)(2,1)S(1)}, u32[]{:S(2)}, u32[]{:S(2)}) collective-permute-start(bf16[128,1024]{1,0:T(8,128)(2,1)S(1)} %get-tuple-element.72.own_ref), channel_id=1, source_target_pairs={{0,1},{1,0},{2,3},{3,2},{4,5},{5,4},{6,7},{7,6},{8,9},{9,8},{10,11... | collective-permute-start | bytes 786440 | tf_op jit(solution)/shard_map/ppermute | solution.py:34
  5.4 4.9 %collective-permute-done.2.rec_ref = bf16[128,1024]{1,0:T(8,128)(2,1)S(1)} collective-permute-done((bf16[128,1024]{1,0:T(8,128)(2,1)S(1)}, bf16[128,1024]{1,0:T(8,128)(2,1)S(1)}, u32[]{:S(2)}, u32[]{:S(2)}) %collective-permute-start.2) | collective-permute-done | bytes 262176 | tf_op jit(solution)/shard_map/ppermute | solution.py:34
  10.3 2.6 %collective-permute-start.3 = (bf16[128,1024]{1,0:T(8,128)(2,1)S(1)}, bf16[128,1024]{1,0:T(8,128)(2,1)S(1)}, u32[]{:S(2)}, u32[]{:S(2)}) collective-permute-start(bf16[128,1024]{1,0:T(8,128)(2,1)S(1)} %collective-permute-done.2.rec_ref), channel_id=1, source_target_pairs={{0,2},{1,63},{2,4},{3,1},{4,6},{5,3},{6,8},{7,5},{8,10},{9,7},{10,... | collective-permute-start | bytes 786440 | tf_op jit(solution)/shard_map/ppermute | solution.py:34
  12.9 3.0 %collective-permute-done.rec_ref = bf16[128,1024]{1,0:T(8,128)(2,1)S(1)} collective-permute-done((bf16[128,1024]{1,0:T(8,128)(2,1)S(1)}, bf16[128,1024]{1,0:T(8,128)(2,1)S(1)}, u32[]{:S(2)}, u32[]{:S(2)}) %collective-permute-start) | collective-permute-done | bytes 262176 | tf_op jit(solution)/shard_map/ppermute | solution.py:34
  16.0 2.6 %collective-permute-start.1 = (bf16[128,1024]{1,0:T(8,128)(2,1)S(1)}, bf16[128,1024]{1,0:T(8,128)(2,1)S(1)}, u32[]{:S(2)}, u32[]{:S(2)}) collective-permute-start(bf16[128,1024]{1,0:T(8,128)(2,1)S(1)} %collective-permute-done.rec_ref), channel_id=1, source_target_pairs={{0,2},{1,63},{2,4},{3,1},{4,6},{5,3},{6,8},{7,5},{8,10},{9,7},{10,... | collective-permute-start | bytes 786440 | tf_op jit(solution)/shard_map/ppermute | solution.py:34
  18.6 1.6 %copy-done = bf16[1024,1024]{1,0:T(8,128)(2,1)S(1)} copy-done((bf16[1024,1024]{1,0:T(8,128)(2,1)S(1)}, bf16[1024,1024]{1,0:T(8,128)(2,1)}, u32[]{:S(2)}) %copy-start) | copy-done | bytes 2097176
  23.6 2.4 %shard_map.79 = (bf16[1024,512]{1,0:T(8,128)(2,1)S(1)}, bf16[512,1024]{1,0:T(8,128)(2,1)S(1)}, bf16[100,512]{1,0:T(8,128)(2,1)S(1)}) custom-call(bf16[512,384]{1,0:T(8,128)(2,1)S(1)} %get-tuple-element.38.counts_ref, bf16[128,1024]{1,0:T(8,128)(2,1)S(1)} %get-tuple-element.72.own_ref, bf16[128,1024]{1,0:T(8,128)(2,1)S(1)} %collective-permute-done.2.rec_ref, ...), custom_call_target="tpu_custom_call" | custom-call | tf_op jit(solution)/shard_map/pallas_call | solution.py:53
  26.0 1.3 %collective-permute-start.7 = (bf16[100,512]{1,0:T(8,128)(2,1)S(1)}, bf16[100,512]{1,0:T(8,128)(2,1)S(1)}, u32[]{:S(2)}, u32[]{:S(2)}) collective-permute-start(bf16[100,512]{1,0:T(8,128)(2,1)S(1)} %get-tuple-element.45.own1_ref.refs_3_), channel_id=1, source_target_pairs={{0,128},{128,0},{1,129},{129,1},{2,130},{130,2},{3,131},{131,3},{4... | collective-permute-start | bytes 307208 | tf_op jit(solution)/shard_map/ppermute | solution.py:34
  27.3 2.8 %collective-permute-done.1.fwd_ref = bf16[128,1024]{1,0:T(8,128)(2,1)S(1)} collective-permute-done((bf16[128,1024]{1,0:T(8,128)(2,1)S(1)}, bf16[128,1024]{1,0:T(8,128)(2,1)S(1)}, u32[]{:S(2)}, u32[]{:S(2)}) %collective-permute-start.1) | collective-permute-done | bytes 262176 | tf_op jit(solution)/shard_map/ppermute | solution.py:34
  30.2 2.4 %shard_map.78 = (bf16[1024,512]{1,0:T(8,128)(2,1)S(1)}, bf16[512,1024]{1,0:T(8,128)(2,1)S(1)}, bf16[100,512]{1,0:T(8,128)(2,1)S(1)}) custom-call(bf16[512,384]{1,0:T(8,128)(2,1)S(1)} %get-tuple-element.38.counts_ref, bf16[128,1024]{1,0:T(8,128)(2,1)S(1)} %get-tuple-element.73.own_ref, bf16[128,1024]{1,0:T(8,128)(2,1)S(1)} %collective-permute-done.rec_ref, ...), custom_call_target="tpu_custom_call" | custom-call | tf_op jit(solution)/shard_map/pallas_call | solution.py:53
  32.6 1.3 %collective-permute-start.4 = (bf16[100,512]{1,0:T(8,128)(2,1)S(1)}, bf16[100,512]{1,0:T(8,128)(2,1)S(1)}, u32[]{:S(2)}, u32[]{:S(2)}) collective-permute-start(bf16[100,512]{1,0:T(8,128)(2,1)S(1)} %get-tuple-element.44.own0_ref.refs_2_), channel_id=1, source_target_pairs={{0,128},{128,0},{1,129},{129,1},{2,130},{130,2},{3,131},{131,3},{4... | collective-permute-start | bytes 307208 | tf_op jit(solution)/shard_map/ppermute | solution.py:34
  33.9 2.4 %collective-permute-start.6 = (bf16[100,512]{1,0:T(8,128)(2,1)S(1)}, bf16[100,512]{1,0:T(8,128)(2,1)S(1)}, u32[]{:S(2)}, u32[]{:S(2)}) collective-permute-start(bf16[100,512]{1,0:T(8,128)(2,1)S(1)} %get-tuple-element.45.own1_ref.refs_3_), channel_id=1, source_target_pairs={{0,64},{64,0},{1,65},{65,1},{2,66},{66,2},{3,67},{67,3},{4,68},{68... | collective-permute-start | bytes 307208 | tf_op jit(solution)/shard_map/ppermute | solution.py:34
  36.7 2.7 %collective-permute-start.8 = (bf16[100,512]{1,0:T(8,128)(2,1)S(1)}, bf16[100,512]{1,0:T(8,128)(2,1)S(1)}, u32[]{:S(2)}, u32[]{:S(2)}) collective-permute-start(bf16[100,512]{1,0:T(8,128)(2,1)S(1)} %collective-permute-done.4.refs_0_), channel_id=1, source_target_pairs={{0,64},{64,0},{1,65},{65,1},{2,66},{66,2},{3,67},{67,3},{4,68},{68... | collective-permute-start | bytes 307208 | tf_op jit(solution)/shard_map/ppermute | solution.py:34
  40.5 1.9 %shard_map.81 = (bf16[100,512]{1,0:T(8,128)(2,1)S(1)}, bf16[100,512]{1,0:T(8,128)(2,1)S(1)}, bf16[512,512]{1,0:T(8,128)(2,1)S(1)}, bf16[512,512]{1,0:T(8,128)(2,1)S(1)}, bf16[32,2,16,512]{3,2,1,0:T(8,128)(2,1)S(1)}) custom-call(s32[1]{0:T(128)S(6)} %copy.8.len_ref, f32[100,512]{1,0:T(8,128)S(1)} %get-tuple-element.46.refs_0_, ...), custom_call_target="tpu_custom_call" | custom-call | tf_op jit(solution)/shard_map/pallas_call | solution.py:53
  43.0 1.6 %shard_map.82 = (bf16[512,512]{1,0:T(8,128)(2,1)S(1)}, bf16[512,512]{1,0:T(8,128)(2,1)S(1)}, bf16[32,2,16,512]{3,2,1,0:T(8,128)(2,1)S(1)}) custom-call(bf16[100,1024]{1,0:T(8,128)(2,1)S(1)} %get-tuple-element.37.wo_ref.refs_8_, bf16[1024,512]{1,0:T(8,128)(2,1)S(1)} %get-tuple-element.40.refs_9_.t0, bf16[1024,512]{1,0:T(8,128)(2,1)S(1)} %get-tuple-element.41.refs_10_.t1, ...), custom_call_target="tpu_custom_call" | custom-call | tf_op jit(solution)/shard_map/pallas_call | solution.py:53
  44.6 1.8 %shard_map.88 = (f32[128,1024]{1,0:T(8,128)S(1)}, f32[128,1024]{1,0:T(8,128)S(1)}, bf16[128,1024]{1,0:T(8,128)(2,1)S(1)}) custom-call(bf16[384,512]{1,0:T(8,128)(2,1)S(1)} %get-tuple-element.61.flipped_ref, bf16[1024,1024]{1,0:T(8,128)(2,1)S(1)} %get-tuple-element.39.w_ref, bf16[512,512]{1,0:T(8,128)(2,1)S(1)} %get-tuple-element.62.give_ref, ...), custom_call_target="tpu_custom_call" | custom-call | tf_op jit(solution)/shard_map/pallas_call | solution.py:53
  46.4 3.3 %collective-permute-start.20 = (bf16[128,1024]{1,0:T(8,128)(2,1)S(1)}, bf16[128,1024]{1,0:T(8,128)(2,1)S(1)}, u32[]{:S(2)}, u32[]{:S(2)}) collective-permute-start(bf16[128,1024]{1,0:T(8,128)(2,1)S(1)} %get-tuple-element.70), channel_id=1, source_target_pairs={{0,62},{1,3},{2,0},{3,5},{4,2},{5,7},{6,4},{7,9},{8,6},{9,11},{10,... | collective-permute-start | bytes 786440 | tf_op jit(solution)/shard_map/ppermute | solution.py:34
  49.8 1.8 %shard_map.89 = (f32[128,1024]{1,0:T(8,128)S(1)}, f32[128,1024]{1,0:T(8,128)S(1)}, bf16[128,1024]{1,0:T(8,128)(2,1)S(1)}) custom-call(bf16[384,512]{1,0:T(8,128)(2,1)S(1)} %get-tuple-element.61.flipped_ref, bf16[1024,1024]{1,0:T(8,128)(2,1)S(1)} %get-tuple-element.39.w_ref, bf16[512,512]{1,0:T(8,128)(2,1)S(1)} %get-tuple-element.65.give_ref, ...), custom_call_target="tpu_custom_call" | custom-call | tf_op jit(solution)/shard_map/pallas_call | solution.py:53
  51.6 1.8 %collective-permute-start.21 = (bf16[128,1024]{1,0:T(8,128)(2,1)S(1)}, bf16[128,1024]{1,0:T(8,128)(2,1)S(1)}, u32[]{:S(2)}, u32[]{:S(2)}) collective-permute-start(bf16[128,1024]{1,0:T(8,128)(2,1)S(1)} %get-tuple-element.71), channel_id=1, source_target_pairs={{0,62},{1,3},{2,0},{3,5},{4,2},{5,7},{6,4},{7,9},{8,6},{9,11},{10,... | collective-permute-start | bytes 786440 | tf_op jit(solution)/shard_map/ppermute | solution.py:34
  53.4 1.8 %collective-permute-done.20.far0_ref = bf16[128,1024]{1,0:T(8,128)(2,1)S(1)} collective-permute-done((bf16[128,1024]{1,0:T(8,128)(2,1)S(1)}, bf16[128,1024]{1,0:T(8,128)(2,1)S(1)}, u32[]{:S(2)}, u32[]{:S(2)}) %collective-permute-start.20) | collective-permute-done | bytes 262176 | tf_op jit(solution)/shard_map/ppermute | solution.py:34
  55.2 5.6 %collective-permute-done.21.far1_ref = bf16[128,1024]{1,0:T(8,128)(2,1)S(1)} collective-permute-done((bf16[128,1024]{1,0:T(8,128)(2,1)S(1)}, bf16[128,1024]{1,0:T(8,128)(2,1)S(1)}, u32[]{:S(2)}, u32[]{:S(2)}) %collective-permute-start.21) | collective-permute-done | bytes 262176 | tf_op jit(solution)/shard_map/ppermute | solution.py:34
  60.9 8.3 %collective-permute-start.22 = (bf16[2,128,1024]{2,1,0:T(8,128)(2,1)S(1)}, bf16[2,128,1024]{2,1,0:T(8,128)(2,1)S(1)}, u32[]{:S(2)}, u32[]{:S(2)}) collective-permute-start(bf16[2,128,1024]{2,1,0:T(8,128)(2,1)S(1)} %shard_map.90), channel_id=1, source_target_pairs={{0,1},{1,0},{2,3},{3,2},{4,5},{5,4},{6,7},{7,6},{8,9},{9,8},{10,11... | collective-permute-start | bytes 1572872 | tf_op jit(solution)/shard_map/ppermute | solution.py:34
  69.7 3.1 %collective-permute-start.13 = (bf16[32,16,256]{2,1,0:T(8,128)(2,1)S(1)}, bf16[32,16,256]{2,1,0:T(8,128)(2,1)S(1)}, u32[]{:S(2)}, u32[]{:S(2)}) collective-permute-start(bf16[32,16,256]{2,1,0:T(8,128)(2,1)S(1)} %get-tuple-element.56), channel_id=1, source_target_pairs={{0,129},{1,128},{128,1},{129,0},{2,131},{3,130},{130,3},{131,2},{4... | collective-permute-start | bytes 786440 | tf_op jit(solution)/shard_map/ppermute | solution.py:34
  72.8 13.3 %collective-permute-done.11.second_ref = bf16[32,16,256]{2,1,0:T(8,128)(2,1)S(1)} collective-permute-done((bf16[32,16,256]{2,1,0:T(8,128)(2,1)S(1)}, bf16[32,16,256]{2,1,0:T(8,128)(2,1)S(1)}, u32[]{:S(2)}, u32[]{:S(2)}) %collective-permute-start.11) | collective-permute-done | bytes 262176 | tf_op jit(solution)/shard_map/ppermute | solution.py:34
  86.1 5.3 %collective-permute-done.12.third_ref = bf16[32,16,256]{2,1,0:T(8,128)(2,1)S(1)} collective-permute-done((bf16[32,16,256]{2,1,0:T(8,128)(2,1)S(1)}, bf16[32,16,256]{2,1,0:T(8,128)(2,1)S(1)}, u32[]{:S(2)}, u32[]{:S(2)}) %collective-permute-start.12) | collective-permute-done | bytes 262176 | tf_op jit(solution)/shard_map/ppermute | solution.py:34
  91.4 1.4 %collective-permute-done.13.fourth_ref = bf16[32,16,256]{2,1,0:T(8,128)(2,1)S(1)} collective-permute-done((bf16[32,16,256]{2,1,0:T(8,128)(2,1)S(1)}, bf16[32,16,256]{2,1,0:T(8,128)(2,1)S(1)}, u32[]{:S(2)}, u32[]{:S(2)}) %collective-permute-start.13) | collective-permute-done | bytes 262176 | tf_op jit(solution)/shard_map/ppermute | solution.py:34
  93.2 2.7 %collective-permute-start.16 = (bf16[8,16,256]{2,1,0:T(8,128)(2,1)S(1)}, bf16[8,16,256]{2,1,0:T(8,128)(2,1)S(1)}, u32[]{:S(2)}, u32[]{:S(2)}) collective-permute-start(bf16[8,16,256]{2,1,0:T(8,128)(2,1)S(1)} %get-tuple-element.60), channel_id=1, source_target_pairs={{0,48},{16,0},{32,16},{48,32},{1,49},{17,1},{33,17},{49,33},{2,50}... | collective-permute-start | bytes 196616 | tf_op jit(solution)/shard_map/ppermute | solution.py:34
  95.8 2.0 %collective-permute-done.14.refs_0_ = bf16[8,16,256]{2,1,0:T(8,128)(2,1)S(1)} collective-permute-done((bf16[8,16,256]{2,1,0:T(8,128)(2,1)S(1)}, bf16[8,16,256]{2,1,0:T(8,128)(2,1)S(1)}, u32[]{:S(2)}, u32[]{:S(2)}) %collective-permute-start.14) | collective-permute-done | bytes 65568 | tf_op jit(solution)/shard_map/ppermute | solution.py:34
  97.8 1.8 %collective-permute-done.15.refs_1_ = bf16[8,16,256]{2,1,0:T(8,128)(2,1)S(1)} collective-permute-done((bf16[8,16,256]{2,1,0:T(8,128)(2,1)S(1)}, bf16[8,16,256]{2,1,0:T(8,128)(2,1)S(1)}, u32[]{:S(2)}, u32[]{:S(2)}) %collective-permute-start.15) | collective-permute-done | bytes 65568 | tf_op jit(solution)/shard_map/ppermute | solution.py:34
  99.6 9.6 %all_to_all.5.parts_ref = bf16[8,16,256]{2,1,0:T(8,128)(2,1)S(1)} all-to-all(bf16[8,16,256]{2,1,0:T(8,128)(2,1)S(1)} %shard_map.85), channel_id=1, replica_groups=mesh['xl'=2,'c'=2,'y'=4,'z'=8,'xh'=2] {'z'}, dimensions={0} | all-to-all | bytes 131072 | tf_op jit(solution)/shard_map/all_to_all | solution.py:316
  109.2 2.9 %collective-permute-start.19 = (bf16[16,256]{1,0:T(8,128)(2,1)S(1)}, bf16[16,256]{1,0:T(8,128)(2,1)S(1)}, u32[]{:S(2)}, u32[]{:S(2)}) collective-permute-start(bf16[16,256]{1,0:T(8,128)(2,1)S(1)} %shard_map.86.mine_ref), channel_id=1, source_target_pairs={{0,192},{64,128},{128,64},{192,0},{1,193},{65,129},{129,65},{193,1... | collective-permute-start | bytes 24584 | tf_op jit(solution)/shard_map/ppermute | solution.py:34
  113.4 1.2 %collective-permute-done.17.x_ref = bf16[16,256]{1,0:T(8,128)(2,1)S(1)} collective-permute-done((bf16[16,256]{1,0:T(8,128)(2,1)S(1)}, bf16[16,256]{1,0:T(8,128)(2,1)S(1)}, u32[]{:S(2)}, u32[]{:S(2)}) %collective-permute-start.17) | collective-permute-done | bytes 8224 | tf_op jit(solution)/shard_map/ppermute | solution.py:34
  (39 shorter events, 8.8 us)
Async XLA Ops:
  1.7 8.6 %collective-permute-start.2 = (bf16[128,1024]{1,0:T(8,128)(2,1)S(1)}, bf16[128,1024]{1,0:T(8,128)(2,1)S(1)}, u32[]{:S(2)}, u32[]{:S(2)}) collective-permute-start(bf16[128,1024]{1,0:T(8,128)(2,1)S(1)} %get-tuple-element.72.own_ref), channel_id=1, source_target_pairs={{0,1},{1,0},{2,3},{3,2},{4,5},{5,4},{6,7},{7,6},{8,9},{9,8},{10,11... | collective-permute-start | bytes 786440 | tf_op jit(solution)/shard_map/ppermute | solution.py:34
  5.3 10.6 %collective-permute-start = (bf16[128,1024]{1,0:T(8,128)(2,1)S(1)}, bf16[128,1024]{1,0:T(8,128)(2,1)S(1)}, u32[]{:S(2)}, u32[]{:S(2)}) collective-permute-start(bf16[128,1024]{1,0:T(8,128)(2,1)S(1)} %get-tuple-element.73.own_ref), channel_id=1, source_target_pairs={{0,1},{1,0},{2,3},{3,2},{4,5},{5,4},{6,7},{7,6},{8,9},{9,8},{10,11... | collective-permute-start | bytes 786440 | tf_op jit(solution)/shard_map/ppermute | solution.py:34
  10.3 13.2 %collective-permute-start.3 = (bf16[128,1024]{1,0:T(8,128)(2,1)S(1)}, bf16[128,1024]{1,0:T(8,128)(2,1)S(1)}, u32[]{:S(2)}, u32[]{:S(2)}) collective-permute-start(bf16[128,1024]{1,0:T(8,128)(2,1)S(1)} %collective-permute-done.2.rec_ref), channel_id=1, source_target_pairs={{0,2},{1,63},{2,4},{3,1},{4,6},{5,3},{6,8},{7,5},{8,10},{9,7},{10,... | collective-permute-start | bytes 786440 | tf_op jit(solution)/shard_map/ppermute | solution.py:34
  16.0 14.2 %collective-permute-start.1 = (bf16[128,1024]{1,0:T(8,128)(2,1)S(1)}, bf16[128,1024]{1,0:T(8,128)(2,1)S(1)}, u32[]{:S(2)}, u32[]{:S(2)}) collective-permute-start(bf16[128,1024]{1,0:T(8,128)(2,1)S(1)} %collective-permute-done.rec_ref), channel_id=1, source_target_pairs={{0,2},{1,63},{2,4},{3,1},{4,6},{5,3},{6,8},{7,5},{8,10},{9,7},{10,... | collective-permute-start | bytes 786440 | tf_op jit(solution)/shard_map/ppermute | solution.py:34
  18.6 1.6 %copy-start = (bf16[1024,1024]{1,0:T(8,128)(2,1)S(1)}, bf16[1024,1024]{1,0:T(8,128)(2,1)}, u32[]{:S(2)}) copy-start(bf16[1024,1024]{1,0:T(8,128)(2,1)} %refs_0_.1) | copy-start | bytes 6291460
  20.1 0.9 copy-start.1
  21.1 0.9 copy-start.2
  22.0 0.7 copy-start.3
  26.0 10.2 %collective-permute-start.7 = (bf16[100,512]{1,0:T(8,128)(2,1)S(1)}, bf16[100,512]{1,0:T(8,128)(2,1)S(1)}, u32[]{:S(2)}, u32[]{:S(2)}) collective-permute-start(bf16[100,512]{1,0:T(8,128)(2,1)S(1)} %get-tuple-element.45.own1_ref.refs_3_), channel_id=1, source_target_pairs={{0,128},{128,0},{1,129},{129,1},{2,130},{130,2},{3,131},{131,3},{4... | collective-permute-start | bytes 307208 | tf_op jit(solution)/shard_map/ppermute | solution.py:34
  32.6 4.2 %collective-permute-start.4 = (bf16[100,512]{1,0:T(8,128)(2,1)S(1)}, bf16[100,512]{1,0:T(8,128)(2,1)S(1)}, u32[]{:S(2)}, u32[]{:S(2)}) collective-permute-start(bf16[100,512]{1,0:T(8,128)(2,1)S(1)} %get-tuple-element.44.own0_ref.refs_2_), channel_id=1, source_target_pairs={{0,128},{128,0},{1,129},{129,1},{2,130},{130,2},{3,131},{131,3},{4... | collective-permute-start | bytes 307208 | tf_op jit(solution)/shard_map/ppermute | solution.py:34
  33.9 6.2 %collective-permute-start.6 = (bf16[100,512]{1,0:T(8,128)(2,1)S(1)}, bf16[100,512]{1,0:T(8,128)(2,1)S(1)}, u32[]{:S(2)}, u32[]{:S(2)}) collective-permute-start(bf16[100,512]{1,0:T(8,128)(2,1)S(1)} %get-tuple-element.45.own1_ref.refs_3_), channel_id=1, source_target_pairs={{0,64},{64,0},{1,65},{65,1},{2,66},{66,2},{3,67},{67,3},{4,68},{68... | collective-permute-start | bytes 307208 | tf_op jit(solution)/shard_map/ppermute | solution.py:34
  36.2 3.9 %collective-permute-start.5 = (bf16[100,512]{1,0:T(8,128)(2,1)S(1)}, bf16[100,512]{1,0:T(8,128)(2,1)S(1)}, u32[]{:S(2)}, u32[]{:S(2)}) collective-permute-start(bf16[100,512]{1,0:T(8,128)(2,1)S(1)} %get-tuple-element.44.own0_ref.refs_2_), channel_id=1, source_target_pairs={{0,64},{64,0},{1,65},{65,1},{2,66},{66,2},{3,67},{67,3},{4,68},{68... | collective-permute-start | bytes 307208 | tf_op jit(solution)/shard_map/ppermute | solution.py:34
  36.2 4.2 %collective-permute-start.9 = (bf16[100,512]{1,0:T(8,128)(2,1)S(1)}, bf16[100,512]{1,0:T(8,128)(2,1)S(1)}, u32[]{:S(2)}, u32[]{:S(2)}) collective-permute-start(bf16[100,512]{1,0:T(8,128)(2,1)S(1)} %collective-permute-done.7.refs_4_), channel_id=1, source_target_pairs={{0,64},{64,0},{1,65},{65,1},{2,66},{66,2},{3,67},{67,3},{4,68},{68... | collective-permute-start | bytes 307208 | tf_op jit(solution)/shard_map/ppermute | solution.py:34
  36.7 3.7 %collective-permute-start.8 = (bf16[100,512]{1,0:T(8,128)(2,1)S(1)}, bf16[100,512]{1,0:T(8,128)(2,1)S(1)}, u32[]{:S(2)}, u32[]{:S(2)}) collective-permute-start(bf16[100,512]{1,0:T(8,128)(2,1)S(1)} %collective-permute-done.4.refs_0_), channel_id=1, source_target_pairs={{0,64},{64,0},{1,65},{65,1},{2,66},{66,2},{3,67},{67,3},{4,68},{68... | collective-permute-start | bytes 307208 | tf_op jit(solution)/shard_map/ppermute | solution.py:34
  42.4 26.8 %collective-permute-start.10 = (bf16[32,2,16,512]{3,2,1,0:T(8,128)(2,1)S(1)}, bf16[32,2,16,512]{3,2,1,0:T(8,128)(2,1)S(1)}, u32[]{:S(2)}, u32[]{:S(2)}) collective-permute-start(bf16[32,2,16,512]{3,2,1,0:T(8,128)(2,1)S(1)} %get-tuple-element.52), channel_id=1, source_target_pairs={{0,64},{64,0},{1,65},{65,1},{2,66},{66,2},{3,67},{67,3},{4,68},{68... | collective-permute-start | bytes 3145736 | tf_op jit(solution)/shard_map/ppermute | solution.py:34
  46.4 8.8 %collective-permute-start.20 = (bf16[128,1024]{1,0:T(8,128)(2,1)S(1)}, bf16[128,1024]{1,0:T(8,128)(2,1)S(1)}, u32[]{:S(2)}, u32[]{:S(2)}) collective-permute-start(bf16[128,1024]{1,0:T(8,128)(2,1)S(1)} %get-tuple-element.70), channel_id=1, source_target_pairs={{0,62},{1,3},{2,0},{3,5},{4,2},{5,7},{6,4},{7,9},{8,6},{9,11},{10,... | collective-permute-start | bytes 786440 | tf_op jit(solution)/shard_map/ppermute | solution.py:34
  51.6 9.2 %collective-permute-start.21 = (bf16[128,1024]{1,0:T(8,128)(2,1)S(1)}, bf16[128,1024]{1,0:T(8,128)(2,1)S(1)}, u32[]{:S(2)}, u32[]{:S(2)}) collective-permute-start(bf16[128,1024]{1,0:T(8,128)(2,1)S(1)} %get-tuple-element.71), channel_id=1, source_target_pairs={{0,62},{1,3},{2,0},{3,5},{4,2},{5,7},{6,4},{7,9},{8,6},{9,11},{10,... | collective-permute-start | bytes 786440 | tf_op jit(solution)/shard_map/ppermute | solution.py:34
  60.9 51.6 %collective-permute-start.22 = (bf16[2,128,1024]{2,1,0:T(8,128)(2,1)S(1)}, bf16[2,128,1024]{2,1,0:T(8,128)(2,1)S(1)}, u32[]{:S(2)}, u32[]{:S(2)}) collective-permute-start(bf16[2,128,1024]{2,1,0:T(8,128)(2,1)S(1)} %shard_map.90), channel_id=1, source_target_pairs={{0,1},{1,0},{2,3},{3,2},{4,5},{5,4},{6,7},{7,6},{8,9},{9,8},{10,11... | collective-permute-start | bytes 1572872 | tf_op jit(solution)/shard_map/ppermute | solution.py:34
  69.5 16.6 %collective-permute-start.11 = (bf16[32,16,256]{2,1,0:T(8,128)(2,1)S(1)}, bf16[32,16,256]{2,1,0:T(8,128)(2,1)S(1)}, u32[]{:S(2)}, u32[]{:S(2)}) collective-permute-start(bf16[32,16,256]{2,1,0:T(8,128)(2,1)S(1)} %get-tuple-element.54), channel_id=1, source_target_pairs={{0,1},{1,0},{2,3},{3,2},{4,5},{5,4},{6,7},{7,6},{8,9},{9,8},{10,11... | collective-permute-start | bytes 786440 | tf_op jit(solution)/shard_map/ppermute | solution.py:34
  69.6 21.8 %collective-permute-start.12 = (bf16[32,16,256]{2,1,0:T(8,128)(2,1)S(1)}, bf16[32,16,256]{2,1,0:T(8,128)(2,1)S(1)}, u32[]{:S(2)}, u32[]{:S(2)}) collective-permute-start(bf16[32,16,256]{2,1,0:T(8,128)(2,1)S(1)} %get-tuple-element.55), channel_id=1, source_target_pairs={{0,128},{128,0},{1,129},{129,1},{2,130},{130,2},{3,131},{131,3},{4... | collective-permute-start | bytes 786440 | tf_op jit(solution)/shard_map/ppermute | solution.py:34
  69.7 23.2 %collective-permute-start.13 = (bf16[32,16,256]{2,1,0:T(8,128)(2,1)S(1)}, bf16[32,16,256]{2,1,0:T(8,128)(2,1)S(1)}, u32[]{:S(2)}, u32[]{:S(2)}) collective-permute-start(bf16[32,16,256]{2,1,0:T(8,128)(2,1)S(1)} %get-tuple-element.56), channel_id=1, source_target_pairs={{0,129},{1,128},{128,1},{129,0},{2,131},{3,130},{130,3},{131,2},{4... | collective-permute-start | bytes 786440 | tf_op jit(solution)/shard_map/ppermute | solution.py:34
  93.0 4.8 %collective-permute-start.14 = (bf16[8,16,256]{2,1,0:T(8,128)(2,1)S(1)}, bf16[8,16,256]{2,1,0:T(8,128)(2,1)S(1)}, u32[]{:S(2)}, u32[]{:S(2)}) collective-permute-start(bf16[8,16,256]{2,1,0:T(8,128)(2,1)S(1)} %get-tuple-element.58), channel_id=1, source_target_pairs={{0,32},{16,48},{32,0},{48,16},{1,33},{17,49},{33,1},{49,17},{2,34}... | collective-permute-start | bytes 196616 | tf_op jit(solution)/shard_map/ppermute | solution.py:34
  93.1 6.5 %collective-permute-start.15 = (bf16[8,16,256]{2,1,0:T(8,128)(2,1)S(1)}, bf16[8,16,256]{2,1,0:T(8,128)(2,1)S(1)}, u32[]{:S(2)}, u32[]{:S(2)}) collective-permute-start(bf16[8,16,256]{2,1,0:T(8,128)(2,1)S(1)} %get-tuple-element.59), channel_id=1, source_target_pairs={{0,16},{16,32},{32,48},{48,0},{1,17},{17,33},{33,49},{49,1},{2,18}... | collective-permute-start | bytes 196616 | tf_op jit(solution)/shard_map/ppermute | solution.py:34
  93.2 6.4 %collective-permute-start.16 = (bf16[8,16,256]{2,1,0:T(8,128)(2,1)S(1)}, bf16[8,16,256]{2,1,0:T(8,128)(2,1)S(1)}, u32[]{:S(2)}, u32[]{:S(2)}) collective-permute-start(bf16[8,16,256]{2,1,0:T(8,128)(2,1)S(1)} %get-tuple-element.60), channel_id=1, source_target_pairs={{0,48},{16,0},{32,16},{48,32},{1,49},{17,1},{33,17},{49,33},{2,50}... | collective-permute-start | bytes 196616 | tf_op jit(solution)/shard_map/ppermute | solution.py:34
  109.2 4.2 %collective-permute-start.19 = (bf16[16,256]{1,0:T(8,128)(2,1)S(1)}, bf16[16,256]{1,0:T(8,128)(2,1)S(1)}, u32[]{:S(2)}, u32[]{:S(2)}) collective-permute-start(bf16[16,256]{1,0:T(8,128)(2,1)S(1)} %shard_map.86.mine_ref), channel_id=1, source_target_pairs={{0,192},{64,128},{128,64},{192,0},{1,193},{65,129},{129,65},{193,1... | collective-permute-start | bytes 24584 | tf_op jit(solution)/shard_map/ppermute | solution.py:34
  112.1 1.3 %collective-permute-start.18 = (bf16[16,256]{1,0:T(8,128)(2,1)S(1)}, bf16[16,256]{1,0:T(8,128)(2,1)S(1)}, u32[]{:S(2)}, u32[]{:S(2)}) collective-permute-start(bf16[16,256]{1,0:T(8,128)(2,1)S(1)} %shard_map.86.mine_ref), channel_id=1, source_target_pairs={{0,64},{64,0},{1,65},{65,1},{2,66},{66,2},{3,67},{67,3},{4,68},{68... | collective-permute-start | bytes 24584 | tf_op jit(solution)/shard_map/ppermute | solution.py:34
  112.1 2.5 %collective-permute-start.17 = (bf16[16,256]{1,0:T(8,128)(2,1)S(1)}, bf16[16,256]{1,0:T(8,128)(2,1)S(1)}, u32[]{:S(2)}, u32[]{:S(2)}) collective-permute-start(bf16[16,256]{1,0:T(8,128)(2,1)S(1)} %shard_map.86.mine_ref), channel_id=1, source_target_pairs={{0,128},{128,0},{1,129},{129,1},{2,130},{130,2},{3,131},{131,3},{4... | collective-permute-start | bytes 24584 | tf_op jit(solution)/shard_map/ppermute | solution.py:34
